TPU v7x, 32 devices: a whole 2x2x4 slice. The times are simulated.
32 devices in a mesh: section: 4 (over z), node: 4 (over x, core), local: 2 (over y).
Axes of the slice: x: 2, y: 2, z: 4, core: 2. Of those that a mesh axis runs over, the one named last changes fastest.
Arguments:
- section_inputs: bfloat16 [4, 8, 4, 196, 512], P('section', ('node', 'local')), may hold values from -6 to 6
- grad_in: bfloat16 [4, 8, 196, 512], P('section', ('node', 'local')), may hold values from -6 to 6
- loss_grad: bfloat16 [8, 3, 196, 512], P(('node', 'local')), may hold values from -6 to 6
- w_reduce: bfloat16 [4, 512, 256], P('section'), may hold values from -0.25 to 0.25
- w_spatial: bfloat16 [4, 2304, 256], P('section'), may hold values from -0.125 to 0.125
- w_expand: bfloat16 [4, 256, 512], P('section'), may hold values from -0.375 to 0.375
- err_reduce: bfloat16 [4, 8, 512, 256], P('section', ('node', 'local')), may hold values from -360 to 360
- err_spatial: bfloat16 [4, 8, 2304, 256], P('section', ('node', 'local')), may hold values from -360 to 360
- err_expand: bfloat16 [4, 8, 256, 512], P('section', ('node', 'local')), may hold values from -360 to 360
- prior_reduce: float32 [4, 32, 256], P('section'), may hold values from -6 to 6
- prior_spatial: float32 [4, 32, 256], P('section'), may hold values from -6 to 6
- prior_expand: float32 [4, 32, 512], P('section'), may hold values from -6 to 6
Outputs:
- leaving: bfloat16 [4, 8, 196, 512], P('section', ('node', 'local'))
- basis_reduce: float32 [4, 32, 512], P('section', None, ('node', 'local'))
- basis_spatial: float32 [4, 32, 2304], P('section', None, ('node', 'local'))
- basis_expand: float32 [4, 32, 256], P('section', None, ('node', 'local'))
- right_reduce: float32 [4, 32, 256], P('section', None, ('node', 'local'))
- right_spatial: float32 [4, 32, 256], P('section', None, ('node', 'local'))
- right_expand: float32 [4, 32, 512], P('section', None, ('node', 'local'))
All inputs are finite; a program needn't handle non-finite values.
Results may differ from a plain program's by a relative error of at most 0.0095.
Values may be sent and summed in bfloat16 or wider, within the bound.
No kernel may reach another device: no remote copies, remote signals or barrier semaphores. Data moves between devices by JAX's collectives and lax.ppermute only.
A program may use at most 128 MiB of HBM per device.

v0:
```python
import math

import jax
import jax.numpy as jnp
from jax import lax
from jax.sharding import PartitionSpec as P

SIDE = 14


precise = lax.Precision.HIGHEST


def shifted_2(block, axis, distance):
    devices = range(lax.axis_size(axis))
    route = [(i - distance, i) for i in devices if i - distance in devices]
    return lax.ppermute(block, axis, route)


def silu_slope(values):
    logistic = jax.nn.sigmoid(values)
    return logistic * (1.0 + values * (1.0 - logistic))


def tap_shift(values, row_step, col_step, image_side):
    pixels = values.shape[0]
    offset = row_step * image_side + col_step
    padded = jnp.pad(values, ((image_side + 1, image_side + 1), (0, 0)))
    moved = lax.slice_in_dim(
        padded, image_side + 1 + offset, image_side + 1 + offset + pixels, axis=0
    )
    column = lax.broadcasted_iota(jnp.int32, (pixels, 1), 0) % image_side + col_step
    inside = jnp.logical_and(column >= 0, column < image_side)
    return jnp.where(inside, moved, jnp.zeros_like(moved))


def inner_rows(left_operand, right_operand):
    return lax.dot_general(
        left_operand, right_operand, (((0,), (0,)), ((), ())), preferred_element_type=jnp.float32
    )


def inner_cols(left_operand, right_operand, accuracy=None):
    return lax.dot_general(
        left_operand,
        right_operand,
        (((1,), (1,)), ((), ())),
        precision=accuracy,
        preferred_element_type=jnp.float32,
    )


def block_backward(inputs, upstream, reduce_weight, spatial_weight, expand_weight, image_side):
    channels = reduce_weight.shape[1]
    pre_reduce = jnp.dot(inputs, reduce_weight, preferred_element_type=jnp.float32)
    hidden_one = jax.nn.silu(pre_reduce).astype(jnp.bfloat16)
    shifted = []
    pre_spatial = jnp.zeros((inputs.shape[0], channels), jnp.float32)
    for tap in range(9):
        moved = tap_shift(hidden_one, tap // 3 - 1, tap % 3 - 1, image_side)
        shifted.append(moved)
        pre_spatial = pre_spatial + jnp.dot(
            moved,
            spatial_weight[tap * channels : (tap + 1) * channels],
            preferred_element_type=jnp.float32,
        )
    hidden_two = jax.nn.silu(pre_spatial).astype(jnp.bfloat16)
    back_two = inner_cols(upstream, expand_weight)
    back_spatial = (back_two * silu_slope(pre_spatial)).astype(jnp.bfloat16)
    back_one = jnp.zeros((inputs.shape[0], channels), jnp.float32)
    for tap in range(9):
        tap_term = inner_cols(back_spatial, spatial_weight[tap * channels : (tap + 1) * channels])
        back_one = back_one + tap_shift(tap_term, 1 - tap // 3, 1 - tap % 3, image_side)
    back_reduce = (back_one * silu_slope(pre_reduce)).astype(jnp.bfloat16)
    leaving = (upstream.astype(jnp.float32) + inner_cols(back_reduce, reduce_weight)).astype(
        jnp.bfloat16
    )
    spatial_grad = jnp.concatenate(
        [inner_rows(shifted[tap], back_spatial) for tap in range(9)], axis=0
    )
    gradients = (inner_rows(inputs, back_reduce), spatial_grad, inner_rows(hidden_two, upstream))
    return (leaving, gradients)


def local(
    section_inputs,
    grad_in,
    loss_grad,
    w_reduce,
    w_spatial,
    w_expand,
    err_reduce,
    err_spatial,
    err_expand,
    prior_reduce,
    prior_spatial,
    prior_expand,
):
    image_side = SIDE
    weights = (w_reduce[0], w_spatial[0], w_expand[0])
    last_section = lax.axis_index("section") == lax.axis_size("section") - 1
    upstream = grad_in[0, 0]
    leaving = upstream
    totals = tuple((jnp.zeros(weights[member].shape, jnp.float32) for member in range(3)))
    for tick_index in range(section_inputs.shape[2]):
        if tick_index > 0:
            arrived = shifted_2(leaving, "section", -1)
            upstream = jnp.where(last_section, loss_grad[0, tick_index - 1], arrived)
        leaving, gradients = block_backward(
            section_inputs[0, 0, tick_index],
            upstream,
            weights[0],
            weights[1],
            weights[2],
            image_side,
        )
        totals = tuple((totals[member] + gradients[member] for member in range(3)))
    errors = (err_reduce[0, 0], err_spatial[0, 0], err_expand[0, 0])
    matrices = tuple((totals[member] + errors[member].astype(jnp.float32) for member in range(3)))
    priors = (prior_reduce[0], prior_spatial[0], prior_expand[0])
    factors = tuple((inner_cols(priors[member], matrices[member], precise) for member in range(3)))
    replicas = lax.axis_size(("node", "local"))
    replica_index = lax.axis_index(("node", "local"))
    basis_list = []
    summed = lax.psum((factors[0], factors[1], factors[2]), ("node", "local"))
    partial_rights = []
    for member in range(3):
        triangle = jnp.linalg.cholesky(inner_cols(summed[member], summed[member], precise))
        orthonormal = lax.linalg.triangular_solve(
            triangle, summed[member], left_side=True, lower=True
        )
        slice_width = orthonormal.shape[1] // replicas
        own_rows = lax.dynamic_slice_in_dim(
            orthonormal, replica_index * slice_width, slice_width, 1
        )
        basis_list.append(math.sqrt(orthonormal.shape[1]) * own_rows)
        partial_rights.append(
            jnp.dot(
                orthonormal, matrices[member], precision=precise, preferred_element_type=jnp.float32
            )
        )
    between = (
        lax.psum_scatter(
            partial_rights[0].astype(jnp.bfloat16), "node", scatter_dimension=1, tiled=True
        ).astype(jnp.float32),
        lax.psum_scatter(
            partial_rights[1].astype(jnp.bfloat16), "node", scatter_dimension=1, tiled=True
        ).astype(jnp.float32),
        lax.psum_scatter(
            partial_rights[2].astype(jnp.bfloat16), "node", scatter_dimension=1, tiled=True
        ).astype(jnp.float32),
    )
    rights = (
        lax.psum_scatter(between[0], "local", scatter_dimension=1, tiled=True),
        lax.psum_scatter(between[1], "local", scatter_dimension=1, tiled=True),
        lax.psum_scatter(between[2], "local", scatter_dimension=1, tiled=True),
    )
    right_list = tuple(
        (rights[member] / (replicas * math.sqrt(matrices[member].shape[0])) for member in range(3))
    )
    return (
        leaving[None, None],
        basis_list[0][None],
        basis_list[1][None],
        basis_list[2][None],
        right_list[0][None],
        right_list[1][None],
        right_list[2][None],
    )


def solution(mesh):
    return jax.shard_map(
        local,
        mesh=mesh,
        in_specs=(
            P("section", ("node", "local"), None, None, None),
            P("section", ("node", "local"), None, None),
            P(("node", "local"), None, None, None),
            P("section", None, None),
            P("section", None, None),
            P("section", None, None),
            P("section", ("node", "local"), None, None),
            P("section", ("node", "local"), None, None),
            P("section", ("node", "local"), None, None),
            P("section", None, None),
            P("section", None, None),
            P("section", None, None),
        ),
        out_specs=(
            P("section", ("node", "local"), None, None),
            P("section", None, ("node", "local")),
            P("section", None, ("node", "local")),
            P("section", None, ("node", "local")),
            P("section", None, ("node", "local")),
            P("section", None, ("node", "local")),
            P("section", None, ("node", "local")),
        ),
        check_vma=False,
    )
```

profile of v0, /device:TPU:0, one launch (start us, length us, event | category | flops | bytes accessed | tf_op | source)
XLA Modules:
  0.0 292.2 jit_solution(3530639854416297702)
XLA Ops:
  8.1 4.7 %fusion.439 = (bf16[1,1,1,196,512]{4,2,3,1,0:T(2,128)(2,1)S(1)}, bf16[1,1,1,196,512]{4,2,3,1,0:T(2,128)(2,1)}, bf16[1,1,1,196,512]{4,2,3,1,0:T(2,128)(2,1)}, bf16[1,1,1,196,512]{4,2,3,1,0:T(2,128)(2,1)S(1)}) fusion(bf16[1,1,4,196,512]{4,2,3,1,0:T(4,128)(2,1)} %param.13), kind=kLoop, calls=%fused_computation.670 | loop fusion | bytes 1605632 | tf_op jit(solution)/shard_map/slice | solution.py:110
  20.2 2.0 fusion.123
  44.7 1.8 constant_dynamic-update-slice_fusion.7
  46.5 1.7 constant_dynamic-update-slice_fusion.6
  48.2 1.7 constant_dynamic-update-slice_fusion.5
  49.9 1.7 constant_dynamic-update-slice_fusion.4
  51.6 1.7 constant_dynamic-update-slice_fusion.3
  65.9 4.6 %collective-permute-done.1 = bf16[196,512]{1,0:T(8,128)(2,1)S(1)} collective-permute-done((bf16[196,512]{1,0:T(8,128)(2,1)S(1)}, bf16[196,512]{1,0:T(8,128)(2,1)S(1)}, u32[]{:S(2)}, u32[]{:S(2)}) %collective-permute-start.1) | collective-permute-done | bytes 200736 | tf_op jit(solution)/shard_map/ppermute | solution.py:17
  79.1 2.6 collective-permute-done.2
  87.4 23.9 %psum.23 = f32[32,256]{1,0:T(8,128)S(1)} all-reduce(f32[32,256]{1,0:T(8,128)S(1)} %convolution_bitcast_fusion.2), channel_id=1, replica_groups=mesh['section'=4,'node'=4,'local'=2] {'node','local'}, use_global_device_ids=true, to_apply=%region_4.6 | all-reduce | flops 8192 | bytes 65536 | tf_op jit(solution)/shard_map/psum | solution.py:125
  111.5 2.9 cholesky.81
  115.7 2.4 custom-call.13
  135.0 3.4 %convolution_bitcast_fusion = f32[32,2304]{1,0:T(8,128)} fusion(bf16[1,1,2304,256]{3,2,1,0:T(8,128)(2,1)S(1)} %copy-done.2, f32[1,1,2304,256]{3,2,1,0:T(8,128)S(1)} %copy-done.6, f32[1,1,2304,256]{3,2,1,0:T(8,128)S(1)} %copy-done.10, f32[1,1,2304,256]{3,2,1,0:T(8,128)S(1)} %copy-done.5, f32[1,1,2304,256]{3,2,1,0:T(8,128)S(1)} %copy-done.8, ...), kind=kOutput, calls=%fused_computation | convolution fusion | flops 229441536 | bytes 10944512 | tf_op jit(solution)/shard_map/dot_general | solution.py:44
  141.8 9.6 %reduce-scatter.29.cloned.1.call-done = f32[64,32]{1,0:T(8,128)} async-done(((f32[128,32]{1,0:T(8,128)}), f32[64,32]{1,0:T(8,128)}) %reduce-scatter.29.cloned.1.call-update) | async-done | bytes 8208
  152.9 44.8 %all-reduce.39.cloned.1.call-done = (f32[32,512]{1,0:T(8,128)}, f32[32,2304]{1,0:T(8,128)}) async-done(((f32[32,512]{1,0:T(8,128)}, f32[32,2304]{1,0:T(8,128)}), (f32[32,512]{1,0:T(8,128)}, f32[32,2304]{1,0:T(8,128)})) %all-reduce.39.cloned.1.call-update) | async-done | bytes 360464 | tf_op jit(solution)/shard_map/psum | solution.py:125
  200.3 2.9 %cholesky.70 = f32[32,32]{1,0:T(8,128)S(1)} custom-call(f32[32,32]{1,0:T(8,128)S(1)} %fusion.327), custom_call_target="Cholesky" | custom-call | tf_op jit(solution)/shard_map/jit(cholesky)/cholesky | solution.py:128
  204.6 2.4 custom-call.12
  208.5 2.9 cholesky.59
  212.8 2.4 custom-call.11
  217.7 5.3 %fusion.48 = bf16[32,256]{1,0:T(8,128)(2,1)S(1)} fusion(f32[32,2304]{1,0:T(8,128)S(1)} %fusion.325, bf16[1,1,2304,256]{3,2,1,0:T(8,128)(2,1)S(1)} %copy-done.2, f32[2304,256]{1,0:T(8,128)} %constant_dynamic-update-slice_fusion.27, f32[2304,256]{1,0:T(8,128)} %copy-done.12, f32[2304,256]{1,0:T(8,128)} %constant_dynamic-update-slice_fusion, ...), kind=kOutput, calls=%fused_computation.98 | convolution fusion | flops 229449728 | bytes 10928128 | tf_op jit(solution)/shard_map/dot_general | solution.py:138
  224.6 12.9 %reduce-scatter.19.cloned.1.call-done = bf16[64,32]{1,0:T(8,128)(2,1)} async-done(((bf16[256,32]{1,0:T(8,128)(2,1)}), bf16[64,32]{1,0:T(8,128)(2,1)}) %reduce-scatter.19.cloned.1.call-update) | async-done | bytes 4112
  239.7 19.6 %reduce-scatter.23.cloned.1.call-done = bf16[64,32]{1,0:T(8,128)(2,1)} async-done(((bf16[256,32]{1,0:T(8,128)(2,1)}), bf16[64,32]{1,0:T(8,128)(2,1)}) %reduce-scatter.23.cloned.1.call-update) | async-done | bytes 4112
  260.8 10.5 %reduce-scatter.21.cloned.1.call-done = f32[32,32]{1,0:T(8,128)} async-done(((f32[64,32]{1,0:T(8,128)}), f32[32,32]{1,0:T(8,128)}) %reduce-scatter.21.cloned.1.call-update) | async-done | bytes 4112
  272.7 10.6 %reduce-scatter.25.cloned.1.call-done = f32[32,32]{1,0:T(8,128)} async-done(((f32[64,32]{1,0:T(8,128)}), f32[32,32]{1,0:T(8,128)}) %reduce-scatter.25.cloned.1.call-update) | async-done | bytes 4112
  (302 shorter events, 96.2 us)
Async XLA Ops:
  8.0 131.1 %reduce-scatter.27.cloned.1.call-start = ((), (), s32[]{:S(2)}) async-start(), calls=%async_computation.10 | async-start | bytes 163840
  12.8 11.5 %copy-start.15 = (bf16[1,1,1,196,512]{4,2,3,1,0:T(2,128)(2,1)}, bf16[1,1,1,196,512]{4,2,3,1,0:T(2,128)(2,1)S(1)}, u32[]{:S(2)}) copy-start(bf16[1,1,1,196,512]{4,2,3,1,0:T(2,128)(2,1)S(1)} %get-tuple-element.10) | copy-start | bytes 602116
  18.6 37.1 %collective-permute-start = (bf16[196,512]{1,0:T(8,128)(2,1)}, bf16[196,512]{1,0:T(8,128)(2,1)}, u32[]{:S(2)}, u32[]{:S(2)}) collective-permute-start(bf16[196,512]{1,0:T(8,128)(2,1)} %fusion.15), channel_id=1, source_target_pairs={{8,0},{16,8},{24,16},{9,1},{17,9},{25,17},{10,2},{18,10},{26,18},{... | collective-permute-start | bytes 602120 | tf_op jit(solution)/shard_map/ppermute | solution.py:17
  44.0 11.5 %copy-start.22 = (f32[196,256]{1,0:T(8,128)S(1)}, f32[196,256]{1,0:T(8,128)}, u32[]{:S(2)}) copy-start(f32[196,256]{1,0:T(8,128)} %convolution_add_fusion.23) | copy-start | bytes 602116
  44.7 8.6 %copy-start.13 = (f32[256,256]{1,0:T(8,128)S(1)}, f32[256,256]{1,0:T(8,128)}, u32[]{:S(2)}) copy-start(f32[256,256]{1,0:T(8,128)} %get-tuple-element.71) | copy-start | bytes 786436
  44.7 9.3 %copy-start.14 = (f32[256,256]{1,0:T(8,128)S(1)}, f32[256,256]{1,0:T(8,128)}, u32[]{:S(2)}) copy-start(f32[256,256]{1,0:T(8,128)} %get-tuple-element.73) | copy-start | bytes 786436
  44.7 11.0 %copy-start.23 = (bf16[1,3,196,512]{3,2,1,0:T(8,128)(2,1)S(1)}, bf16[1,3,196,512]{3,2,1,0:T(8,128)(2,1)}, u32[]{:S(2)}) copy-start(bf16[1,3,196,512]{3,2,1,0:T(8,128)(2,1)} %param.15) | copy-start | bytes 1806340
  46.5 10.2 %copy-start.34 = (bf16[1,256,512]{2,1,0:T(8,128)(2,1)S(1)}, bf16[1,256,512]{2,1,0:T(8,128)(2,1)}, u32[]{:S(2)}) copy-start(bf16[1,256,512]{2,1,0:T(8,128)(2,1)} %param.18) | copy-start | bytes 786436
  59.8 10.7 %collective-permute-start.1 = (bf16[196,512]{1,0:T(8,128)(2,1)S(1)}, bf16[196,512]{1,0:T(8,128)(2,1)S(1)}, u32[]{:S(2)}, u32[]{:S(2)}) collective-permute-start(bf16[196,512]{1,0:T(8,128)(2,1)S(1)} %add_convert_fusion.2), channel_id=1, source_target_pairs={{8,0},{16,8},{24,16},{9,1},{17,9},{25,17},{10,2},{18,10},{26,18},{... | collective-permute-start | bytes 602120 | tf_op jit(solution)/shard_map/ppermute | solution.py:17
  64.2 6.2 %copy-start.21 = (f32[196,256]{1,0:T(8,128)S(1)}, f32[196,256]{1,0:T(8,128)}, u32[]{:S(2)}) copy-start(f32[196,256]{1,0:T(8,128)} %convolution_add_fusion.14) | copy-start | bytes 602116
  73.6 8.1 %collective-permute-start.2 = (bf16[196,512]{1,0:T(8,128)(2,1)S(1)}, bf16[196,512]{1,0:T(8,128)(2,1)S(1)}, u32[]{:S(2)}, u32[]{:S(2)}) collective-permute-start(bf16[196,512]{1,0:T(8,128)(2,1)S(1)} %add_convert_fusion.1), channel_id=1, source_target_pairs={{8,0},{16,8},{24,16},{9,1},{17,9},{25,17},{10,2},{18,10},{26,18},{... | collective-permute-start | bytes 602120 | tf_op jit(solution)/shard_map/ppermute | solution.py:17
  119.6 31.8 %reduce-scatter.29.cloned.1.call-start = ((), (), s32[]{:S(2)}) async-start(), calls=%async_computation.11 | async-start | bytes 98304
  120.7 7.9 %copy-start.16 = (bf16[1,1,1,196,512]{4,2,3,1,0:T(2,128)(2,1)S(1)}, bf16[1,1,1,196,512]{4,2,3,1,0:T(2,128)(2,1)}, u32[]{:S(2)}) copy-start(bf16[1,1,1,196,512]{4,2,3,1,0:T(2,128)(2,1)} %copy-done.15) | copy-start | bytes 602116
  121.7 13.3 %copy-start.10 = (f32[1,1,2304,256]{3,2,1,0:T(8,128)S(1)}, f32[1,1,2304,256]{3,2,1,0:T(8,128)}, u32[]{:S(2)}) copy-start(f32[1,1,2304,256]{3,2,1,0:T(8,128)} %copy-done.9) | copy-start | bytes 7077892
  124.7 10.3 %copy-start.8 = (f32[1,1,2304,256]{3,2,1,0:T(8,128)S(1)}, f32[1,1,2304,256]{3,2,1,0:T(8,128)}, u32[]{:S(2)}) copy-start(f32[1,1,2304,256]{3,2,1,0:T(8,128)} %copy-done.7) | copy-start | bytes 7077892
  128.6 6.4 %copy-start.6 = (f32[1,1,2304,256]{3,2,1,0:T(8,128)S(1)}, f32[1,1,2304,256]{3,2,1,0:T(8,128)}, u32[]{:S(2)}) copy-start(f32[1,1,2304,256]{3,2,1,0:T(8,128)} %get-tuple-element.38) | copy-start | bytes 7077892
  128.8 6.2 %copy-start.2 = (bf16[1,1,2304,256]{3,2,1,0:T(8,128)(2,1)S(1)}, bf16[1,1,2304,256]{3,2,1,0:T(8,128)(2,1)}, u32[]{:S(2)}) copy-start(bf16[1,1,2304,256]{3,2,1,0:T(8,128)(2,1)} %param.20) | copy-start | bytes 3538948
  128.8 6.2 %copy-start.5 = (f32[1,1,2304,256]{3,2,1,0:T(8,128)S(1)}, f32[1,1,2304,256]{3,2,1,0:T(8,128)}, u32[]{:S(2)}) copy-start(f32[1,1,2304,256]{3,2,1,0:T(8,128)} %copy-done.4) | copy-start | bytes 7077892
  128.9 6.2 %copy-start.31 = (f32[1,32,256]{2,1,0:T(8,128)S(1)}, f32[1,32,256]{2,1,0:T(8,128)}, u32[]{:S(2)}) copy-start(f32[1,32,256]{2,1,0:T(8,128)} %param.23) | copy-start | bytes 98308
  140.8 56.9 %all-reduce.39.cloned.1.call-start = ((), (), s32[]{:S(2)}) async-start(), calls=%async_computation.12 | async-start | bytes 720896 | tf_op jit(solution)/shard_map/psum | solution.py:125
  141.5 95.9 %reduce-scatter.19.cloned.1.call-start = ((), (), s32[]{:S(2)}) async-start(), calls=%async_computation.6 | async-start | bytes 81920
  217.7 41.6 %reduce-scatter.23.cloned.1.call-start = ((), (), s32[]{:S(2)}) async-start(), calls=%async_computation.8 | async-start | bytes 81920
  223.8 47.5 %reduce-scatter.21.cloned.1.call-start = ((), (), s32[]{:S(2)}) async-start(), calls=%async_computation.7 | async-start | bytes 49152
  238.9 44.4 %reduce-scatter.25.cloned.1.call-start = ((), (), s32[]{:S(2)}) async-start(), calls=%async_computation.9 | async-start | bytes 49152
  (24 other events, 63.4 us)
Sparse Core Ops, SparseCore 0:
  119.7 19.3 reduce-scatter.26
  141.3 10.0 reduce-scatter.28
  217.8 19.5 reduce-scatter.18
  239.7 19.5 reduce-scatter.22
  261.3 9.9 reduce-scatter.20
  273.4 9.9 reduce-scatter.24
Sparse Core Ops, SparseCore 1:
  144.4 53.2 all-reduce.38
where the time goes:
time: 293 us; the launch traced here: 292 us
  waiting for transfers between devices  115 us (39%)
  matrix products  68.9 us (24%)
  local copies, waits for them, and re-layouts  37.5 us (13%)
  other arithmetic  25 us (9%)
  blocking collectives  23.9 us (8%)
  between operations  16.9 us (6%)
  starting transfers between devices  4.56 us (2%)
    unnamed x13, waiting for transfers between devices  63.4 us
    psum x1, waiting for transfers between devices, local(): summed = lax.psum((factors[0], factors[1], factors[2]), ('node', 'local'))  44.8 us
    unnamed x121, local copies, waits for them, and re-layouts  31.1 us
    dot_general x44, matrix products, inner_rows(): lax.dot_general(left_operand, right_operand, (((0,), (0,)), ((), ())), pr...  27 us
    psum x1, blocking collectives, local(): summed = lax.psum((factors[0], factors[1], factors[2]), ('node', 'local'))  23.9 us
    dot_general x50, matrix products, inner_cols(): lax.dot_general(left_operand, right_operand, (((1,), (1,)), ((), ())), pr...  19.7 us
    another operation x9, other arithmetic, local(): jnp.linalg.cholesky(inner_cols(summed[member], summed[member], precise))  10.8 us
    dot_general x36, matrix products, block_backward(): jnp.dot(moved, spatial_weight[tap * channels:(tap + 1) * channels], prefe...  10.2 us
  transfers between devices with their start and end apart: 10, of which 8 were waited for; matrix products, arithmetic and copies ran while one was open for 25% of the time, Pallas kernels for 0%

commit v1 on v0

v1 whole, which is shorter than its diff:
```python
import functools
import math

import jax
import jax.numpy as jnp
from jax import lax
from jax.experimental import pallas as pl
from jax.experimental.pallas import tpu as pltpu
from jax.sharding import PartitionSpec as P

F32 = jnp.float32
BF16 = jnp.bfloat16
PAD = 16
REPLICA_AXES = ("node", "local")
precise = lax.Precision.HIGHEST

NN = (((1,), (0,)), ((), ()))
NT = (((1,), (1,)), ((), ()))
TN = (((0,), (0,)), ((), ()))


def mm(left, right, dims=NN, accuracy=None):
    return lax.dot_general(left, right, dims, precision=accuracy, preferred_element_type=F32)


def whole(shape):
    return pl.BlockSpec(shape, lambda i: (0,) * len(shape))


def picked(shape, index):
    return pl.BlockSpec((None,) + shape, lambda i: (index,) + (0,) * len(shape))


def call(body, name, operands, specs, outs, scratch=()):
    return pl.pallas_call(
        body,
        name=name,
        grid=(1,),
        in_specs=specs,
        out_specs=[whole(shape) for shape, _ in outs],
        out_shape=[jax.ShapeDtypeStruct(shape, kind) for shape, kind in outs],
        scratch_shapes=list(scratch),
    )(*operands)


def split(values):
    high = values.astype(BF16)
    low = (values - high.astype(F32)).astype(BF16)
    return jnp.concatenate([high, low], axis=0)


def joined(values):
    rank = values.shape[0] // 2
    return values[:rank] + values[rank:]


def low_rank(prior, grads, inputs):
    inner = joined(mm(split(prior), grads, NT))
    return joined(mm(split(inner), inputs))


def spread_taps(values, padded, columns, side, reverse):
    pixels, channels = values.shape
    column = lax.rem(lax.broadcasted_iota(jnp.int32, (pixels, 1), 0), side)
    zeros = jnp.zeros((PAD, channels), F32)
    for variant in range(3):
        padded[variant, 0:PAD] = zeros
        padded[variant, PAD + pixels : PAD + pixels + PAD] = zeros
    padded[0, PAD : PAD + pixels] = jnp.where(column != side - 1, values, 0.0)
    padded[1, PAD : PAD + pixels] = values
    padded[2, PAD : PAD + pixels] = jnp.where(column != 0, values, 0.0)
    for tap in range(9):
        source = 8 - tap if reverse else tap
        start = PAD + (source // 3 - 1) * side + source % 3 - 1
        columns[:, tap * channels : (tap + 1) * channels] = padded[
            source % 3, start : start + pixels
        ].astype(BF16)


def forward(inputs, w_reduce, w_spatial, padded, columns, hidden, slope_one, slope_two, side):
    pre = mm(inputs[...], w_reduce[...])
    logistic = jax.nn.sigmoid(pre)
    slope_one[...] = logistic * (1.0 + pre * (1.0 - logistic))
    spread_taps(pre * logistic, padded, columns, side, False)
    pre = mm(columns[...], w_spatial[...])
    logistic = jax.nn.sigmoid(pre)
    slope_two[...] = logistic * (1.0 + pre * (1.0 - logistic))
    hidden[...] = (pre * logistic).astype(BF16)


def backward(up, w_reduce, w_spatial, w_expand, slope_one, slope_two, padded, taps, side):
    channels = slope_one.shape[1]
    grad = mm(up, w_expand[...], NT) * slope_two[...]
    spread_taps(grad, padded, taps, side, True)
    back = None
    for tap in range(9):
        block = slice(tap * channels, (tap + 1) * channels)
        term = mm(taps[:, block], w_spatial[block, :], NT)
        back = term if back is None else back + term
    grad_two = grad.astype(BF16)
    grad_one = (back * slope_one[...]).astype(BF16)
    leaving = (up.astype(F32) + mm(grad_one, w_reduce[...], NT)).astype(BF16)
    return grad_two, grad_one, leaving


def first_body(side, x, up, wr, ws, we, cols, hid, gb, ga, dx, padded, taps, s1, s2):
    forward(x, wr, ws, padded, cols, hid, s1, s2, side)
    gb[...], ga[...], dx[...] = backward(up[...], wr, ws, we, s1, s2, padded, taps, side)


def ahead_body(side, count, x, wr, ws, *refs):
    padded = refs[-1]
    for step in range(count):
        cols, hid, s1, s2 = refs[4 * step : 4 * step + 4]
        forward(x.at[step + 1], wr, ws, padded, cols, hid, s1, s2, side)


def chosen(arrived, loss):
    last = lax.axis_index("section") == lax.axis_size("section") - 1
    return jnp.where(last, loss[...], arrived[...])


def middle_body(side, arrived, loss, wr, ws, we, s1, s2, up, gb, ga, dx, padded, taps):
    value = chosen(arrived, loss)
    up[...] = value
    gb[...], ga[...], dx[...] = backward(value, wr, ws, we, s1, s2, padded, taps, side)


def start_body(er, es, ee, pr, ps, pe, pt, etr, ets):
    rows, spatial = er.shape[0], es.shape[0]
    pt[:, 0:rows] = joined(mm(split(pr[...]), er[...], NT))
    pt[:, rows : rows + spatial] = joined(mm(split(ps[...]), es[...], NT))
    pt[:, rows + spatial :] = joined(mm(split(pe[...]), ee[...], NT))
    etr[...] = er[...].astype(F32).T
    ets[...] = es[...].astype(F32).T


def add_factor(pt_in, pt_out, x, cols, hid, up, gb, ga, pr, ps, pe):
    rows, spatial = x.shape[1], cols.shape[1]
    end = rows + spatial
    pt_out[:, 0:rows] = pt_in[:, 0:rows] + low_rank(pr[...], ga, x[...])
    pt_out[:, rows:end] = pt_in[:, rows:end] + low_rank(ps[...], gb, cols[...])
    pt_out[:, end:] = pt_in[:, end:] + low_rank(pe[...], up, hid[...])


def sums_body(count, x, etr, ets, ee, pt, pr, ps, pe, *refs):
    pt_out, mr, ms, me = refs[-4:]
    source = pt
    for step in range(count):
        cols, hid, up, gb, ga = refs[5 * step : 5 * step + 5]
        add_factor(source, pt_out, x.at[step], cols, hid, up[...], gb[...], ga[...], pr, ps, pe)
        source = pt_out
    for step in range(count):
        cols, hid, up, gb, ga = refs[5 * step : 5 * step + 5]
        base_r = etr[...] if step == 0 else mr[...]
        mr[...] = base_r + mm(ga[...], x[step], TN)
        base_s = ets[...] if step == 0 else ms[...]
        ms[...] = base_s + mm(gb[...], cols[...], TN)
        base_e = ee[...].astype(F32) if step == 0 else me[...]
        me[...] = base_e + mm(hid[...], up[...], TN)


def last_body(side, x, arrived, loss, wr, ws, we, cols, hid, s1, s2, pt, pr, ps, pe,
              up, gb, ga, dx, *refs):
    outs, (padded, taps, factor) = refs[:-3], refs[-3:]
    value = chosen(arrived, loss)
    up[...] = value
    gb[...], ga[...], dx[...] = backward(value, wr, ws, we, s1, s2, padded, taps, side)
    if len(outs) == 1:
        add_factor(pt, outs[0], x, cols, hid, value, gb[...], ga[...], pr, ps, pe)
        return
    add_factor(pt, factor, x, cols, hid, value, gb[...], ga[...], pr, ps, pe)
    keep, send = outs
    chips, _, width = keep.shape
    me = lax.axis_index(REPLICA_AXES)
    for chip in range(chips):
        kept = pl.multiple_of((me ^ flips(chip, False)) * width, width)
        keep[chip] = factor[:, pl.ds(kept, width)]
        sent = pl.multiple_of((me ^ flips(chip, True)) * width, width)
        send[chip] = factor[:, pl.ds(sent, width)].astype(BF16)


def finish_body(x, mr, ms, me, cols, hid, up, gb, ga, br, bs, be):
    br[...] = (mr[...] + mm(ga[...], x[...], TN)).astype(BF16)
    bs[...] = (ms[...] + mm(gb[...], cols[...], TN)).astype(BF16)
    be[...] = (me[...] + mm(hid[...], up[...], TN)).astype(BF16)


def flips(chip, other_core):
    local_bits = lax.axis_size("local").bit_length() - 1
    low = chip & (lax.axis_size("local") - 1)
    high = chip >> local_bits
    return low | (int(other_core) << local_bits) | (high << (local_bits + 1))


def swap(values, mask):
    count = lax.axis_size(REPLICA_AXES)
    return lax.ppermute(values, REPLICA_AXES, [(i, i ^ mask) for i in range(count)])


def fold_body(keep, got, own, *sends):
    own[...] = keep[0] + got[0].astype(F32)
    for chip, send in enumerate(sends, 1):
        send[...] = (keep[chip] + got[chip].astype(F32)).astype(BF16)


def total_body(own, *refs):
    total = own[...]
    for ref in refs[:-1]:
        total = total + ref[...].astype(F32)
    refs[-1][...] = total.astype(BF16)


def right_body(chips, *refs):
    mine = refs[:chips]
    other, br, bs, be, pt, keep, send, flat, pieces = refs[chips:]
    me = lax.axis_index(REPLICA_AXES)
    width = flat.shape[1] // (2 * chips)
    for chip in range(chips):
        at = pl.multiple_of((me ^ flips(chip, False)) * width, width)
        flat[:, pl.ds(at, width)] = mine[chip][...].astype(F32)
        at = pl.multiple_of((me ^ flips(chip, True)) * width, width)
        flat[:, pl.ds(at, width)] = other[chip].astype(F32)
    full = flat[...].astype(BF16)
    pt[...] = full
    rows, spatial = br.shape[1], bs.shape[1]
    parts = (
        mm(full[:, :rows], br[...], NT),
        mm(full[:, rows : rows + spatial], bs[...], NT),
        mm(full[:, rows + spatial :], be[...]),
    )
    count = 2 * chips
    for piece in range(count):
        cut = []
        for part in parts:
            wide = part.shape[1] // count
            cut.append(part[:, piece * wide : (piece + 1) * wide])
        pieces[piece] = jnp.concatenate(cut, axis=1)
    for chip in range(chips):
        keep[chip] = pieces[me ^ flips(chip, False)]
        send[chip] = pieces[me ^ flips(chip, True)].astype(BF16)


def inverse_factor(gram):
    rank = gram.shape[0]
    row = lax.broadcasted_iota(jnp.int32, (rank, 2 * rank), 0)
    lane = lax.broadcasted_iota(jnp.int32, (rank, 2 * rank), 1)
    table = jnp.concatenate([gram, jnp.zeros_like(gram)], axis=1)
    table = jnp.where(lane == row + rank, 1.0, table)
    scale = jnp.zeros((rank, 1), F32)
    for step in range(rank):
        column = table[:, step : step + 1]
        pivot = table[step : step + 1, step : step + 1]
        ratio = column / pivot
        scale = jnp.where(row[:, :1] == step, lax.rsqrt(pivot), scale)
        table = jnp.where(row > step, table - ratio * table[step : step + 1, :], table)
    return table[:, rank:] * scale


def basis_body(splits, pt, inverse, *outs):
    me = lax.axis_index(REPLICA_AXES)
    count = lax.axis_size(REPLICA_AXES)
    start = 0
    for member, rows in enumerate(splits):
        full = pt[:, start : start + rows]
        linv = inverse_factor(mm(full, full, NT))
        inverse[member] = linv
        wide = rows // count
        window = min(-(-wide // 128) * 128 + (128 if 128 % wide and wide % 128 else 0), rows)
        first = me * wide
        aligned = pl.multiple_of(first // 128 * 128, 128)
        block = pt[:, pl.ds(start + aligned, window)].astype(F32)
        moved = pltpu.roll(block, lax.rem(window - (first - aligned), window), 1)
        outs[member][...] = math.sqrt(rows) * mm(linv, moved[:, :wide], NN, precise)
        start += rows


def end_body(splits, replicas, inverse, own, a, b, c, *outs):
    total = own[...] + a[...].astype(F32) + b[...].astype(F32) + c[...].astype(F32)
    start = 0
    for member, out in enumerate(outs):
        wide = out.shape[1]
        scale = 1.0 / (replicas * math.sqrt(splits[member]))
        out[...] = scale * mm(inverse[member], total[:, start : start + wide], NN, precise)
        start += wide


def shifted(block):
    count = lax.axis_size("section")
    return lax.ppermute(block, "section", [(i, i - 1) for i in range(1, count)])


def specs_of(operands):
    return [whole(operand.shape) for operand in operands]


def general_tail(pt, matrices, splits):
    replicas = lax.axis_size(REPLICA_AXES)
    me = lax.axis_index(REPLICA_AXES)
    total = lax.psum(pt, REPLICA_AXES)
    bases, rights = [], []
    start = 0
    for member, rows in enumerate(splits):
        part = total[:, start : start + rows]
        start += rows
        triangle = jnp.linalg.cholesky(mm(part, part, NT, precise))
        unit = lax.linalg.triangular_solve(triangle, part, left_side=True, lower=True)
        wide = rows // replicas
        own = lax.dynamic_slice_in_dim(unit, me * wide, wide, 1)
        bases.append(math.sqrt(rows) * own)
        matrix = matrices[member].astype(F32)
        dims = NN if member == 2 else NT
        right = mm(unit, matrix, dims, precise)
        right = lax.psum_scatter(
            right.astype(BF16), REPLICA_AXES, scatter_dimension=1, tiled=True
        ).astype(F32)
        rights.append(right / (replicas * math.sqrt(rows)))
    return bases, rights


def local(
    section_inputs,
    grad_in,
    loss_grad,
    w_reduce,
    w_spatial,
    w_expand,
    err_reduce,
    err_spatial,
    err_expand,
    prior_reduce,
    prior_spatial,
    prior_expand,
):
    x = section_inputs[0, 0]
    loss = loss_grad[0]
    wr, ws, we = w_reduce[0], w_spatial[0], w_expand[0]
    er, es, ee = err_reduce[0, 0], err_spatial[0, 0], err_expand[0, 0]
    pr, ps, pe = prior_reduce[0], prior_spatial[0], prior_expand[0]
    ticks, pixels, out = x.shape
    mid = wr.shape[1]
    taps = ws.shape[0]
    rank = pr.shape[0]
    side = math.isqrt(pixels)
    total = out + taps + mid
    splits = (out, taps, mid)

    image = (pixels, out)
    inner = (pixels, mid)
    wide = (pixels, taps)
    padded = pltpu.VMEM((3, pixels + 2 * PAD, mid), F32)
    tap_space = pltpu.VMEM(wide, BF16)
    saved = [(wide, BF16), (inner, BF16), (inner, F32), (inner, F32)]
    grads = [(inner, BF16), (inner, BF16), (image, BF16)]

    weights = (wr, ws, we)
    up = grad_in[0, 0]
    cols, hid, gb, ga, dx = call(
        functools.partial(first_body, side),
        "first_tick",
        (x, up) + weights,
        [picked(image, 0)] + specs_of((up,) + weights),
        saved[:2] + grads,
        (padded, tap_space, pltpu.VMEM(inner, F32), pltpu.VMEM(inner, F32)),
    )
    done = [(cols, hid, up, gb, ga)]
    arrived = shifted(dx)
    ahead = call(
        functools.partial(ahead_body, side, ticks - 1),
        "forward_ahead",
        (x, wr, ws),
        specs_of((x, wr, ws)),
        saved * (ticks - 1),
        (padded,),
    )
    pt, etr, ets = call(
        start_body,
        "error_terms",
        (er, es, ee, pr, ps, pe),
        specs_of((er, es, ee, pr, ps, pe)),
        [((rank, total), F32), ((mid, out), F32), ((mid, taps), F32)],
    )
    for tick in range(1, ticks - 1):
        cols, hid, s1, s2 = ahead[4 * tick - 4 : 4 * tick]
        operands = weights + (s1, s2)
        up, gb, ga, dx = call(
            functools.partial(middle_body, side),
            "middle_tick",
            (arrived, loss) + operands,
            [whole(image), picked(image, tick - 1)] + specs_of(operands),
            [(image, BF16)] + grads,
            (padded, tap_space),
        )
        done.append((cols, hid, up, gb, ga))
        arrived = shifted(dx)
    flat = tuple(part for group in done for part in group)
    operands = (x, etr, ets, ee, pt, pr, ps, pe) + flat
    pt, mr, ms, me = call(
        functools.partial(sums_body, ticks - 1),
        "running_sums",
        operands,
        specs_of(operands),
        [((rank, total), F32), ((mid, out), F32), ((mid, taps), F32), ((mid, out), F32)],
    )

    replicas = lax.axis_size(REPLICA_AXES)
    piece = total // replicas
    fast = replicas == 8 and lax.axis_size("node") == 4 and piece % 128 == 0
    chips = replicas // 2
    cols, hid, s1, s2 = ahead[4 * ticks - 8 : 4 * ticks - 4]
    operands = weights + (cols, hid, s1, s2, pt, pr, ps, pe)
    parts = (chips, rank, piece)
    extra = [(parts, F32), (parts, BF16)] if fast else [((rank, total), F32)]
    up, gb, ga, leaving, *factor = call(
        functools.partial(last_body, side),
        "last_tick",
        (x, arrived, loss) + operands,
        [picked(image, ticks - 1), whole(image), picked(image, ticks - 2)] + specs_of(operands),
        [(image, BF16)] + grads + extra,
        (padded, tap_space, pltpu.VMEM((rank, total), F32)),
    )
    operands = (mr, ms, me, cols, hid, up, gb, ga)
    matrices = call(
        finish_body,
        "final_sums",
        (x,) + operands,
        [picked(image, ticks - 1)] + specs_of(operands),
        [((mid, out), BF16), ((mid, taps), BF16), ((mid, out), BF16)],
    )
    if not fast:
        bases, rights = general_tail(factor[0], matrices, splits)
        return tuple(value[None] for value in [leaving[None], *bases, *rights])

    def scattered(keep, send, name):
        got = swap(send, flips(0, True))
        own, *sends = call(
            fold_body,
            name,
            (keep, got),
            specs_of((keep, got)),
            [(keep.shape[1:], F32)] + [(keep.shape[1:], BF16)] * (chips - 1),
        )
        return own, [swap(value, flips(chip, False)) for chip, value in enumerate(sends, 1)]

    own, others = scattered(*factor, "fold_factor")
    (own,) = call(
        total_body,
        "total_factor",
        (own, *others),
        specs_of((own, *others)),
        [((rank, piece), BF16)],
    )
    mine = [own] + [swap(own, flips(chip, False)) for chip in range(1, chips)]
    other = swap(jnp.stack(mine), flips(0, True))
    part = (mid + mid + out) // replicas
    operands = (*mine, other, *matrices)
    pt, keep, send = call(
        functools.partial(right_body, chips),
        "right_products",
        operands,
        specs_of(operands),
        [((rank, total), BF16), ((chips, rank, part), F32), ((chips, rank, part), BF16)],
        (pltpu.VMEM((rank, total), F32), pltpu.VMEM((replicas, rank, part), F32)),
    )
    own, others = scattered(keep, send, "fold_right")
    inverse, *bases = call(
        functools.partial(basis_body, splits),
        "basis",
        (pt,),
        specs_of((pt,)),
        [((3, rank, rank), F32)] + [((rank, rows // replicas), F32) for rows in splits],
    )
    operands = (inverse, own, *others)
    rights = call(
        functools.partial(end_body, splits, replicas),
        "right_factors",
        operands,
        specs_of(operands),
        [((rank, columns // replicas), F32) for columns in (mid, mid, out)],
    )
    return tuple(value[None] for value in [leaving[None], *bases, *rights])


def solution(mesh):
    replica = P("section", REPLICA_AXES)
    weight = P("section")
    column = P("section", None, REPLICA_AXES)
    return jax.shard_map(
        local,
        mesh=mesh,
        in_specs=(replica, replica, P(REPLICA_AXES)) + (weight,) * 3 + (replica,) * 3 + (weight,) * 3,
        out_specs=(replica,) + (column,) * 6,
        check_vma=False,
    )
```

time: 293 us -> 98.7 us (0.34)
  waiting for transfers between devices: 115 us -> 20.4 us
  matrix products: 68.9 us -> 0 us
  Pallas kernels: 0 us -> 53.7 us
  local copies, waits for them, and re-layouts: 37.5 us -> 7.32 us
  other arithmetic: 25 us -> 0.77 us
  blocking collectives: 23.9 us -> 0 us
  between operations: 16.9 us -> 0.77 us
  starting transfers between devices: 4.56 us -> 15 us
    dot_general x137 -> x0, matrix products: 66.1 us -> none  [the longest x44 27 us: inner_rows(): lax.dot_general(left_operand, right_operand, (((0,), (0,)), ((), ())), pr...]
    unnamed x13 -> x0, waiting for transfers between devices: 63.4 us -> none
    pallas_call x0 -> x14, Pallas kernels: none -> 53.7 us  [call(): pl.pallas_call(body, name=name, grid=(1,), in_specs=specs, out_specs=[who...]
    psum x1 -> x0, waiting for transfers between devices: 44.8 us -> none  [local(): summed = lax.psum((factors[0], factors[1], factors[2]), ('node', 'local'))]
    psum x1 -> x0, blocking collectives: 23.9 us -> none  [local(): summed = lax.psum((factors[0], factors[1], factors[2]), ('node', 'local'))]
    unnamed x121 -> x31, local copies, waits for them, and re-layouts: 31.1 us -> 7.32 us
    another operation x15 -> x1, other arithmetic: 20 us -> 0.77 us  [local(): other = swap(jnp.stack(mine), flips(0, True))]
    ppermute x3 -> x15, waiting for transfers between devices: 7.23 us -> 20.4 us  [the longest x3 10.8 us: shifted(): return lax.ppermute(block, 'section', [(i, i - 1) for i in range(1, count)])]
  transfers between devices with their start and end apart: 10 -> 15, of which waited for: 8 -> 10; matrix products, arithmetic and copies ran while one was open for 25% -> 0% of each run, Pallas kernels for 0% -> 29%
where the time goes in v1:
time: 98.7 us; the launch traced here: 98 us
  Pallas kernels  53.7 us (54%)
  waiting for transfers between devices  20.4 us (21%)
  starting transfers between devices  15 us (15%)
  local copies, waits for them, and re-layouts  7.32 us (7%)
    pallas_call x14, Pallas kernels, call(): pl.pallas_call(body, name=name, grid=(1,), in_specs=specs, out_specs=[who...  53.7 us
    ppermute x12, starting transfers between devices, swap(): lax.ppermute(values, REPLICA_AXES, [(i, i ^ mask) for i in range(count)])  11 us
    ppermute x3, waiting for transfers between devices, shifted(): return lax.ppermute(block, 'section', [(i, i - 1) for i in range(1, count)])  10.8 us
    ppermute x12, waiting for transfers between devices, swap(): lax.ppermute(values, REPLICA_AXES, [(i, i ^ mask) for i in range(count)])  9.52 us
    unnamed x31, local copies, waits for them, and re-layouts  7.32 us
    ppermute x3, starting transfers between devices, shifted(): return lax.ppermute(block, 'section', [(i, i - 1) for i in range(1, count)])  4.02 us
  transfers between devices with their start and end apart: 15, of which 10 were waited for; matrix products, arithmetic and copies ran while one was open for 0% of the time, Pallas kernels for 29%

profile of v1, /device:TPU:0, one launch (start us, length us, event | category | flops | bytes accessed | tf_op | source)
XLA Modules:
  0.0 98.0 jit_solution(7623004711417577723)
XLA Ops:
  0.6 2.2 %copy.21 = bf16[1,1,4,196,512]{4,3,2,1,0:T(8,128)(2,1)} copy(bf16[1,1,4,196,512]{4,2,3,1,0:T(4,128)(2,1)} %param.12) | data formatting | bytes 1605632 | tf_op args[0]
  2.8 4.1 %first_tick.1 = (bf16[196,2304]{1,0:T(8,128)(2,1)}, bf16[196,256]{1,0:T(8,128)(2,1)}, bf16[196,256]{1,0:T(8,128)(2,1)}, bf16[196,256]{1,0:T(8,128)(2,1)}, bf16[196,512]{1,0:T(8,128)(2,1)}) custom-call(bf16[4,196,512]{2,1,0:T(8,128)(2,1)} %bitcast.25, bf16[196,512]{1,0:T(8,128)(2,1)} %bitcast.50, bf16[512,256]{1,0:T(8,128)(2,1)} %bitcast.35, ...), custom_call_target="tpu_custom_call" | custom-call | tf_op jit(solution)/shard_map/first_tick/pallas_call | solution.py:35
  8.2 5.2 %forward_ahead.1 = (bf16[196,2304]{1,0:T(8,128)(2,1)}, bf16[196,256]{1,0:T(8,128)(2,1)}, f32[196,256]{1,0:T(8,128)}, f32[196,256]{1,0:T(8,128)}, bf16[196,2304]{...) custom-call(bf16[4,196,512]{2,1,0:T(8,128)(2,1)} %bitcast.26, ...), custom_call_target="tpu_custom_call" | custom-call | tf_op jit(solution)/shard_map/forward_ahead/pallas_call | solution.py:35
  13.4 3.8 %collective-permute-done.arrived = bf16[196,512]{1,0:T(8,128)(2,1)S(1)} collective-permute-done((bf16[196,512]{1,0:T(8,128)(2,1)}, bf16[196,512]{1,0:T(8,128)(2,1)S(1)}, u32[]{:S(2)}, u32[]{:S(2)}) %collective-permute-start) | collective-permute-done | bytes 200736 | tf_op jit(solution)/shard_map/ppermute | solution.py:290
  17.8 3.5 %middle_tick.2 = (bf16[196,512]{1,0:T(8,128)(2,1)}, bf16[196,256]{1,0:T(8,128)(2,1)}, bf16[196,256]{1,0:T(8,128)(2,1)}, bf16[196,512]{1,0:T(8,128)(2,1)}) custom-call(bf16[196,512]{1,0:T(8,128)(2,1)} %copy-done, bf16[3,196,512]{2,1,0:T(8,128)(2,1)} %bitcast.40, bf16[512,256]{1,0:T(8,128)(2,1)} %bitcast.37, bf16[2304,256]{1,0:T(8,128)(2,1)} %bitcast.32, ...), custom_call_target="tpu_custom_call" | custom-call | tf_op jit(solution)/shard_map/middle_tick/pallas_call | solution.py:35
  22.6 7.0 %collective-permute-done.1.arrived = bf16[196,512]{1,0:T(8,128)(2,1)S(1)} collective-permute-done((bf16[196,512]{1,0:T(8,128)(2,1)}, bf16[196,512]{1,0:T(8,128)(2,1)S(1)}, u32[]{:S(2)}, u32[]{:S(2)}) %collective-permute-start.1) | collective-permute-done | bytes 200736 | tf_op jit(solution)/shard_map/ppermute | solution.py:290
  30.3 3.5 %middle_tick.3 = (bf16[196,512]{1,0:T(8,128)(2,1)}, bf16[196,256]{1,0:T(8,128)(2,1)}, bf16[196,256]{1,0:T(8,128)(2,1)}, bf16[196,512]{1,0:T(8,128)(2,1)}) custom-call(bf16[196,512]{1,0:T(8,128)(2,1)} %copy-done.1, bf16[3,196,512]{2,1,0:T(8,128)(2,1)} %bitcast.41, bf16[512,256]{1,0:T(8,128)(2,1)} %bitcast.38, bf16[2304,256]{1,0:T(8,128)(2,1)} %bitcast.33, ...), custom_call_target="tpu_custom_call" | custom-call | tf_op jit(solution)/shard_map/middle_tick/pallas_call | solution.py:35
  33.8 1.5 %collective-permute-start.2 = (bf16[196,512]{1,0:T(8,128)(2,1)}, bf16[196,512]{1,0:T(8,128)(2,1)S(1)}, u32[]{:S(2)}, u32[]{:S(2)}) collective-permute-start(bf16[196,512]{1,0:T(8,128)(2,1)} %get-tuple-element.72), channel_id=1, source_target_pairs={{8,0},{16,8},{24,16},{9,1},{17,9},{25,17},{10,2},{18,10},{26,18},{... | collective-permute-start | bytes 602120 | tf_op jit(solution)/shard_map/ppermute | solution.py:290
  35.3 3.5 %error_terms.1 = (f32[32,3072]{1,0:T(8,128)}, f32[256,512]{1,0:T(8,128)}, f32[256,2304]{1,0:T(8,128)}) custom-call(bf16[512,256]{1,0:T(8,128)(2,1)} %bitcast.61, bf16[2304,256]{1,0:T(8,128)(2,1)} %bitcast.47, bf16[256,512]{1,0:T(8,128)(2,1)} %bitcast.48, f32[32,256]{1,0:T(8,128)} %bitcast.55, f32[32,256]{1,0:T(8,128)} %bitcast.58, f32[32,512]{1,0:T(8,128)} %bitcast.52), custom_call_target="tpu_custom_call" | custom-call | tf_op jit(solution)/shard_map/error_terms/pallas_call | solution.py:35
  38.8 8.4 %running_sums.1 = (f32[32,3072]{1,0:T(8,128)}, f32[256,512]{1,0:T(8,128)}, f32[256,2304]{1,0:T(8,128)}, f32[256,512]{1,0:T(8,128)}) custom-call(bf16[4,196,512]{2,1,0:T(8,128)(2,1)} %bitcast.27, f32[256,512]{1,0:T(8,128)} %get-tuple-element.77.etr, f32[256,2304]{1,0:T(8,128)} %get-tuple-element.78.ets, bf16[256,512]{1,0:T(8,128)(2,1)} %bitcast.49, ...), custom_call_target="tpu_custom_call" | custom-call | tf_op jit(solution)/shard_map/running_sums/pallas_call | solution.py:35
  47.9 4.8 %last_tick.1 = (bf16[196,512]{1,0:T(8,128)(2,1)}, bf16[196,256]{1,0:T(8,128)(2,1)}, bf16[196,256]{1,0:T(8,128)(2,1)}, bf16[196,512]{1,0:T(8,128)(2,1)}, f32[4,32...) custom-call(bf16[4,196,512]{2,1,0:T(8,128)(2,1)} %bitcast.28, bf16[196,512]{1,0:T(8,128)(2,1)} %copy-done.2, ...), custom_call_target="tpu_custom_call" | custom-call | tf_op jit(solution)/shard_map/last_tick/pallas_call | solution.py:35
  52.7 1.5 %collective-permute-done.3.got = bf16[4,32,384]{2,1,0:T(8,128)(2,1)S(1)} collective-permute-done((bf16[4,32,384]{2,1,0:T(8,128)(2,1)}, bf16[4,32,384]{2,1,0:T(8,128)(2,1)S(1)}, u32[]{:S(2)}, u32[]{:S(2)}) %collective-permute-start.3) | collective-permute-done | bytes 98336 | tf_op jit(solution)/shard_map/ppermute | solution.py:198
  54.8 1.6 %fold_factor.1 = (f32[32,384]{1,0:T(8,128)}, bf16[32,384]{1,0:T(8,128)(2,1)}, bf16[32,384]{1,0:T(8,128)(2,1)}, bf16[32,384]{1,0:T(8,128)(2,1)}) custom-call(f32[4,32,384]{2,1,0:T(8,128)} %get-tuple-element.96.keep, bf16[4,32,384]{2,1,0:T(8,128)(2,1)} %copy-done.3), custom_call_target="tpu_custom_call" | custom-call | tf_op jit(solution)/shard_map/fold_factor/pallas_call | solution.py:35
  57.9 1.5 %collective-permute-start.5 = (bf16[32,384]{1,0:T(8,128)(2,1)}, bf16[32,384]{1,0:T(8,128)(2,1)S(1)}, u32[]{:S(2)}, u32[]{:S(2)}) collective-permute-start(bf16[32,384]{1,0:T(8,128)(2,1)} %get-tuple-element.100), channel_id=1, source_target_pairs={{0,4},{1,5},{2,6},{3,7},{4,0},{5,1},{6,2},{7,3},{8,12},{9,13},{10,... | collective-permute-start | bytes 73736 | tf_op jit(solution)/shard_map/ppermute | solution.py:198
  60.5 1.6 %collective-permute-done.5.refs_1_ = bf16[32,384]{1,0:T(8,128)(2,1)S(1)} collective-permute-done((bf16[32,384]{1,0:T(8,128)(2,1)}, bf16[32,384]{1,0:T(8,128)(2,1)S(1)}, u32[]{:S(2)}, u32[]{:S(2)}) %collective-permute-start.5) | collective-permute-done | bytes 24608 | tf_op jit(solution)/shard_map/ppermute | solution.py:198
  62.1 2.2 %collective-permute-done.6.refs_2_ = bf16[32,384]{1,0:T(8,128)(2,1)S(1)} collective-permute-done((bf16[32,384]{1,0:T(8,128)(2,1)}, bf16[32,384]{1,0:T(8,128)(2,1)S(1)}, u32[]{:S(2)}, u32[]{:S(2)}) %collective-permute-start.6) | collective-permute-done | bytes 24608 | tf_op jit(solution)/shard_map/ppermute | solution.py:198
  67.5 2.3 %collective-permute-start.9 = (bf16[32,384]{1,0:T(8,128)(2,1)}, bf16[32,384]{1,0:T(8,128)(2,1)S(1)}, u32[]{:S(2)}, u32[]{:S(2)}) collective-permute-start(bf16[32,384]{1,0:T(8,128)(2,1)} %total_factor.1.refs_0_), channel_id=1, source_target_pairs={{0,5},{1,4},{2,7},{3,6},{4,1},{5,0},{6,3},{7,2},{8,13},{9,12},{10,... | collective-permute-start | bytes 73736 | tf_op jit(solution)/shard_map/ppermute | solution.py:198
  70.9 1.6 %collective-permute-done.9.refs_3_ = bf16[32,384]{1,0:T(8,128)(2,1)S(1)} collective-permute-done((bf16[32,384]{1,0:T(8,128)(2,1)}, bf16[32,384]{1,0:T(8,128)(2,1)S(1)}, u32[]{:S(2)}, u32[]{:S(2)}) %collective-permute-start.9) | collective-permute-done | bytes 24608 | tf_op jit(solution)/shard_map/ppermute | solution.py:198
  73.3 4.1 %final_sums.1 = (bf16[256,512]{1,0:T(8,128)(2,1)}, bf16[256,2304]{1,0:T(8,128)(2,1)}, bf16[256,512]{1,0:T(8,128)(2,1)}) custom-call(bf16[4,196,512]{2,1,0:T(8,128)(2,1)} %bitcast.29, f32[256,512]{1,0:T(8,128)} %get-tuple-element.102.mr, f32[256,2304]{1,0:T(8,128)} %get-tuple-element.103.ms, f32[256,512]{1,0:T(8,128)} %get-tuple-element.104.me, ...), custom_call_target="tpu_custom_call" | custom-call | tf_op jit(solution)/shard_map/final_sums/pallas_call | solution.py:35
  78.0 2.8 %right_products.1 = (bf16[32,3072]{1,0:T(8,128)(2,1)}, f32[4,32,128]{2,1,0:T(8,128)}, bf16[4,32,128]{2,1,0:T(8,128)(2,1)}) custom-call(bf16[32,384]{1,0:T(8,128)(2,1)} %total_factor.1.refs_0_, bf16[32,384]{1,0:T(8,128)(2,1)} %copy-done.5, bf16[32,384]{1,0:T(8,128)(2,1)} %copy-done.6, bf16[32,384]{1,0:T(8,128)(2,1)} %copy-done.7, ...), custom_call_target="tpu_custom_call" | custom-call | tf_op jit(solution)/shard_map/right_products/pallas_call | solution.py:35
  83.0 1.5 %fold_right.1 = (f32[32,128]{1,0:T(8,128)}, bf16[32,128]{1,0:T(8,128)(2,1)}, bf16[32,128]{1,0:T(8,128)(2,1)}, bf16[32,128]{1,0:T(8,128)(2,1)}) custom-call(f32[4,32,128]{2,1,0:T(8,128)} %get-tuple-element.116.keep, bf16[4,32,128]{2,1,0:T(8,128)(2,1)} %copy-done.8), custom_call_target="tpu_custom_call" | custom-call | tf_op jit(solution)/shard_map/fold_right/pallas_call | solution.py:35
  85.9 1.5 %collective-permute-start.13 = (bf16[32,128]{1,0:T(8,128)(2,1)}, bf16[32,128]{1,0:T(8,128)(2,1)S(1)}, u32[]{:S(2)}, u32[]{:S(2)}) collective-permute-start(bf16[32,128]{1,0:T(8,128)(2,1)} %get-tuple-element.120), channel_id=1, source_target_pairs={{0,4},{1,5},{2,6},{3,7},{4,0},{5,1},{6,2},{7,3},{8,12},{9,13},{10,... | collective-permute-start | bytes 24584 | tf_op jit(solution)/shard_map/ppermute | solution.py:198
  88.0 7.7 %basis.1 = (f32[3,32,32]{2,1,0:T(8,128)}, f32[32,64]{1,0:T(8,128)}, f32[32,288]{1,0:T(8,128)}, f32[32,32]{1,0:T(8,128)}) custom-call(bf16[32,3072]{1,0:T(8,128)(2,1)} %get-tuple-element.111.pt), custom_call_target="tpu_custom_call" | custom-call | tf_op jit(solution)/shard_map/basis/pallas_call | solution.py:35
  96.3 1.7 %right_factors.1 = (f32[32,32]{1,0:T(8,128)}, f32[32,32]{1,0:T(8,128)}, f32[32,64]{1,0:T(8,128)}) custom-call(f32[3,32,32]{2,1,0:T(8,128)} %get-tuple-element.115.inverse, f32[32,128]{1,0:T(8,128)} %get-tuple-element.118.own, bf16[32,128]{1,0:T(8,128)(2,1)} %copy-done.12, bf16[32,128]{1,0:T(8,128)(2,1)} %copy-done.13, bf16[32,128]{1,0:T(8,128)(2,1)} %copy-done.14), custom_call_target="tpu_custom_call" | custom-call | tf_op jit(solution)/shard_map/right_factors/pallas_call | solution.py:35
  (52 shorter events, 18.3 us)
Async XLA Ops:
  6.9 10.2 %collective-permute-start = (bf16[196,512]{1,0:T(8,128)(2,1)}, bf16[196,512]{1,0:T(8,128)(2,1)S(1)}, u32[]{:S(2)}, u32[]{:S(2)}) collective-permute-start(bf16[196,512]{1,0:T(8,128)(2,1)} %get-tuple-element.66), channel_id=1, source_target_pairs={{8,0},{16,8},{24,16},{9,1},{17,9},{25,17},{10,2},{18,10},{26,18},{... | collective-permute-start | bytes 602120 | tf_op jit(solution)/shard_map/ppermute | solution.py:290
  17.2 0.7 copy-start
  21.3 8.3 %collective-permute-start.1 = (bf16[196,512]{1,0:T(8,128)(2,1)}, bf16[196,512]{1,0:T(8,128)(2,1)S(1)}, u32[]{:S(2)}, u32[]{:S(2)}) collective-permute-start(bf16[196,512]{1,0:T(8,128)(2,1)} %get-tuple-element.69), channel_id=1, source_target_pairs={{8,0},{16,8},{24,16},{9,1},{17,9},{25,17},{10,2},{18,10},{26,18},{... | collective-permute-start | bytes 602120 | tf_op jit(solution)/shard_map/ppermute | solution.py:290
  29.6 0.7 copy-start.1
  33.8 13.4 %collective-permute-start.2 = (bf16[196,512]{1,0:T(8,128)(2,1)}, bf16[196,512]{1,0:T(8,128)(2,1)S(1)}, u32[]{:S(2)}, u32[]{:S(2)}) collective-permute-start(bf16[196,512]{1,0:T(8,128)(2,1)} %get-tuple-element.72), channel_id=1, source_target_pairs={{8,0},{16,8},{24,16},{9,1},{17,9},{25,17},{10,2},{18,10},{26,18},{... | collective-permute-start | bytes 602120 | tf_op jit(solution)/shard_map/ppermute | solution.py:290
  47.2 0.7 copy-start.2
  52.7 1.5 %collective-permute-start.3 = (bf16[4,32,384]{2,1,0:T(8,128)(2,1)}, bf16[4,32,384]{2,1,0:T(8,128)(2,1)S(1)}, u32[]{:S(2)}, u32[]{:S(2)}) collective-permute-start(bf16[4,32,384]{2,1,0:T(8,128)(2,1)} %get-tuple-element.97), channel_id=1, source_target_pairs={{0,2},{1,3},{2,0},{3,1},{4,6},{5,7},{6,4},{7,5},{8,10},{9,11},{10,... | collective-permute-start | bytes 294920 | tf_op jit(solution)/shard_map/ppermute | solution.py:198
  56.4 4.0 %collective-permute-start.4 = (bf16[32,384]{1,0:T(8,128)(2,1)}, bf16[32,384]{1,0:T(8,128)(2,1)S(1)}, u32[]{:S(2)}, u32[]{:S(2)}) collective-permute-start(bf16[32,384]{1,0:T(8,128)(2,1)} %get-tuple-element.99), channel_id=1, source_target_pairs={{0,1},{1,0},{2,3},{3,2},{4,5},{5,4},{6,7},{7,6},{8,9},{9,8},{10,11... | collective-permute-start | bytes 73736 | tf_op jit(solution)/shard_map/ppermute | solution.py:198
  57.9 4.3 %collective-permute-start.5 = (bf16[32,384]{1,0:T(8,128)(2,1)}, bf16[32,384]{1,0:T(8,128)(2,1)S(1)}, u32[]{:S(2)}, u32[]{:S(2)}) collective-permute-start(bf16[32,384]{1,0:T(8,128)(2,1)} %get-tuple-element.100), channel_id=1, source_target_pairs={{0,4},{1,5},{2,6},{3,7},{4,0},{5,1},{6,2},{7,3},{8,12},{9,13},{10,... | collective-permute-start | bytes 73736 | tf_op jit(solution)/shard_map/ppermute | solution.py:198
  59.3 4.9 %collective-permute-start.6 = (bf16[32,384]{1,0:T(8,128)(2,1)}, bf16[32,384]{1,0:T(8,128)(2,1)S(1)}, u32[]{:S(2)}, u32[]{:S(2)}) collective-permute-start(bf16[32,384]{1,0:T(8,128)(2,1)} %get-tuple-element.101), channel_id=1, source_target_pairs={{0,5},{1,4},{2,7},{3,6},{4,1},{5,0},{6,3},{7,2},{8,13},{9,12},{10,... | collective-permute-start | bytes 73736 | tf_op jit(solution)/shard_map/ppermute | solution.py:198
  60.5 3.8 %copy-start.9 = (bf16[32,384]{1,0:T(8,128)(2,1)}, bf16[32,384]{1,0:T(8,128)(2,1)S(1)}, u32[]{:S(2)}) copy-start(bf16[32,384]{1,0:T(8,128)(2,1)S(1)} %collective-permute-done.4.refs_0_) | copy-start | bytes 73732
  62.1 2.2 %copy-start.10 = (bf16[32,384]{1,0:T(8,128)(2,1)}, bf16[32,384]{1,0:T(8,128)(2,1)S(1)}, u32[]{:S(2)}) copy-start(bf16[32,384]{1,0:T(8,128)(2,1)S(1)} %collective-permute-done.5.refs_1_) | copy-start | bytes 73732
  66.3 4.0 %collective-permute-start.7 = (bf16[32,384]{1,0:T(8,128)(2,1)}, bf16[32,384]{1,0:T(8,128)(2,1)S(1)}, u32[]{:S(2)}, u32[]{:S(2)}) collective-permute-start(bf16[32,384]{1,0:T(8,128)(2,1)} %total_factor.1.refs_0_), channel_id=1, source_target_pairs={{0,1},{1,0},{2,3},{3,2},{4,5},{5,4},{6,7},{7,6},{8,9},{9,8},{10,11... | collective-permute-start | bytes 73736 | tf_op jit(solution)/shard_map/ppermute | solution.py:198
  66.8 4.0 %collective-permute-start.8 = (bf16[32,384]{1,0:T(8,128)(2,1)}, bf16[32,384]{1,0:T(8,128)(2,1)S(1)}, u32[]{:S(2)}, u32[]{:S(2)}) collective-permute-start(bf16[32,384]{1,0:T(8,128)(2,1)} %total_factor.1.refs_0_), channel_id=1, source_target_pairs={{0,4},{1,5},{2,6},{3,7},{4,0},{5,1},{6,2},{7,3},{8,12},{9,13},{10,... | collective-permute-start | bytes 73736 | tf_op jit(solution)/shard_map/ppermute | solution.py:198
  67.5 4.9 %collective-permute-start.9 = (bf16[32,384]{1,0:T(8,128)(2,1)}, bf16[32,384]{1,0:T(8,128)(2,1)S(1)}, u32[]{:S(2)}, u32[]{:S(2)}) collective-permute-start(bf16[32,384]{1,0:T(8,128)(2,1)} %total_factor.1.refs_0_), channel_id=1, source_target_pairs={{0,5},{1,4},{2,7},{3,6},{4,1},{5,0},{6,3},{7,2},{8,13},{9,12},{10,... | collective-permute-start | bytes 73736 | tf_op jit(solution)/shard_map/ppermute | solution.py:198
  70.4 7.0 %copy-start.5 = (bf16[32,384]{1,0:T(8,128)(2,1)}, bf16[32,384]{1,0:T(8,128)(2,1)S(1)}, u32[]{:S(2)}) copy-start(bf16[32,384]{1,0:T(8,128)(2,1)S(1)} %collective-permute-done.7.refs_1_) | copy-start | bytes 73732
  70.9 6.5 %copy-start.6 = (bf16[32,384]{1,0:T(8,128)(2,1)}, bf16[32,384]{1,0:T(8,128)(2,1)S(1)}, u32[]{:S(2)}) copy-start(bf16[32,384]{1,0:T(8,128)(2,1)S(1)} %collective-permute-done.8.refs_2_) | copy-start | bytes 73732
  72.4 5.0 %copy-start.7 = (bf16[32,384]{1,0:T(8,128)(2,1)}, bf16[32,384]{1,0:T(8,128)(2,1)S(1)}, u32[]{:S(2)}) copy-start(bf16[32,384]{1,0:T(8,128)(2,1)S(1)} %collective-permute-done.9.refs_3_) | copy-start | bytes 73732
  73.2 4.2 %collective-permute-start.10 = (bf16[4,32,384]{2,1,0:T(8,128)(2,1)S(1)}, bf16[4,32,384]{2,1,0:T(8,128)(2,1)S(1)}, u32[]{:S(2)}, u32[]{:S(2)}) collective-permute-start(bf16[4,32,384]{2,1,0:T(8,128)(2,1)S(1)} %pad_maximum_fusion), channel_id=1, source_target_pairs={{0,2},{1,3},{2,0},{3,1},{4,6},{5,7},{6,4},{7,5},{8,10},{9,11},{10,... | collective-permute-start | bytes 294920 | tf_op jit(solution)/shard_map/ppermute | solution.py:198
  77.4 0.6 copy-start.4
  80.9 1.6 %collective-permute-start.11 = (bf16[4,32,128]{2,1,0:T(8,128)(2,1)}, bf16[4,32,128]{2,1,0:T(8,128)(2,1)S(1)}, u32[]{:S(2)}, u32[]{:S(2)}) collective-permute-start(bf16[4,32,128]{2,1,0:T(8,128)(2,1)} %get-tuple-element.117), channel_id=1, source_target_pairs={{0,2},{1,3},{2,0},{3,1},{4,6},{5,7},{6,4},{7,5},{8,10},{9,11},{10,... | collective-permute-start | bytes 98312 | tf_op jit(solution)/shard_map/ppermute | solution.py:198
  84.5 11.2 %collective-permute-start.12 = (bf16[32,128]{1,0:T(8,128)(2,1)}, bf16[32,128]{1,0:T(8,128)(2,1)S(1)}, u32[]{:S(2)}, u32[]{:S(2)}) collective-permute-start(bf16[32,128]{1,0:T(8,128)(2,1)} %get-tuple-element.119), channel_id=1, source_target_pairs={{0,1},{1,0},{2,3},{3,2},{4,5},{5,4},{6,7},{7,6},{8,9},{9,8},{10,11... | collective-permute-start | bytes 24584 | tf_op jit(solution)/shard_map/ppermute | solution.py:198
  85.9 9.8 %collective-permute-start.13 = (bf16[32,128]{1,0:T(8,128)(2,1)}, bf16[32,128]{1,0:T(8,128)(2,1)S(1)}, u32[]{:S(2)}, u32[]{:S(2)}) collective-permute-start(bf16[32,128]{1,0:T(8,128)(2,1)} %get-tuple-element.120), channel_id=1, source_target_pairs={{0,4},{1,5},{2,6},{3,7},{4,0},{5,1},{6,2},{7,3},{8,12},{9,13},{10,... | collective-permute-start | bytes 24584 | tf_op jit(solution)/shard_map/ppermute | solution.py:198
  87.4 8.3 %collective-permute-start.14 = (bf16[32,128]{1,0:T(8,128)(2,1)}, bf16[32,128]{1,0:T(8,128)(2,1)S(1)}, u32[]{:S(2)}, u32[]{:S(2)}) collective-permute-start(bf16[32,128]{1,0:T(8,128)(2,1)} %get-tuple-element.121), channel_id=1, source_target_pairs={{0,5},{1,4},{2,7},{3,6},{4,1},{5,0},{6,3},{7,2},{8,13},{9,12},{10,... | collective-permute-start | bytes 24584 | tf_op jit(solution)/shard_map/ppermute | solution.py:198
  (6 other events, 3.7 us)

commit v2 on v1

--- a/solution.py
+++ b/solution.py
@@ -11,6 +11,7 @@
 F32 = jnp.float32
 BF16 = jnp.bfloat16
 PAD = 16
+VMEM_LIMIT = 16 * 1024 * 1024
 REPLICA_AXES = ("node", "local")
 precise = lax.Precision.HIGHEST
 
@@ -23,24 +24,18 @@
     return lax.dot_general(left, right, dims, precision=accuracy, preferred_element_type=F32)
 
 
-def whole(shape):
-    return pl.BlockSpec(shape, lambda i: (0,) * len(shape))
-
-
-def picked(shape, index):
-    return pl.BlockSpec((None,) + shape, lambda i: (index,) + (0,) * len(shape))
-
-
-def call(body, name, operands, specs, outs, scratch=()):
+def call(body, name, operands, outs, scratch=(), results=0):
+    kept = len(outs) - results
     return pl.pallas_call(
         body,
         name=name,
-        grid=(1,),
-        in_specs=specs,
-        out_specs=[whole(shape) for shape, _ in outs],
-        out_shape=[jax.ShapeDtypeStruct(shape, kind) for shape, kind in outs],
+        in_specs=[pl.BlockSpec(memory_space=pltpu.VMEM)] * len(operands),
+        out_specs=[pl.BlockSpec(memory_space=pltpu.VMEM)] * len(outs),
+        out_shape=[pltpu.VMEM(*out) for out in outs[:kept]]
+        + [jax.ShapeDtypeStruct(*out) for out in outs[kept:]],
         scratch_shapes=list(scratch),
-    )(*operands)
+        compiler_params=pltpu.CompilerParams(vmem_limit_bytes=VMEM_LIMIT),
+    )(*[pltpu.with_memory_space_constraint(operand, pltpu.VMEM) for operand in operands])
 
 
 def split(values):
@@ -104,7 +99,7 @@
 
 
 def first_body(side, x, up, wr, ws, we, cols, hid, gb, ga, dx, padded, taps, s1, s2):
-    forward(x, wr, ws, padded, cols, hid, s1, s2, side)
+    forward(x.at[0], wr, ws, padded, cols, hid, s1, s2, side)
     gb[...], ga[...], dx[...] = backward(up[...], wr, ws, we, s1, s2, padded, taps, side)
 
 
@@ -115,13 +110,13 @@
         forward(x.at[step + 1], wr, ws, padded, cols, hid, s1, s2, side)
 
 
-def chosen(arrived, loss):
+def chosen(arrived, loss, tick):
     last = lax.axis_index("section") == lax.axis_size("section") - 1
-    return jnp.where(last, loss[...], arrived[...])
-
-
-def middle_body(side, arrived, loss, wr, ws, we, s1, s2, up, gb, ga, dx, padded, taps):
-    value = chosen(arrived, loss)
+    return jnp.where(last, loss[tick - 1], arrived[...])
+
+
+def middle_body(side, tick, arrived, loss, wr, ws, we, s1, s2, up, gb, ga, dx, padded, taps):
+    value = chosen(arrived, loss, tick)
     up[...] = value
     gb[...], ga[...], dx[...] = backward(value, wr, ws, we, s1, s2, padded, taps, side)
 
@@ -160,16 +155,16 @@
         me[...] = base_e + mm(hid[...], up[...], TN)
 
 
-def last_body(side, x, arrived, loss, wr, ws, we, cols, hid, s1, s2, pt, pr, ps, pe,
+def last_body(side, tick, x, arrived, loss, wr, ws, we, cols, hid, s1, s2, pt, pr, ps, pe,
               up, gb, ga, dx, *refs):
     outs, (padded, taps, factor) = refs[:-3], refs[-3:]
-    value = chosen(arrived, loss)
+    value = chosen(arrived, loss, tick)
     up[...] = value
     gb[...], ga[...], dx[...] = backward(value, wr, ws, we, s1, s2, padded, taps, side)
     if len(outs) == 1:
-        add_factor(pt, outs[0], x, cols, hid, value, gb[...], ga[...], pr, ps, pe)
+        add_factor(pt, outs[0], x.at[tick], cols, hid, value, gb[...], ga[...], pr, ps, pe)
         return
-    add_factor(pt, factor, x, cols, hid, value, gb[...], ga[...], pr, ps, pe)
+    add_factor(pt, factor, x.at[tick], cols, hid, value, gb[...], ga[...], pr, ps, pe)
     keep, send = outs
     chips, _, width = keep.shape
     me = lax.axis_index(REPLICA_AXES)
@@ -180,8 +175,8 @@
         send[chip] = factor[:, pl.ds(sent, width)].astype(BF16)
 
 
-def finish_body(x, mr, ms, me, cols, hid, up, gb, ga, br, bs, be):
-    br[...] = (mr[...] + mm(ga[...], x[...], TN)).astype(BF16)
+def finish_body(tick, x, mr, ms, me, cols, hid, up, gb, ga, br, bs, be):
+    br[...] = (mr[...] + mm(ga[...], x[tick], TN)).astype(BF16)
     bs[...] = (ms[...] + mm(gb[...], cols[...], TN)).astype(BF16)
     be[...] = (me[...] + mm(hid[...], up[...], TN)).astype(BF16)
 
@@ -288,10 +283,6 @@
 def shifted(block):
     count = lax.axis_size("section")
     return lax.ppermute(block, "section", [(i, i - 1) for i in range(1, count)])
-
-
-def specs_of(operands):
-    return [whole(operand.shape) for operand in operands]
 
 
 def general_tail(pt, matrices, splits):
@@ -359,7 +350,6 @@
         functools.partial(first_body, side),
         "first_tick",
         (x, up) + weights,
-        [picked(image, 0)] + specs_of((up,) + weights),
         saved[:2] + grads,
         (padded, tap_space, pltpu.VMEM(inner, F32), pltpu.VMEM(inner, F32)),
     )
@@ -369,7 +359,6 @@
         functools.partial(ahead_body, side, ticks - 1),
         "forward_ahead",
         (x, wr, ws),
-        specs_of((x, wr, ws)),
         saved * (ticks - 1),
         (padded,),
     )
@@ -377,17 +366,15 @@
         start_body,
         "error_terms",
         (er, es, ee, pr, ps, pe),
-        specs_of((er, es, ee, pr, ps, pe)),
         [((rank, total), F32), ((mid, out), F32), ((mid, taps), F32)],
     )
     for tick in range(1, ticks - 1):
         cols, hid, s1, s2 = ahead[4 * tick - 4 : 4 * tick]
         operands = weights + (s1, s2)
         up, gb, ga, dx = call(
-            functools.partial(middle_body, side),
+            functools.partial(middle_body, side, tick),
             "middle_tick",
             (arrived, loss) + operands,
-            [whole(image), picked(image, tick - 1)] + specs_of(operands),
             [(image, BF16)] + grads,
             (padded, tap_space),
         )
@@ -399,7 +386,6 @@
         functools.partial(sums_body, ticks - 1),
         "running_sums",
         operands,
-        specs_of(operands),
         [((rank, total), F32), ((mid, out), F32), ((mid, taps), F32), ((mid, out), F32)],
     )
 
@@ -412,19 +398,17 @@
     parts = (chips, rank, piece)
     extra = [(parts, F32), (parts, BF16)] if fast else [((rank, total), F32)]
     up, gb, ga, leaving, *factor = call(
-        functools.partial(last_body, side),
+        functools.partial(last_body, side, ticks - 1),
         "last_tick",
         (x, arrived, loss) + operands,
-        [picked(image, ticks - 1), whole(image), picked(image, ticks - 2)] + specs_of(operands),
         [(image, BF16)] + grads + extra,
         (padded, tap_space, pltpu.VMEM((rank, total), F32)),
     )
     operands = (mr, ms, me, cols, hid, up, gb, ga)
     matrices = call(
-        finish_body,
+        functools.partial(finish_body, ticks - 1),
         "final_sums",
         (x,) + operands,
-        [picked(image, ticks - 1)] + specs_of(operands),
         [((mid, out), BF16), ((mid, taps), BF16), ((mid, out), BF16)],
     )
     if not fast:
@@ -437,7 +421,6 @@
             fold_body,
             name,
             (keep, got),
-            specs_of((keep, got)),
             [(keep.shape[1:], F32)] + [(keep.shape[1:], BF16)] * (chips - 1),
         )
         return own, [swap(value, flips(chip, False)) for chip, value in enumerate(sends, 1)]
@@ -447,7 +430,6 @@
         total_body,
         "total_factor",
         (own, *others),
-        specs_of((own, *others)),
         [((rank, piece), BF16)],
     )
     mine = [own] + [swap(own, flips(chip, False)) for chip in range(1, chips)]
@@ -458,7 +440,6 @@
         functools.partial(right_body, chips),
         "right_products",
         operands,
-        specs_of(operands),
         [((rank, total), BF16), ((chips, rank, part), F32), ((chips, rank, part), BF16)],
         (pltpu.VMEM((rank, total), F32), pltpu.VMEM((replicas, rank, part), F32)),
     )
@@ -467,7 +448,6 @@
         functools.partial(basis_body, splits),
         "basis",
         (pt,),
-        specs_of((pt,)),
         [((3, rank, rank), F32)] + [((rank, rows // replicas), F32) for rows in splits],
     )
     operands = (inverse, own, *others)
@@ -475,7 +455,6 @@
         functools.partial(end_body, splits, replicas),
         "right_factors",
         operands,
-        specs_of(operands),
         [((rank, columns // replicas), F32) for columns in (mid, mid, out)],
     )
     return tuple(value[None] for value in [leaving[None], *bases, *rights])

time: 98.7 us -> 69.3 us (0.70)
  Pallas kernels: 53.7 us -> 19.8 us
  waiting for transfers between devices: 20.4 us -> 25.1 us
    pallas_call x14, Pallas kernels: 53.7 us -> 19.8 us  [call(): pl.pallas_call(body, name=name, in_specs=[pl.BlockSpec(memory_space=pltpu...]
    ppermute x3, waiting for transfers between devices: 10.8 us -> 15.7 us  [shifted(): return lax.ppermute(block, 'section', [(i, i - 1) for i in range(1, count)])]
    unnamed x31 -> x34, local copies, waits for them, and re-layouts: 7.32 us -> 7.89 us
  transfers between devices with their start and end apart: 15 -> 15, of which waited for: 10 -> 12; matrix products, arithmetic and copies ran while one was open for 0% -> 4% of each run, Pallas kernels for 29% -> 19%
where the time goes in v2:
time: 69.3 us; the launch traced here: 69 us
  waiting for transfers between devices  25.1 us (36%)
  Pallas kernels  19.8 us (29%)
  starting transfers between devices  15.3 us (22%)
  local copies, waits for them, and re-layouts  7.89 us (11%)
  between operations  0.89 us (1%)
    pallas_call x14, Pallas kernels, call(): pl.pallas_call(body, name=name, in_specs=[pl.BlockSpec(memory_space=pltpu...  19.8 us
    ppermute x3, waiting for transfers between devices, shifted(): return lax.ppermute(block, 'section', [(i, i - 1) for i in range(1, count)])  15.7 us
    ppermute x12, starting transfers between devices, swap(): lax.ppermute(values, REPLICA_AXES, [(i, i ^ mask) for i in range(count)])  11 us
    ppermute x12, waiting for transfers between devices, swap(): lax.ppermute(values, REPLICA_AXES, [(i, i ^ mask) for i in range(count)])  9.46 us
    unnamed x34, local copies, waits for them, and re-layouts  7.89 us
    ppermute x3, starting transfers between devices, shifted(): return lax.ppermute(block, 'section', [(i, i - 1) for i in range(1, count)])  4.32 us
  transfers between devices with their start and end apart: 15, of which 12 were waited for; matrix products, arithmetic and copies ran while one was open for 4% of the time, Pallas kernels for 19%

profile of v2, /device:TPU:0, one launch (start us, length us, event | category | flops | bytes accessed | tf_op | source)
XLA Modules:
  0.0 69.0 jit_solution(14035460869056404857)
XLA Ops:
  0.7 1.4 %copy.21 = bf16[1,1,4,196,512]{4,3,2,1,0:T(8,128)(2,1)S(1)} copy(bf16[1,1,4,196,512]{4,2,3,1,0:T(4,128)(2,1)} %param.12) | data formatting | bytes 1605632 | tf_op args[0]
  4.1 1.9 %first_tick.1 = (bf16[196,2304]{1,0:T(8,128)(2,1)S(1)}, bf16[196,256]{1,0:T(8,128)(2,1)S(1)}, bf16[196,256]{1,0:T(8,128)(2,1)S(1)}, bf16[196,256]{1,0:T(8,128)(2,1)S(1)}, bf16[196,512]{1,0:T(8,128)(2,1)S(1)}) custom-call(bf16[4,196,512]{2,1,0:T(8,128)(2,1)S(1)} %bitcast.32, bf16[196,512]{1,0:T(8,128)(2,1)S(1)} %bitcast.57, bf16[512,256]{1,0:T(8,128)(2,1)S(1)} %bitcast.42, ...), custom_call_target="tpu_custom_call" | custom-call | tf_op jit(solution)/shard_map/first_tick/pallas_call | solution.py:29
  6.0 1.4 %collective-permute-start = (bf16[196,512]{1,0:T(8,128)(2,1)S(1)}, bf16[196,512]{1,0:T(8,128)(2,1)S(1)}, u32[]{:S(2)}, u32[]{:S(2)}) collective-permute-start(bf16[196,512]{1,0:T(8,128)(2,1)S(1)} %get-tuple-element.66), channel_id=1, source_target_pairs={{8,0},{16,8},{24,16},{9,1},{17,9},{25,17},{10,2},{18,10},{26,18},{... | collective-permute-start | bytes 602120 | tf_op jit(solution)/shard_map/ppermute | solution.py:285
  7.5 1.9 %forward_ahead.1 = (bf16[196,2304]{1,0:T(8,128)(2,1)S(1)}, bf16[196,256]{1,0:T(8,128)(2,1)S(1)}, f32[196,256]{1,0:T(8,128)S(1)}, f32[196,256]{1,0:T(8,128)S(1)},...) custom-call(bf16[4,196,512]{2,1,0:T(8,128)(2,1)S(1)} %bitcast.33, ...), custom_call_target="tpu_custom_call" | custom-call | tf_op jit(solution)/shard_map/forward_ahead/pallas_call | solution.py:29
  9.4 6.8 %collective-permute-done.arrived = bf16[196,512]{1,0:T(8,128)(2,1)S(1)} collective-permute-done((bf16[196,512]{1,0:T(8,128)(2,1)S(1)}, bf16[196,512]{1,0:T(8,128)(2,1)S(1)}, u32[]{:S(2)}, u32[]{:S(2)}) %collective-permute-start) | collective-permute-done | bytes 200736 | tf_op jit(solution)/shard_map/ppermute | solution.py:285
  16.2 1.1 %middle_tick.2 = (bf16[196,512]{1,0:T(8,128)(2,1)S(1)}, bf16[196,256]{1,0:T(8,128)(2,1)S(1)}, bf16[196,256]{1,0:T(8,128)(2,1)S(1)}, bf16[196,512]{1,0:T(8,128)(2,1)S(1)}) custom-call(bf16[196,512]{1,0:T(8,128)(2,1)S(1)} %collective-permute-done.arrived, bf16[3,196,512]{2,1,0:T(8,128)(2,1)S(1)} %bitcast.47, bf16[512,256]{1,0:T(8,128)(2,1)S(1)} %bitcast.44, ...), custom_call_target="tpu_custom_call" | custom-call | tf_op jit(solution)/shard_map/middle_tick/pallas_call | solution.py:29
  17.3 1.3 %collective-permute-start.1 = (bf16[196,512]{1,0:T(8,128)(2,1)S(1)}, bf16[196,512]{1,0:T(8,128)(2,1)S(1)}, u32[]{:S(2)}, u32[]{:S(2)}) collective-permute-start(bf16[196,512]{1,0:T(8,128)(2,1)S(1)} %get-tuple-element.69), channel_id=1, source_target_pairs={{8,0},{16,8},{24,16},{9,1},{17,9},{25,17},{10,2},{18,10},{26,18},{... | collective-permute-start | bytes 602120 | tf_op jit(solution)/shard_map/ppermute | solution.py:285
  18.6 6.8 %collective-permute-done.1.arrived = bf16[196,512]{1,0:T(8,128)(2,1)S(1)} collective-permute-done((bf16[196,512]{1,0:T(8,128)(2,1)S(1)}, bf16[196,512]{1,0:T(8,128)(2,1)S(1)}, u32[]{:S(2)}, u32[]{:S(2)}) %collective-permute-start.1) | collective-permute-done | bytes 200736 | tf_op jit(solution)/shard_map/ppermute | solution.py:285
  25.5 1.1 %middle_tick.3 = (bf16[196,512]{1,0:T(8,128)(2,1)S(1)}, bf16[196,256]{1,0:T(8,128)(2,1)S(1)}, bf16[196,256]{1,0:T(8,128)(2,1)S(1)}, bf16[196,512]{1,0:T(8,128)(2,1)S(1)}) custom-call(bf16[196,512]{1,0:T(8,128)(2,1)S(1)} %collective-permute-done.1.arrived, bf16[3,196,512]{2,1,0:T(8,128)(2,1)S(1)} %bitcast.48, bf16[512,256]{1,0:T(8,128)(2,1)S(1)} %bitcast.45, ...), custom_call_target="tpu_custom_call" | custom-call | tf_op jit(solution)/shard_map/middle_tick/pallas_call | solution.py:29
  26.6 1.6 %collective-permute-start.2 = (bf16[196,512]{1,0:T(8,128)(2,1)S(1)}, bf16[196,512]{1,0:T(8,128)(2,1)S(1)}, u32[]{:S(2)}, u32[]{:S(2)}) collective-permute-start(bf16[196,512]{1,0:T(8,128)(2,1)S(1)} %get-tuple-element.72), channel_id=1, source_target_pairs={{8,0},{16,8},{24,16},{9,1},{17,9},{25,17},{10,2},{18,10},{26,18},{... | collective-permute-start | bytes 602120 | tf_op jit(solution)/shard_map/ppermute | solution.py:285
  29.0 3.4 %running_sums.1 = (f32[32,3072]{1,0:T(8,128)S(1)}, f32[256,512]{1,0:T(8,128)S(1)}, f32[256,2304]{1,0:T(8,128)S(1)}, f32[256,512]{1,0:T(8,128)S(1)}) custom-call(bf16[4,196,512]{2,1,0:T(8,128)(2,1)S(1)} %bitcast.34, f32[256,512]{1,0:T(8,128)S(1)} %get-tuple-element.77.etr, f32[256,2304]{1,0:T(8,128)S(1)} %get-tuple-element.78.ets, ...), custom_call_target="tpu_custom_call" | custom-call | tf_op jit(solution)/shard_map/running_sums/pallas_call | solution.py:29
  32.4 2.0 %collective-permute-done.2.arrived = bf16[196,512]{1,0:T(8,128)(2,1)S(1)} collective-permute-done((bf16[196,512]{1,0:T(8,128)(2,1)S(1)}, bf16[196,512]{1,0:T(8,128)(2,1)S(1)}, u32[]{:S(2)}, u32[]{:S(2)}) %collective-permute-start.2) | collective-permute-done | bytes 200736 | tf_op jit(solution)/shard_map/ppermute | solution.py:285
  34.4 1.9 %last_tick.1 = (bf16[196,512]{1,0:T(8,128)(2,1)S(1)}, bf16[196,256]{1,0:T(8,128)(2,1)S(1)}, bf16[196,256]{1,0:T(8,128)(2,1)S(1)}, bf16[196,512]{1,0:T(8,128)(2,1...) custom-call(bf16[4,196,512]{2,1,0:T(8,128)(2,1)S(1)} %bitcast.35, ...), custom_call_target="tpu_custom_call" | custom-call | tf_op jit(solution)/shard_map/last_tick/pallas_call | solution.py:29
  36.4 1.3 %collective-permute-done.3.got = bf16[4,32,384]{2,1,0:T(8,128)(2,1)S(1)} collective-permute-done((bf16[4,32,384]{2,1,0:T(8,128)(2,1)S(1)}, bf16[4,32,384]{2,1,0:T(8,128)(2,1)S(1)}, u32[]{:S(2)}, u32[]{:S(2)}) %collective-permute-start.3) | collective-permute-done | bytes 98336 | tf_op jit(solution)/shard_map/ppermute | solution.py:193
  37.7 1.5 %collective-permute-start.4 = (bf16[32,384]{1,0:T(8,128)(2,1)S(1)}, bf16[32,384]{1,0:T(8,128)(2,1)S(1)}, u32[]{:S(2)}, u32[]{:S(2)}) collective-permute-start(bf16[32,384]{1,0:T(8,128)(2,1)S(1)} %get-tuple-element.99), channel_id=1, source_target_pairs={{0,1},{1,0},{2,3},{3,2},{4,5},{5,4},{6,7},{7,6},{8,9},{9,8},{10,11... | collective-permute-start | bytes 73736 | tf_op jit(solution)/shard_map/ppermute | solution.py:193
  39.2 1.5 %collective-permute-start.5 = (bf16[32,384]{1,0:T(8,128)(2,1)S(1)}, bf16[32,384]{1,0:T(8,128)(2,1)S(1)}, u32[]{:S(2)}, u32[]{:S(2)}) collective-permute-start(bf16[32,384]{1,0:T(8,128)(2,1)S(1)} %get-tuple-element.100), channel_id=1, source_target_pairs={{0,4},{1,5},{2,6},{3,7},{4,0},{5,1},{6,2},{7,3},{8,12},{9,13},{10,... | collective-permute-start | bytes 73736 | tf_op jit(solution)/shard_map/ppermute | solution.py:193
  41.6 1.6 %collective-permute-done.5.refs_1_ = bf16[32,384]{1,0:T(8,128)(2,1)S(1)} collective-permute-done((bf16[32,384]{1,0:T(8,128)(2,1)S(1)}, bf16[32,384]{1,0:T(8,128)(2,1)S(1)}, u32[]{:S(2)}, u32[]{:S(2)}) %collective-permute-start.5) | collective-permute-done | bytes 24608 | tf_op jit(solution)/shard_map/ppermute | solution.py:193
  43.2 2.2 %collective-permute-done.6.refs_2_ = bf16[32,384]{1,0:T(8,128)(2,1)S(1)} collective-permute-done((bf16[32,384]{1,0:T(8,128)(2,1)S(1)}, bf16[32,384]{1,0:T(8,128)(2,1)S(1)}, u32[]{:S(2)}, u32[]{:S(2)}) %collective-permute-start.6) | collective-permute-done | bytes 24608 | tf_op jit(solution)/shard_map/ppermute | solution.py:193
  46.7 2.3 %collective-permute-start.9 = (bf16[32,384]{1,0:T(8,128)(2,1)S(1)}, bf16[32,384]{1,0:T(8,128)(2,1)S(1)}, u32[]{:S(2)}, u32[]{:S(2)}) collective-permute-start(bf16[32,384]{1,0:T(8,128)(2,1)S(1)} %total_factor.1.refs_0_), channel_id=1, source_target_pairs={{0,5},{1,4},{2,7},{3,6},{4,1},{5,0},{6,3},{7,2},{8,13},{9,12},{10,... | collective-permute-start | bytes 73736 | tf_op jit(solution)/shard_map/ppermute | solution.py:193
  49.8 1.6 %collective-permute-done.9.refs_3_ = bf16[32,384]{1,0:T(8,128)(2,1)S(1)} collective-permute-done((bf16[32,384]{1,0:T(8,128)(2,1)S(1)}, bf16[32,384]{1,0:T(8,128)(2,1)S(1)}, u32[]{:S(2)}, u32[]{:S(2)}) %collective-permute-start.9) | collective-permute-done | bytes 24608 | tf_op jit(solution)/shard_map/ppermute | solution.py:193
  53.7 1.1 %collective-permute-done.11.got = bf16[4,32,128]{2,1,0:T(8,128)(2,1)S(1)} collective-permute-done((bf16[4,32,128]{2,1,0:T(8,128)(2,1)S(1)}, bf16[4,32,128]{2,1,0:T(8,128)(2,1)S(1)}, u32[]{:S(2)}, u32[]{:S(2)}) %collective-permute-start.11) | collective-permute-done | bytes 32800 | tf_op jit(solution)/shard_map/ppermute | solution.py:193
  54.7 1.5 %collective-permute-start.12 = (bf16[32,128]{1,0:T(8,128)(2,1)S(1)}, bf16[32,128]{1,0:T(8,128)(2,1)S(1)}, u32[]{:S(2)}, u32[]{:S(2)}) collective-permute-start(bf16[32,128]{1,0:T(8,128)(2,1)S(1)} %get-tuple-element.119), channel_id=1, source_target_pairs={{0,1},{1,0},{2,3},{3,2},{4,5},{5,4},{6,7},{7,6},{8,9},{9,8},{10,11... | collective-permute-start | bytes 24584 | tf_op jit(solution)/shard_map/ppermute | solution.py:193
  56.2 1.5 %collective-permute-start.13 = (bf16[32,128]{1,0:T(8,128)(2,1)S(1)}, bf16[32,128]{1,0:T(8,128)(2,1)S(1)}, u32[]{:S(2)}, u32[]{:S(2)}) collective-permute-start(bf16[32,128]{1,0:T(8,128)(2,1)S(1)} %get-tuple-element.120), channel_id=1, source_target_pairs={{0,4},{1,5},{2,6},{3,7},{4,0},{5,1},{6,2},{7,3},{8,12},{9,13},{10,... | collective-permute-start | bytes 24584 | tf_op jit(solution)/shard_map/ppermute | solution.py:193
  59.0 6.1 %basis.1 = (f32[3,32,32]{2,1,0:T(8,128)S(1)}, f32[32,64]{1,0:T(8,128)S(1)}, f32[32,288]{1,0:T(8,128)S(1)}, f32[32,32]{1,0:T(8,128)S(1)}) custom-call(bf16[32,3072]{1,0:T(8,128)(2,1)S(1)} %get-tuple-element.111.pt), custom_call_target="tpu_custom_call" | custom-call | tf_op jit(solution)/shard_map/basis/pallas_call | solution.py:29
  (55 shorter events, 13.4 us)
Async XLA Ops:
  6.0 10.2 %copy-start.2 = (bf16[1,3,196,512]{3,2,1,0:T(8,128)(2,1)S(1)}, bf16[1,3,196,512]{3,2,1,0:T(8,128)(2,1)}, u32[]{:S(2)}) copy-start(bf16[1,3,196,512]{3,2,1,0:T(8,128)(2,1)} %param.14) | copy-start | bytes 1806340
  6.0 10.2 %collective-permute-start = (bf16[196,512]{1,0:T(8,128)(2,1)S(1)}, bf16[196,512]{1,0:T(8,128)(2,1)S(1)}, u32[]{:S(2)}, u32[]{:S(2)}) collective-permute-start(bf16[196,512]{1,0:T(8,128)(2,1)S(1)} %get-tuple-element.66), channel_id=1, source_target_pairs={{8,0},{16,8},{24,16},{9,1},{17,9},{25,17},{10,2},{18,10},{26,18},{... | collective-permute-start | bytes 602120 | tf_op jit(solution)/shard_map/ppermute | solution.py:285
  17.3 8.1 %collective-permute-start.1 = (bf16[196,512]{1,0:T(8,128)(2,1)S(1)}, bf16[196,512]{1,0:T(8,128)(2,1)S(1)}, u32[]{:S(2)}, u32[]{:S(2)}) collective-permute-start(bf16[196,512]{1,0:T(8,128)(2,1)S(1)} %get-tuple-element.69), channel_id=1, source_target_pairs={{8,0},{16,8},{24,16},{9,1},{17,9},{25,17},{10,2},{18,10},{26,18},{... | collective-permute-start | bytes 602120 | tf_op jit(solution)/shard_map/ppermute | solution.py:285
  25.5 2.8 %copy-start.5 = (bf16[1,1,2304,256]{3,2,1,0:T(8,128)(2,1)S(1)}, bf16[1,1,2304,256]{3,2,1,0:T(8,128)(2,1)}, u32[]{:S(2)}) copy-start(bf16[1,1,2304,256]{3,2,1,0:T(8,128)(2,1)} %param.19) | copy-start | bytes 3538948
  25.5 2.8 %copy-start.6 = (bf16[1,1,256,512]{3,2,1,0:T(8,128)(2,1)S(1)}, bf16[1,1,256,512]{3,2,1,0:T(8,128)(2,1)}, u32[]{:S(2)}) copy-start(bf16[1,1,256,512]{3,2,1,0:T(8,128)(2,1)} %param.20) | copy-start | bytes 786436
  25.5 2.8 %copy-start.9 = (f32[1,32,512]{2,1,0:T(8,128)S(1)}, f32[1,32,512]{2,1,0:T(8,128)}, u32[]{:S(2)}) copy-start(f32[1,32,512]{2,1,0:T(8,128)} %param.23) | copy-start | bytes 196612
  25.5 2.8 %copy-start.10 = (f32[1,32,256]{2,1,0:T(8,128)S(1)}, f32[1,32,256]{2,1,0:T(8,128)}, u32[]{:S(2)}) copy-start(f32[1,32,256]{2,1,0:T(8,128)} %param.21) | copy-start | bytes 98308
  25.5 2.8 %copy-start.11 = (f32[1,32,256]{2,1,0:T(8,128)S(1)}, f32[1,32,256]{2,1,0:T(8,128)}, u32[]{:S(2)}) copy-start(f32[1,32,256]{2,1,0:T(8,128)} %param.22) | copy-start | bytes 98308
  25.5 2.8 %copy-start.12 = (bf16[1,1,512,256]{3,2,1,0:T(8,128)(2,1)S(1)}, bf16[1,1,512,256]{3,2,1,0:T(8,128)(2,1)}, u32[]{:S(2)}) copy-start(bf16[1,1,512,256]{3,2,1,0:T(8,128)(2,1)} %param.18) | copy-start | bytes 786436
  26.6 2.4 %copy-start.8 = (bf16[1,1,196,512]{3,2,1,0:T(8,128)(2,1)S(1)}, bf16[1,1,196,512]{3,2,1,0:T(8,128)(2,1)}, u32[]{:S(2)}) copy-start(bf16[1,1,196,512]{3,2,1,0:T(8,128)(2,1)} %param.13) | copy-start | bytes 602116
  26.6 7.8 %collective-permute-start.2 = (bf16[196,512]{1,0:T(8,128)(2,1)S(1)}, bf16[196,512]{1,0:T(8,128)(2,1)S(1)}, u32[]{:S(2)}, u32[]{:S(2)}) collective-permute-start(bf16[196,512]{1,0:T(8,128)(2,1)S(1)} %get-tuple-element.72), channel_id=1, source_target_pairs={{8,0},{16,8},{24,16},{9,1},{17,9},{25,17},{10,2},{18,10},{26,18},{... | collective-permute-start | bytes 602120 | tf_op jit(solution)/shard_map/ppermute | solution.py:285
  29.0 5.4 %copy-start.4 = (bf16[1,256,512]{2,1,0:T(8,128)(2,1)S(1)}, bf16[1,256,512]{2,1,0:T(8,128)(2,1)}, u32[]{:S(2)}) copy-start(bf16[1,256,512]{2,1,0:T(8,128)(2,1)} %param.17) | copy-start | bytes 786436
  36.3 1.4 %collective-permute-start.3 = (bf16[4,32,384]{2,1,0:T(8,128)(2,1)S(1)}, bf16[4,32,384]{2,1,0:T(8,128)(2,1)S(1)}, u32[]{:S(2)}, u32[]{:S(2)}) collective-permute-start(bf16[4,32,384]{2,1,0:T(8,128)(2,1)S(1)} %get-tuple-element.97), channel_id=1, source_target_pairs={{0,2},{1,3},{2,0},{3,1},{4,6},{5,7},{6,4},{7,5},{8,10},{9,11},{10,... | collective-permute-start | bytes 294920 | tf_op jit(solution)/shard_map/ppermute | solution.py:193
  37.7 3.9 %collective-permute-start.4 = (bf16[32,384]{1,0:T(8,128)(2,1)S(1)}, bf16[32,384]{1,0:T(8,128)(2,1)S(1)}, u32[]{:S(2)}, u32[]{:S(2)}) collective-permute-start(bf16[32,384]{1,0:T(8,128)(2,1)S(1)} %get-tuple-element.99), channel_id=1, source_target_pairs={{0,1},{1,0},{2,3},{3,2},{4,5},{5,4},{6,7},{7,6},{8,9},{9,8},{10,11... | collective-permute-start | bytes 73736 | tf_op jit(solution)/shard_map/ppermute | solution.py:193
  39.2 4.0 %collective-permute-start.5 = (bf16[32,384]{1,0:T(8,128)(2,1)S(1)}, bf16[32,384]{1,0:T(8,128)(2,1)S(1)}, u32[]{:S(2)}, u32[]{:S(2)}) collective-permute-start(bf16[32,384]{1,0:T(8,128)(2,1)S(1)} %get-tuple-element.100), channel_id=1, source_target_pairs={{0,4},{1,5},{2,6},{3,7},{4,0},{5,1},{6,2},{7,3},{8,12},{9,13},{10,... | collective-permute-start | bytes 73736 | tf_op jit(solution)/shard_map/ppermute | solution.py:193
  40.7 4.7 %collective-permute-start.6 = (bf16[32,384]{1,0:T(8,128)(2,1)S(1)}, bf16[32,384]{1,0:T(8,128)(2,1)S(1)}, u32[]{:S(2)}, u32[]{:S(2)}) collective-permute-start(bf16[32,384]{1,0:T(8,128)(2,1)S(1)} %get-tuple-element.101), channel_id=1, source_target_pairs={{0,5},{1,4},{2,7},{3,6},{4,1},{5,0},{6,3},{7,2},{8,13},{9,12},{10,... | collective-permute-start | bytes 73736 | tf_op jit(solution)/shard_map/ppermute | solution.py:193
  45.4 3.9 %collective-permute-start.7 = (bf16[32,384]{1,0:T(8,128)(2,1)S(1)}, bf16[32,384]{1,0:T(8,128)(2,1)S(1)}, u32[]{:S(2)}, u32[]{:S(2)}) collective-permute-start(bf16[32,384]{1,0:T(8,128)(2,1)S(1)} %total_factor.1.refs_0_), channel_id=1, source_target_pairs={{0,1},{1,0},{2,3},{3,2},{4,5},{5,4},{6,7},{7,6},{8,9},{9,8},{10,11... | collective-permute-start | bytes 73736 | tf_op jit(solution)/shard_map/ppermute | solution.py:193
  46.0 3.8 %collective-permute-start.8 = (bf16[32,384]{1,0:T(8,128)(2,1)S(1)}, bf16[32,384]{1,0:T(8,128)(2,1)S(1)}, u32[]{:S(2)}, u32[]{:S(2)}) collective-permute-start(bf16[32,384]{1,0:T(8,128)(2,1)S(1)} %total_factor.1.refs_0_), channel_id=1, source_target_pairs={{0,4},{1,5},{2,6},{3,7},{4,0},{5,1},{6,2},{7,3},{8,12},{9,13},{10,... | collective-permute-start | bytes 73736 | tf_op jit(solution)/shard_map/ppermute | solution.py:193
  46.7 4.7 %collective-permute-start.9 = (bf16[32,384]{1,0:T(8,128)(2,1)S(1)}, bf16[32,384]{1,0:T(8,128)(2,1)S(1)}, u32[]{:S(2)}, u32[]{:S(2)}) collective-permute-start(bf16[32,384]{1,0:T(8,128)(2,1)S(1)} %total_factor.1.refs_0_), channel_id=1, source_target_pairs={{0,5},{1,4},{2,7},{3,6},{4,1},{5,0},{6,3},{7,2},{8,13},{9,12},{10,... | collective-permute-start | bytes 73736 | tf_op jit(solution)/shard_map/ppermute | solution.py:193
  51.4 1.4 %collective-permute-start.10 = (bf16[4,32,384]{2,1,0:T(8,128)(2,1)S(1)}, bf16[4,32,384]{2,1,0:T(8,128)(2,1)S(1)}, u32[]{:S(2)}, u32[]{:S(2)}) collective-permute-start(bf16[4,32,384]{2,1,0:T(8,128)(2,1)S(1)} %pad_maximum_fusion), channel_id=1, source_target_pairs={{0,2},{1,3},{2,0},{3,1},{4,6},{5,7},{6,4},{7,5},{8,10},{9,11},{10,... | collective-permute-start | bytes 294920 | tf_op jit(solution)/shard_map/ppermute | solution.py:193
  53.5 1.3 %collective-permute-start.11 = (bf16[4,32,128]{2,1,0:T(8,128)(2,1)S(1)}, bf16[4,32,128]{2,1,0:T(8,128)(2,1)S(1)}, u32[]{:S(2)}, u32[]{:S(2)}) collective-permute-start(bf16[4,32,128]{2,1,0:T(8,128)(2,1)S(1)} %get-tuple-element.117), channel_id=1, source_target_pairs={{0,2},{1,3},{2,0},{3,1},{4,6},{5,7},{6,4},{7,5},{8,10},{9,11},{10,... | collective-permute-start | bytes 98312 | tf_op jit(solution)/shard_map/ppermute | solution.py:193
  54.7 12.2 %collective-permute-start.12 = (bf16[32,128]{1,0:T(8,128)(2,1)S(1)}, bf16[32,128]{1,0:T(8,128)(2,1)S(1)}, u32[]{:S(2)}, u32[]{:S(2)}) collective-permute-start(bf16[32,128]{1,0:T(8,128)(2,1)S(1)} %get-tuple-element.119), channel_id=1, source_target_pairs={{0,1},{1,0},{2,3},{3,2},{4,5},{5,4},{6,7},{7,6},{8,9},{9,8},{10,11... | collective-permute-start | bytes 24584 | tf_op jit(solution)/shard_map/ppermute | solution.py:193
  56.2 10.8 %collective-permute-start.13 = (bf16[32,128]{1,0:T(8,128)(2,1)S(1)}, bf16[32,128]{1,0:T(8,128)(2,1)S(1)}, u32[]{:S(2)}, u32[]{:S(2)}) collective-permute-start(bf16[32,128]{1,0:T(8,128)(2,1)S(1)} %get-tuple-element.120), channel_id=1, source_target_pairs={{0,4},{1,5},{2,6},{3,7},{4,0},{5,1},{6,2},{7,3},{8,12},{9,13},{10,... | collective-permute-start | bytes 24584 | tf_op jit(solution)/shard_map/ppermute | solution.py:193
  57.7 9.3 %collective-permute-start.14 = (bf16[32,128]{1,0:T(8,128)(2,1)S(1)}, bf16[32,128]{1,0:T(8,128)(2,1)S(1)}, u32[]{:S(2)}, u32[]{:S(2)}) collective-permute-start(bf16[32,128]{1,0:T(8,128)(2,1)S(1)} %get-tuple-element.121), channel_id=1, source_target_pairs={{0,5},{1,4},{2,7},{3,6},{4,1},{5,0},{6,3},{7,2},{8,13},{9,12},{10,... | collective-permute-start | bytes 24584 | tf_op jit(solution)/shard_map/ppermute | solution.py:193
  (4 other events, 4.9 us)

commit v3 on v2

--- a/solution.py
+++ b/solution.py
@@ -8,6 +8,7 @@
 from jax.experimental.pallas import tpu as pltpu
 from jax.sharding import PartitionSpec as P
 
+
 F32 = jnp.float32
 BF16 = jnp.bfloat16
 PAD = 16
@@ -24,18 +25,22 @@
     return lax.dot_general(left, right, dims, precision=accuracy, preferred_element_type=F32)
 
 
-def call(body, name, operands, outs, scratch=(), results=0):
+def call(body, operands, outs, scratch=(), given=0, results=0):
     kept = len(outs) - results
+    vmem, hbm = pl.BlockSpec(memory_space=pltpu.VMEM), pl.BlockSpec(memory_space=pltpu.HBM)
+    place = pltpu.with_memory_space_constraint
+    operands = [place(value, pltpu.HBM) for value in operands[:given]] + [
+        place(value, pltpu.VMEM) for value in operands[given:]
+    ]
     return pl.pallas_call(
         body,
-        name=name,
-        in_specs=[pl.BlockSpec(memory_space=pltpu.VMEM)] * len(operands),
-        out_specs=[pl.BlockSpec(memory_space=pltpu.VMEM)] * len(outs),
+        in_specs=[hbm] * given + [vmem] * (len(operands) - given),
+        out_specs=[vmem] * kept + [hbm] * results,
         out_shape=[pltpu.VMEM(*out) for out in outs[:kept]]
-        + [jax.ShapeDtypeStruct(*out) for out in outs[kept:]],
+        + [pltpu.HBM(*out) for out in outs[kept:]],
         scratch_shapes=list(scratch),
         compiler_params=pltpu.CompilerParams(vmem_limit_bytes=VMEM_LIMIT),
-    )(*[pltpu.with_memory_space_constraint(operand, pltpu.VMEM) for operand in operands])
+    )(*operands)
 
 
 def split(values):
@@ -98,8 +103,19 @@
     return grad_two, grad_one, leaving
 
 
-def first_body(side, x, up, wr, ws, we, cols, hid, gb, ga, dx, padded, taps, s1, s2):
+def first_body(side, x_in, wr_in, ws_in, we_in, up_in, x, wr, ws, we, up, cols, hid, gb, ga, dx,
+               raw, padded, taps, s1, s2, sems):
+    pairs = ((x_in, raw), (wr_in, wr), (ws_in, ws), (we_in, we), (up_in, up))
+    copies = [pltpu.make_async_copy(a, b, sems.at[i]) for i, (a, b) in enumerate(pairs)]
+    for copy in copies:
+        copy.start()
+    copies[0].wait()
+    x[...] = jnp.swapaxes(raw[...], 0, 1)
+    copies[1].wait()
+    copies[2].wait()
     forward(x.at[0], wr, ws, padded, cols, hid, s1, s2, side)
+    copies[3].wait()
+    copies[4].wait()
     gb[...], ga[...], dx[...] = backward(up[...], wr, ws, we, s1, s2, padded, taps, side)
 
 
@@ -156,29 +172,63 @@
 
 
 def last_body(side, tick, x, arrived, loss, wr, ws, we, cols, hid, s1, s2, pt, pr, ps, pe,
-              up, gb, ga, dx, *refs):
+              up, gb, ga, *refs):
     outs, (padded, taps, factor) = refs[:-3], refs[-3:]
+    dx = outs[0]
     value = chosen(arrived, loss, tick)
     up[...] = value
     gb[...], ga[...], dx[...] = backward(value, wr, ws, we, s1, s2, padded, taps, side)
-    if len(outs) == 1:
-        add_factor(pt, outs[0], x.at[tick], cols, hid, value, gb[...], ga[...], pr, ps, pe)
-        return
-    add_factor(pt, factor, x.at[tick], cols, hid, value, gb[...], ga[...], pr, ps, pe)
-    keep, send = outs
-    chips, _, width = keep.shape
-    me = lax.axis_index(REPLICA_AXES)
-    for chip in range(chips):
-        kept = pl.multiple_of((me ^ flips(chip, False)) * width, width)
-        keep[chip] = factor[:, pl.ds(kept, width)]
-        sent = pl.multiple_of((me ^ flips(chip, True)) * width, width)
-        send[chip] = factor[:, pl.ds(sent, width)].astype(BF16)
+    factors = (x.at[tick], cols, hid, value, gb[...], ga[...], pr, ps, pe)
+    if len(outs) == 2:
+        add_factor(pt, outs[1], *factors)
+    else:
+        add_factor(pt, factor, *factors)
+        keep, send = outs[1:]
+        half = keep.shape[1]
+        core = core_index()
+        keep[...] = factor[:, pl.ds(pl.multiple_of(core * half, 128), half)]
+        sent = factor[:, pl.ds(pl.multiple_of((1 - core) * half, 128), half)]
+        send[...] = sent.astype(BF16)
 
 
 def finish_body(tick, x, mr, ms, me, cols, hid, up, gb, ga, br, bs, be):
     br[...] = (mr[...] + mm(ga[...], x[tick], TN)).astype(BF16)
     bs[...] = (ms[...] + mm(gb[...], cols[...], TN)).astype(BF16)
     be[...] = (me[...] + mm(hid[...], up[...], TN)).astype(BF16)
+
+
+def packed_body(tick, dx, x, mr, ms, me, cols, hid, up, gb, ga, keep, send, leaving,
+                tr, ts, te, sem):
+    copy = pltpu.make_async_copy(dx, leaving, sem)
+    copy.start()
+    tr[...] = mr[...] + mm(ga[...], x[tick], TN)
+    ts[...] = ms[...] + mm(gb[...], cols[...], TN)
+    te[...] = me[...] + mm(hid[...], up[...], TN)
+    core = core_index()
+    mid, out = tr.shape
+    taps = ts.shape[1]
+    high, wide = mid // 4, out // 4
+    for block in range(2):
+        rows = slice(block * high, (block + 1) * high)
+        for target, at in ((keep, 2 * block + core), (send, 2 * block + 1 - core)):
+            source = pl.ds(pl.multiple_of(at * high, 8), high)
+            target[rows, 0:out] = tr[source, :].astype(target.dtype)
+            target[rows, out : out + taps] = ts[source, :].astype(target.dtype)
+            lanes = pl.ds(pl.multiple_of(at * wide, 128), wide)
+            part = te[:, lanes].astype(target.dtype)
+            start = out + taps + block * wide
+            target[:, start : start + wide] = part[: mid // 2]
+            start += 2 * wide
+            target[:, start : start + wide] = part[mid // 2 :]
+    copy.wait()
+
+
+def chip_body(keep, got, both):
+    both[...] = (keep[...] + got[...].astype(F32)).astype(BF16)
+
+
+def core_index():
+    return lax.rem(lax.axis_index("node"), 2)
 
 
 def flips(chip, other_core):
@@ -193,91 +243,111 @@
     return lax.ppermute(values, REPLICA_AXES, [(i, i ^ mask) for i in range(count)])
 
 
-def fold_body(keep, got, own, *sends):
-    own[...] = keep[0] + got[0].astype(F32)
-    for chip, send in enumerate(sends, 1):
-        send[...] = (keep[chip] + got[chip].astype(F32)).astype(BF16)
-
-
-def total_body(own, *refs):
-    total = own[...]
-    for ref in refs[:-1]:
-        total = total + ref[...].astype(F32)
-    refs[-1][...] = total.astype(BF16)
-
-
-def right_body(chips, *refs):
-    mine = refs[:chips]
-    other, br, bs, be, pt, keep, send, flat, pieces = refs[chips:]
-    me = lax.axis_index(REPLICA_AXES)
-    width = flat.shape[1] // (2 * chips)
-    for chip in range(chips):
-        at = pl.multiple_of((me ^ flips(chip, False)) * width, width)
-        flat[:, pl.ds(at, width)] = mine[chip][...].astype(F32)
-        at = pl.multiple_of((me ^ flips(chip, True)) * width, width)
-        flat[:, pl.ds(at, width)] = other[chip].astype(F32)
-    full = flat[...].astype(BF16)
-    pt[...] = full
-    rows, spatial = br.shape[1], bs.shape[1]
+def total_body(own, flipped_local, flipped_node, flipped_both, total):
+    near = own[...].astype(F32) + flipped_local[...].astype(F32)
+    far = flipped_node[...].astype(F32) + flipped_both[...].astype(F32)
+    total[...] = (near + far).astype(BF16)
+
+
+def right_body(splits, mine, other, both, pt, keep, *refs):
+    sends, pieces = refs[:-1], refs[-1]
+    half = mine.shape[1]
+    core = core_index()
+    pt[:, pl.ds(pl.multiple_of(core * half, 128), half)] = mine[...]
+    pt[:, pl.ds(pl.multiple_of((1 - core) * half, 128), half)] = other[...]
+    out, taps, _ = splits
+    wide = both.shape[1]
+    expand = jnp.concatenate([both[:, wide - out : wide - out // 2], both[:, wide - out // 2 :]], 0)
     parts = (
-        mm(full[:, :rows], br[...], NT),
-        mm(full[:, rows : rows + spatial], bs[...], NT),
-        mm(full[:, rows + spatial :], be[...]),
-    )
-    count = 2 * chips
+        mm(pt[:, :out], both[:, :out], NT),
+        mm(pt[:, out : out + taps], both[:, out : out + taps], NT),
+        mm(pt[:, out + taps :], expand),
+    )
+    count = len(sends) + 1
     for piece in range(count):
         cut = []
         for part in parts:
-            wide = part.shape[1] // count
-            cut.append(part[:, piece * wide : (piece + 1) * wide])
+            size = part.shape[1] // count
+            cut.append(part[:, piece * size : (piece + 1) * size])
         pieces[piece] = jnp.concatenate(cut, axis=1)
-    for chip in range(chips):
-        keep[chip] = pieces[me ^ flips(chip, False)]
-        send[chip] = pieces[me ^ flips(chip, True)].astype(BF16)
-
-
-def inverse_factor(gram):
-    rank = gram.shape[0]
-    row = lax.broadcasted_iota(jnp.int32, (rank, 2 * rank), 0)
-    lane = lax.broadcasted_iota(jnp.int32, (rank, 2 * rank), 1)
-    table = jnp.concatenate([gram, jnp.zeros_like(gram)], axis=1)
-    table = jnp.where(lane == row + rank, 1.0, table)
-    scale = jnp.zeros((rank, 1), F32)
+    local_size = lax.axis_size("local")
+    me = lax.axis_index("node") // 2 * local_size + lax.axis_index("local")
+    keep[...] = pieces[me]
+    for chip, send in enumerate(sends, 1):
+        send[...] = pieces[me ^ chip].astype(BF16)
+
+
+def inverse_factors(grams):
+    rank = grams[0].shape[0]
+    high = 8
+    row = lax.broadcasted_iota(jnp.int32, (high, 1), 0)
+    lane = lax.broadcasted_iota(jnp.int32, (high, 2 * rank), 1)
+    tables, pivots = [], []
+    for gram in grams:
+        wide = jnp.concatenate([gram, gram], axis=1)
+        blocks = []
+        for start in range(0, rank, high):
+            unit = jnp.where(lane == row + (start + rank), 1.0, 0.0)
+            blocks.append(jnp.where(lane < rank, wide[start : start + high], unit))
+        tables.append(blocks)
+        pivots.append([jnp.ones((high, 1), F32) for _ in blocks])
     for step in range(rank):
-        column = table[:, step : step + 1]
-        pivot = table[step : step + 1, step : step + 1]
-        ratio = column / pivot
-        scale = jnp.where(row[:, :1] == step, lax.rsqrt(pivot), scale)
-        table = jnp.where(row > step, table - ratio * table[step : step + 1, :], table)
-    return table[:, rank:] * scale
-
-
-def basis_body(splits, pt, inverse, *outs):
+        first, at = step // high, step % high
+        for blocks, kept in zip(tables, pivots):
+            pivot = blocks[first][at : at + 1, step : step + 1]
+            line = blocks[first][at : at + 1, :] * (1.0 / pivot)
+            kept[first] = jnp.where(row == at, pivot, kept[first])
+            for index in range(first, len(blocks)):
+                column = blocks[index][:, step : step + 1]
+                if index == first:
+                    column = jnp.where(row > at, column, 0.0)
+                blocks[index] = blocks[index] - column * line
+    return [
+        jnp.concatenate([block[:, rank:] * lax.rsqrt(p) for block, p in zip(blocks, kept)], 0)
+        for blocks, kept in zip(tables, pivots)
+    ]
+
+
+def basis_body(splits, pt, inverse, *refs):
+    count = len(splits)
+    outs, scratch, sems = refs[:count], refs[count : 2 * count], refs[2 * count]
     me = lax.axis_index(REPLICA_AXES)
-    count = lax.axis_size(REPLICA_AXES)
-    start = 0
-    for member, rows in enumerate(splits):
-        full = pt[:, start : start + rows]
-        linv = inverse_factor(mm(full, full, NT))
-        inverse[member] = linv
-        wide = rows // count
+    replicas = lax.axis_size(REPLICA_AXES)
+    starts = [sum(splits[:member]) for member in range(count)]
+    fulls = [pt[:, start : start + rows] for start, rows in zip(starts, splits)]
+    linvs = inverse_factors([mm(full, full, NT) for full in fulls])
+    copies = []
+    for member, (start, rows) in enumerate(zip(starts, splits)):
+        inverse[member] = linvs[member]
+        wide = rows // replicas
         window = min(-(-wide // 128) * 128 + (128 if 128 % wide and wide % 128 else 0), rows)
         first = me * wide
         aligned = pl.multiple_of(first // 128 * 128, 128)
         block = pt[:, pl.ds(start + aligned, window)].astype(F32)
         moved = pltpu.roll(block, lax.rem(window - (first - aligned), window), 1)
-        outs[member][...] = math.sqrt(rows) * mm(linv, moved[:, :wide], NN, precise)
-        start += rows
-
-
-def end_body(splits, replicas, inverse, own, a, b, c, *outs):
+        scratch[member][...] = math.sqrt(rows) * mm(linvs[member], moved[:, :wide], NN, precise)
+        copies.append(pltpu.make_async_copy(scratch[member], outs[member], sems.at[member]))
+        copies[-1].start()
+    for copy in copies:
+        copy.wait()
+
+
+def end_body(splits, replicas, inverse, own, a, b, c, *refs):
+    count = len(splits)
+    outs, scratch, sems = refs[:count], refs[count : 2 * count], refs[2 * count]
     total = own[...] + a[...].astype(F32) + b[...].astype(F32) + c[...].astype(F32)
     start = 0
-    for member, out in enumerate(outs):
-        wide = out.shape[1]
+    copies = []
+    for member in range(count):
+        wide = scratch[member].shape[1]
         scale = 1.0 / (replicas * math.sqrt(splits[member]))
-        out[...] = scale * mm(inverse[member], total[:, start : start + wide], NN, precise)
+        part = total[:, start : start + wide]
+        scratch[member][...] = scale * mm(inverse[member], part, NN, precise)
         start += wide
+        copies.append(pltpu.make_async_copy(scratch[member], outs[member], sems.at[member]))
+        copies[-1].start()
+    for copy in copies:
+        copy.wait()
 
 
 def shifted(block):
@@ -344,27 +414,29 @@
     saved = [(wide, BF16), (inner, BF16), (inner, F32), (inner, F32)]
     grads = [(inner, BF16), (inner, BF16), (image, BF16)]
 
+    matrices = [(wr.shape, BF16), (ws.shape, BF16), (we.shape, BF16)]
+    x, wr, ws, we, up, cols, hid, gb, ga, dx = call(
+        functools.partial(first_body, side),
+        (jnp.swapaxes(x, 0, 1), wr, ws, we, grad_in[0, 0]),
+        [(x.shape, BF16)] + matrices + [(image, BF16)] + saved[:2] + grads,
+        (
+            pltpu.VMEM((pixels, ticks, out), BF16),
+            padded,
+            tap_space,
+            pltpu.VMEM(inner, F32),
+            pltpu.VMEM(inner, F32),
+            pltpu.SemaphoreType.DMA((5,)),
+        ),
+        given=5,
+    )
     weights = (wr, ws, we)
-    up = grad_in[0, 0]
-    cols, hid, gb, ga, dx = call(
-        functools.partial(first_body, side),
-        "first_tick",
-        (x, up) + weights,
-        saved[:2] + grads,
-        (padded, tap_space, pltpu.VMEM(inner, F32), pltpu.VMEM(inner, F32)),
-    )
     done = [(cols, hid, up, gb, ga)]
     arrived = shifted(dx)
     ahead = call(
-        functools.partial(ahead_body, side, ticks - 1),
-        "forward_ahead",
-        (x, wr, ws),
-        saved * (ticks - 1),
-        (padded,),
+        functools.partial(ahead_body, side, ticks - 1), (x, wr, ws), saved * (ticks - 1), (padded,)
     )
     pt, etr, ets = call(
         start_body,
-        "error_terms",
         (er, es, ee, pr, ps, pe),
         [((rank, total), F32), ((mid, out), F32), ((mid, taps), F32)],
     )
@@ -373,7 +445,6 @@
         operands = weights + (s1, s2)
         up, gb, ga, dx = call(
             functools.partial(middle_body, side, tick),
-            "middle_tick",
             (arrived, loss) + operands,
             [(image, BF16)] + grads,
             (padded, tap_space),
@@ -384,78 +455,71 @@
     operands = (x, etr, ets, ee, pt, pr, ps, pe) + flat
     pt, mr, ms, me = call(
         functools.partial(sums_body, ticks - 1),
-        "running_sums",
         operands,
         [((rank, total), F32), ((mid, out), F32), ((mid, taps), F32), ((mid, out), F32)],
     )
 
     replicas = lax.axis_size(REPLICA_AXES)
-    piece = total // replicas
-    fast = replicas == 8 and lax.axis_size("node") == 4 and piece % 128 == 0
+    fast = lax.axis_size("node") == 4 and lax.axis_size("local") == 2 and total % 256 == 0
     chips = replicas // 2
+    half = total // 2
     cols, hid, s1, s2 = ahead[4 * ticks - 8 : 4 * ticks - 4]
-    operands = weights + (cols, hid, s1, s2, pt, pr, ps, pe)
-    parts = (chips, rank, piece)
-    extra = [(parts, F32), (parts, BF16)] if fast else [((rank, total), F32)]
+    extra = [((rank, half), F32), ((rank, half), BF16)] if fast else [((rank, total), F32)]
     up, gb, ga, leaving, *factor = call(
         functools.partial(last_body, side, ticks - 1),
-        "last_tick",
-        (x, arrived, loss) + operands,
+        (x, arrived, loss) + weights + (cols, hid, s1, s2, pt, pr, ps, pe),
         [(image, BF16)] + grads + extra,
         (padded, tap_space, pltpu.VMEM((rank, total), F32)),
     )
-    operands = (mr, ms, me, cols, hid, up, gb, ga)
-    matrices = call(
-        functools.partial(finish_body, ticks - 1),
-        "final_sums",
-        (x,) + operands,
-        [((mid, out), BF16), ((mid, taps), BF16), ((mid, out), BF16)],
-    )
+    sums = (x, mr, ms, me, cols, hid, up, gb, ga)
     if not fast:
+        matrices = call(
+            functools.partial(finish_body, ticks - 1),
+            sums,
+            [((mid, out), BF16), ((mid, taps), BF16), ((mid, out), BF16)],
+        )
         bases, rights = general_tail(factor[0], matrices, splits)
         return tuple(value[None] for value in [leaving[None], *bases, *rights])
 
-    def scattered(keep, send, name):
-        got = swap(send, flips(0, True))
-        own, *sends = call(
-            fold_body,
-            name,
-            (keep, got),
-            [(keep.shape[1:], F32)] + [(keep.shape[1:], BF16)] * (chips - 1),
-        )
-        return own, [swap(value, flips(chip, False)) for chip, value in enumerate(sends, 1)]
-
-    own, others = scattered(*factor, "fold_factor")
-    (own,) = call(
-        total_body,
-        "total_factor",
-        (own, *others),
-        [((rank, piece), BF16)],
-    )
-    mine = [own] + [swap(own, flips(chip, False)) for chip in range(1, chips)]
-    other = swap(jnp.stack(mine), flips(0, True))
+    keep, send = factor
+    (own,) = call(chip_body, (keep, swap(send, flips(0, True))), [((rank, half), BF16)])
+    others = []
+    for chip in range(1, chips):
+        others.append(swap(own, flips(chip, False)))
+    packed = (mid // 2, out + taps + out)
+    keep, send, leaving = call(
+        functools.partial(packed_body, ticks - 1),
+        (leaving,) + sums,
+        [(packed, F32), (packed, BF16), (image, BF16)],
+        [pltpu.VMEM((mid, out), F32), pltpu.VMEM((mid, taps), F32), pltpu.VMEM((mid, out), F32)]
+        + [pltpu.SemaphoreType.DMA],
+        results=1,
+    )
+    (both,) = call(chip_body, (keep, swap(send, flips(0, True))), [(packed, BF16)])
+    (mine,) = call(total_body, (own, *others), [((rank, half), BF16)])
     part = (mid + mid + out) // replicas
-    operands = (*mine, other, *matrices)
-    pt, keep, send = call(
-        functools.partial(right_body, chips),
-        "right_products",
-        operands,
-        [((rank, total), BF16), ((chips, rank, part), F32), ((chips, rank, part), BF16)],
-        (pltpu.VMEM((rank, total), F32), pltpu.VMEM((replicas, rank, part), F32)),
-    )
-    own, others = scattered(keep, send, "fold_right")
+    pt, keep, *sends = call(
+        functools.partial(right_body, splits),
+        (mine, swap(mine, flips(0, True)), both),
+        [((rank, total), BF16), ((rank, part), F32)] + [((rank, part), BF16)] * (chips - 1),
+        [pltpu.VMEM((chips, rank, part), F32)],
+    )
+    others = [swap(send, flips(chip, False)) for chip, send in enumerate(sends, 1)]
+    shapes = [(rank, rows // replicas) for rows in splits]
     inverse, *bases = call(
         functools.partial(basis_body, splits),
-        "basis",
         (pt,),
-        [((3, rank, rank), F32)] + [((rank, rows // replicas), F32) for rows in splits],
-    )
-    operands = (inverse, own, *others)
+        [((3, rank, rank), F32)] + [(shape, F32) for shape in shapes],
+        [pltpu.VMEM(shape, F32) for shape in shapes] + [pltpu.SemaphoreType.DMA((3,))],
+        results=3,
+    )
+    shapes = [(rank, columns // replicas) for columns in (mid, mid, out)]
     rights = call(
         functools.partial(end_body, splits, replicas),
-        "right_factors",
-        operands,
-        [((rank, columns // replicas), F32) for columns in (mid, mid, out)],
+        (inverse, keep, *others),
+        [(shape, F32) for shape in shapes],
+        [pltpu.VMEM(shape, F32) for shape in shapes] + [pltpu.SemaphoreType.DMA((3,))],
+        results=3,
     )
     return tuple(value[None] for value in [leaving[None], *bases, *rights])
 

time: 69.3 us -> 57.9 us (0.84)
  local copies, waits for them, and re-layouts: 7.89 us -> 0.04 us
  starting transfers between devices: 15.3 us -> 12.1 us
  waiting for transfers between devices: 25.1 us -> 23.7 us
  Pallas kernels: 19.8 us -> 20.7 us
    unnamed x34 -> x14, local copies, waits for them, and re-layouts: 7.89 us -> 0.04 us
    ppermute x12 -> x9, starting transfers between devices: 11 us -> 7.75 us  [swap(): lax.ppermute(values, REPLICA_AXES, [(i, i ^ mask) for i in range(count)])]
    ppermute x12 -> x9, waiting for transfers between devices: 9.46 us -> 8.07 us  [swap(): lax.ppermute(values, REPLICA_AXES, [(i, i ^ mask) for i in range(count)])]
    pallas_call x14, Pallas kernels: 19.8 us -> 20.7 us  [call(): pl.pallas_call(body, in_specs=[hbm] * given + [vmem] * (len(operands) - g...]
  transfers between devices with their start and end apart: 15 -> 12, of which waited for: 12 -> 8; matrix products, arithmetic and copies ran while one was open for 4% -> 0% of each run, Pallas kernels for 19% -> 18%
where the time goes in v3:
time: 57.9 us; the launch traced here: 57.7 us
  waiting for transfers between devices  23.7 us (41%)
  Pallas kernels  20.7 us (36%)
  starting transfers between devices  12.1 us (21%)
  between operations  1.05 us (2%)
    pallas_call x14, Pallas kernels, call(): pl.pallas_call(body, in_specs=[hbm] * given + [vmem] * (len(operands) - g...  20.7 us
    ppermute x3, waiting for transfers between devices, shifted(): return lax.ppermute(block, 'section', [(i, i - 1) for i in range(1, count)])  15.7 us
    ppermute x9, waiting for transfers between devices, swap(): lax.ppermute(values, REPLICA_AXES, [(i, i ^ mask) for i in range(count)])  8.07 us
    ppermute x9, starting transfers between devices, swap(): lax.ppermute(values, REPLICA_AXES, [(i, i ^ mask) for i in range(count)])  7.75 us
    ppermute x3, starting transfers between devices, shifted(): return lax.ppermute(block, 'section', [(i, i - 1) for i in range(1, count)])  4.32 us
  transfers between devices with their start and end apart: 12, of which 8 were waited for; matrix products, arithmetic and copies ran while one was open for 0% of the time, Pallas kernels for 18%

profile of v3, /device:TPU:0, one launch (start us, length us, event | category | flops | bytes accessed | tf_op | source)
XLA Modules:
  0.0 57.7 jit_solution(17646296653450113008)
XLA Ops:
  0.6 3.7 %shard_map.171 = (bf16[4,196,512]{2,1,0:T(8,128)(2,1)S(1)}, bf16[512,256]{1,0:T(8,128)(2,1)S(1)}, bf16[2304,256]{1,0:T(8,128)(2,1)S(1)}, bf16[256,512]{1,0:T(8,1...) custom-call(bf16[196,4,512]{2,1,0:T(4,128)(2,1)} %bitcast.38, ...), custom_call_target="tpu_custom_call" | custom-call | tf_op jit(solution)/shard_map/pallas_call | solution.py:35
  4.4 1.4 %collective-permute-start = (bf16[196,512]{1,0:T(8,128)(2,1)S(1)}, bf16[196,512]{1,0:T(8,128)(2,1)S(1)}, u32[]{:S(2)}, u32[]{:S(2)}) collective-permute-start(bf16[196,512]{1,0:T(8,128)(2,1)S(1)} %get-tuple-element.66), channel_id=1, source_target_pairs={{8,0},{16,8},{24,16},{9,1},{17,9},{25,17},{10,2},{18,10},{26,18},{... | collective-permute-start | bytes 602120 | tf_op jit(solution)/shard_map/ppermute | solution.py:355
  5.8 1.9 %shard_map.172 = (bf16[196,2304]{1,0:T(8,128)(2,1)S(1)}, bf16[196,256]{1,0:T(8,128)(2,1)S(1)}, f32[196,256]{1,0:T(8,128)S(1)}, f32[196,256]{1,0:T(8,128)S(1)}, b...) custom-call(bf16[4,196,512]{2,1,0:T(8,128)(2,1)S(1)} %get-tuple-elem, ...), custom_call_target="tpu_custom_call" | custom-call | tf_op jit(solution)/shard_map/pallas_call | solution.py:35
  7.7 6.8 %collective-permute-done.arrived = bf16[196,512]{1,0:T(8,128)(2,1)S(1)} collective-permute-done((bf16[196,512]{1,0:T(8,128)(2,1)S(1)}, bf16[196,512]{1,0:T(8,128)(2,1)S(1)}, u32[]{:S(2)}, u32[]{:S(2)}) %collective-permute-start) | collective-permute-done | bytes 200736 | tf_op jit(solution)/shard_map/ppermute | solution.py:355
  14.5 1.1 %shard_map.173 = (bf16[196,512]{1,0:T(8,128)(2,1)S(1)}, bf16[196,256]{1,0:T(8,128)(2,1)S(1)}, bf16[196,256]{1,0:T(8,128)(2,1)S(1)}, bf16[196,512]{1,0:T(8,128)(2,1)S(1)}) custom-call(bf16[196,512]{1,0:T(8,128)(2,1)S(1)} %collective-permute-done.arrived, bf16[3,196,512]{2,1,0:T(8,128)(2,1)S(1)} %bitcast.21, bf16[512,256]{1,0:T(8,128)(2,1)S(1)} %get-tuple-element.67.wr, ...), custom_call_target="tpu_custom_call" | custom-call | tf_op jit(solution)/shard_map/pallas_call | solution.py:35
  15.7 1.4 %collective-permute-start.1 = (bf16[196,512]{1,0:T(8,128)(2,1)S(1)}, bf16[196,512]{1,0:T(8,128)(2,1)S(1)}, u32[]{:S(2)}, u32[]{:S(2)}) collective-permute-start(bf16[196,512]{1,0:T(8,128)(2,1)S(1)} %get-tuple-element.72), channel_id=1, source_target_pairs={{8,0},{16,8},{24,16},{9,1},{17,9},{25,17},{10,2},{18,10},{26,18},{... | collective-permute-start | bytes 602120 | tf_op jit(solution)/shard_map/ppermute | solution.py:355
  17.2 6.8 %collective-permute-done.1.arrived = bf16[196,512]{1,0:T(8,128)(2,1)S(1)} collective-permute-done((bf16[196,512]{1,0:T(8,128)(2,1)S(1)}, bf16[196,512]{1,0:T(8,128)(2,1)S(1)}, u32[]{:S(2)}, u32[]{:S(2)}) %collective-permute-start.1) | collective-permute-done | bytes 200736 | tf_op jit(solution)/shard_map/ppermute | solution.py:355
  24.0 1.1 %shard_map.174 = (bf16[196,512]{1,0:T(8,128)(2,1)S(1)}, bf16[196,256]{1,0:T(8,128)(2,1)S(1)}, bf16[196,256]{1,0:T(8,128)(2,1)S(1)}, bf16[196,512]{1,0:T(8,128)(2,1)S(1)}) custom-call(bf16[196,512]{1,0:T(8,128)(2,1)S(1)} %collective-permute-done.1.arrived, bf16[3,196,512]{2,1,0:T(8,128)(2,1)S(1)} %bitcast.22, bf16[512,256]{1,0:T(8,128)(2,1)S(1)} %get-tuple-element.67.wr, ...), custom_call_target="tpu_custom_call" | custom-call | tf_op jit(solution)/shard_map/pallas_call | solution.py:35
  25.1 1.5 %collective-permute-start.2 = (bf16[196,512]{1,0:T(8,128)(2,1)S(1)}, bf16[196,512]{1,0:T(8,128)(2,1)S(1)}, u32[]{:S(2)}, u32[]{:S(2)}) collective-permute-start(bf16[196,512]{1,0:T(8,128)(2,1)S(1)} %get-tuple-element.75), channel_id=1, source_target_pairs={{8,0},{16,8},{24,16},{9,1},{17,9},{25,17},{10,2},{18,10},{26,18},{... | collective-permute-start | bytes 602120 | tf_op jit(solution)/shard_map/ppermute | solution.py:355
  27.3 3.4 %shard_map.176 = (f32[32,3072]{1,0:T(8,128)S(1)}, f32[256,512]{1,0:T(8,128)S(1)}, f32[256,2304]{1,0:T(8,128)S(1)}, f32[256,512]{1,0:T(8,128)S(1)}) custom-call(bf16[4,196,512]{2,1,0:T(8,128)(2,1)S(1)} %get-tuple-element.65.x, f32[256,512]{1,0:T(8,128)S(1)} %get-tuple-element.80.etr, f32[256,2304]{1,0:T(8,128)S(1)} %get-tuple-element.81.ets, ...), custom_call_target="tpu_custom_call" | custom-call | tf_op jit(solution)/shard_map/pallas_call | solution.py:35
  30.8 2.0 %collective-permute-done.2.arrived = bf16[196,512]{1,0:T(8,128)(2,1)S(1)} collective-permute-done((bf16[196,512]{1,0:T(8,128)(2,1)S(1)}, bf16[196,512]{1,0:T(8,128)(2,1)S(1)}, u32[]{:S(2)}, u32[]{:S(2)}) %collective-permute-start.2) | collective-permute-done | bytes 200736 | tf_op jit(solution)/shard_map/ppermute | solution.py:355
  32.8 1.9 %shard_map.177 = (bf16[196,512]{1,0:T(8,128)(2,1)S(1)}, bf16[196,256]{1,0:T(8,128)(2,1)S(1)}, bf16[196,256]{1,0:T(8,128)(2,1)S(1)}, bf16[196,512]{1,0:T(8,128)(2...) custom-call(bf16[4,196,512]{2,1,0:T(8,128)(2,1)S(1)} %get-tuple-element.65.x, ...), custom_call_target="tpu_custom_call" | custom-call | tf_op jit(solution)/shard_map/pallas_call | solution.py:35
  34.7 1.5 %shard_map.178 = (f32[128,3328]{1,0:T(8,128)S(1)}, bf16[128,3328]{1,0:T(8,128)(2,1)S(1)}, bf16[196,512]{1,0:T(8,128)(2,1)}) custom-call(bf16[196,512]{1,0:T(8,128)(2,1)S(1)} %get-tuple-element.99.dx, bf16[4,196,512]{2,1,0:T(8,128)(2,1)S(1)} %get-tuple-element.65.x, f32[256,512]{1,0:T(8,128)S(1)} %get-tuple-element.100.mr, ...), custom_call_target="tpu_custom_call" | custom-call | tf_op jit(solution)/shard_map/pallas_call | solution.py:35
  36.7 2.0 %collective-permute-done.3.got = bf16[32,1536]{1,0:T(8,128)(2,1)S(1)} collective-permute-done((bf16[32,1536]{1,0:T(8,128)(2,1)S(1)}, bf16[32,1536]{1,0:T(8,128)(2,1)S(1)}, u32[]{:S(2)}, u32[]{:S(2)}) %collective-permute-start.3) | collective-permute-done | bytes 98336 | tf_op jit(solution)/shard_map/ppermute | solution.py:243
  38.7 1.5 %collective-permute-start.4 = (bf16[32,1536]{1,0:T(8,128)(2,1)S(1)}, bf16[32,1536]{1,0:T(8,128)(2,1)S(1)}, u32[]{:S(2)}, u32[]{:S(2)}) collective-permute-start(bf16[32,1536]{1,0:T(8,128)(2,1)S(1)} %shard_map.179.own), channel_id=1, source_target_pairs={{0,1},{1,0},{2,3},{3,2},{4,5},{5,4},{6,7},{7,6},{8,9},{9,8},{10,11... | collective-permute-start | bytes 294920 | tf_op jit(solution)/shard_map/ppermute | solution.py:243
  40.2 1.5 %collective-permute-start.5 = (bf16[32,1536]{1,0:T(8,128)(2,1)S(1)}, bf16[32,1536]{1,0:T(8,128)(2,1)S(1)}, u32[]{:S(2)}, u32[]{:S(2)}) collective-permute-start(bf16[32,1536]{1,0:T(8,128)(2,1)S(1)} %shard_map.179.own), channel_id=1, source_target_pairs={{0,4},{1,5},{2,6},{3,7},{4,0},{5,1},{6,2},{7,3},{8,12},{9,13},{10,... | collective-permute-start | bytes 294920 | tf_op jit(solution)/shard_map/ppermute | solution.py:243
  42.3 1.3 %collective-permute-done.4.flipped_local = bf16[32,1536]{1,0:T(8,128)(2,1)S(1)} collective-permute-done((bf16[32,1536]{1,0:T(8,128)(2,1)S(1)}, bf16[32,1536]{1,0:T(8,128)(2,1)S(1)}, u32[]{:S(2)}, u32[]{:S(2)}) %collective-permute-start.4) | collective-permute-done | bytes 98336 | tf_op jit(solution)/shard_map/ppermute | solution.py:243
  43.6 2.2 %collective-permute-done.5.flipped_node = bf16[32,1536]{1,0:T(8,128)(2,1)S(1)} collective-permute-done((bf16[32,1536]{1,0:T(8,128)(2,1)S(1)}, bf16[32,1536]{1,0:T(8,128)(2,1)S(1)}, u32[]{:S(2)}, u32[]{:S(2)}) %collective-permute-start.5) | collective-permute-done | bytes 98336 | tf_op jit(solution)/shard_map/ppermute | solution.py:243
  45.8 1.4 %collective-permute-done.6.flipped_both = bf16[32,1536]{1,0:T(8,128)(2,1)S(1)} collective-permute-done((bf16[32,1536]{1,0:T(8,128)(2,1)S(1)}, bf16[32,1536]{1,0:T(8,128)(2,1)S(1)}, u32[]{:S(2)}, u32[]{:S(2)}) %collective-permute-start.6) | collective-permute-done | bytes 98336 | tf_op jit(solution)/shard_map/ppermute | solution.py:243
  47.5 1.1 %collective-permute-done.7.other = bf16[32,1536]{1,0:T(8,128)(2,1)S(1)} collective-permute-done((bf16[32,1536]{1,0:T(8,128)(2,1)S(1)}, bf16[32,1536]{1,0:T(8,128)(2,1)S(1)}, u32[]{:S(2)}, u32[]{:S(2)}) %collective-permute-start.7) | collective-permute-done | bytes 98336 | tf_op jit(solution)/shard_map/ppermute | solution.py:243
  49.1 1.2 %collective-permute-start.9 = (bf16[32,128]{1,0:T(8,128)(2,1)S(1)}, bf16[32,128]{1,0:T(8,128)(2,1)S(1)}, u32[]{:S(2)}, u32[]{:S(2)}) collective-permute-start(bf16[32,128]{1,0:T(8,128)(2,1)S(1)} %get-tuple-element.117), channel_id=1, source_target_pairs={{0,1},{1,0},{2,3},{3,2},{4,5},{5,4},{6,7},{7,6},{8,9},{9,8},{10,11... | collective-permute-start | bytes 24584 | tf_op jit(solution)/shard_map/ppermute | solution.py:243
  50.3 1.4 %collective-permute-start.10 = (bf16[32,128]{1,0:T(8,128)(2,1)S(1)}, bf16[32,128]{1,0:T(8,128)(2,1)S(1)}, u32[]{:S(2)}, u32[]{:S(2)}) collective-permute-start(bf16[32,128]{1,0:T(8,128)(2,1)S(1)} %get-tuple-element.118), channel_id=1, source_target_pairs={{0,4},{1,5},{2,6},{3,7},{4,0},{5,1},{6,2},{7,3},{8,12},{9,13},{10,... | collective-permute-start | bytes 24584 | tf_op jit(solution)/shard_map/ppermute | solution.py:243
  52.7 3.9 %shard_map.183 = (f32[3,32,32]{2,1,0:T(8,128)S(1)}, f32[32,64]{1,0:T(8,128)}, f32[32,288]{1,0:T(8,128)}, f32[32,32]{1,0:T(8,128)}) custom-call(bf16[32,3072]{1,0:T(8,128)(2,1)S(1)} %get-tuple-element.111.pt), custom_call_target="tpu_custom_call" | custom-call | tf_op jit(solution)/shard_map/pallas_call | solution.py:35
  56.6 0.9 %shard_map.184 = (f32[32,32]{1,0:T(8,128)}, f32[32,32]{1,0:T(8,128)}, f32[32,64]{1,0:T(8,128)}) custom-call(f32[3,32,32]{2,1,0:T(8,128)S(1)} %get-tuple-element.115.inverse, f32[32,128]{1,0:T(8,128)S(1)} %get-tuple-element.116.own, bf16[32,128]{1,0:T(8,128)(2,1)S(1)} %collective-permute-done.9.a, bf16[32,128]{1,0:T(8,128)(2,1)S(1)} %collective-permute-done.10.b, ...), custom_call_target="tpu_custom_call" | custom-call | tf_op jit(solution)/shard_map/pallas_call | solution.py:35
  (28 shorter events, 3.5 us)
Async XLA Ops:
  4.4 10.2 %copy-start = (bf16[1,3,196,512]{3,2,1,0:T(8,128)(2,1)S(1)}, bf16[1,3,196,512]{3,2,1,0:T(8,128)(2,1)}, u32[]{:S(2)}) copy-start(bf16[1,3,196,512]{3,2,1,0:T(8,128)(2,1)} %param.14) | copy-start | bytes 1806340
  4.4 10.2 %collective-permute-start = (bf16[196,512]{1,0:T(8,128)(2,1)S(1)}, bf16[196,512]{1,0:T(8,128)(2,1)S(1)}, u32[]{:S(2)}, u32[]{:S(2)}) collective-permute-start(bf16[196,512]{1,0:T(8,128)(2,1)S(1)} %get-tuple-element.66), channel_id=1, source_target_pairs={{8,0},{16,8},{24,16},{9,1},{17,9},{25,17},{10,2},{18,10},{26,18},{... | collective-permute-start | bytes 602120 | tf_op jit(solution)/shard_map/ppermute | solution.py:355
  15.7 10.9 %copy-start.1 = (bf16[1,1,2304,256]{3,2,1,0:T(8,128)(2,1)S(1)}, bf16[1,1,2304,256]{3,2,1,0:T(8,128)(2,1)}, u32[]{:S(2)}) copy-start(bf16[1,1,2304,256]{3,2,1,0:T(8,128)(2,1)} %param.19) | copy-start | bytes 3538948
  15.7 10.9 %copy-start.2 = (bf16[1,1,256,512]{3,2,1,0:T(8,128)(2,1)S(1)}, bf16[1,1,256,512]{3,2,1,0:T(8,128)(2,1)}, u32[]{:S(2)}) copy-start(bf16[1,1,256,512]{3,2,1,0:T(8,128)(2,1)} %param.20) | copy-start | bytes 786436
  15.7 10.9 %copy-start.3 = (f32[1,32,512]{2,1,0:T(8,128)S(1)}, f32[1,32,512]{2,1,0:T(8,128)}, u32[]{:S(2)}) copy-start(f32[1,32,512]{2,1,0:T(8,128)} %param.23) | copy-start | bytes 196612
  15.7 10.9 %copy-start.4 = (f32[1,32,256]{2,1,0:T(8,128)S(1)}, f32[1,32,256]{2,1,0:T(8,128)}, u32[]{:S(2)}) copy-start(f32[1,32,256]{2,1,0:T(8,128)} %param.21) | copy-start | bytes 98308
  15.7 10.9 %copy-start.5 = (f32[1,32,256]{2,1,0:T(8,128)S(1)}, f32[1,32,256]{2,1,0:T(8,128)}, u32[]{:S(2)}) copy-start(f32[1,32,256]{2,1,0:T(8,128)} %param.22) | copy-start | bytes 98308
  15.7 10.9 %copy-start.6 = (bf16[1,1,512,256]{3,2,1,0:T(8,128)(2,1)S(1)}, bf16[1,1,512,256]{3,2,1,0:T(8,128)(2,1)}, u32[]{:S(2)}) copy-start(bf16[1,1,512,256]{3,2,1,0:T(8,128)(2,1)} %param.18) | copy-start | bytes 786436
  15.7 8.3 %collective-permute-start.1 = (bf16[196,512]{1,0:T(8,128)(2,1)S(1)}, bf16[196,512]{1,0:T(8,128)(2,1)S(1)}, u32[]{:S(2)}, u32[]{:S(2)}) collective-permute-start(bf16[196,512]{1,0:T(8,128)(2,1)S(1)} %get-tuple-element.72), channel_id=1, source_target_pairs={{8,0},{16,8},{24,16},{9,1},{17,9},{25,17},{10,2},{18,10},{26,18},{... | collective-permute-start | bytes 602120 | tf_op jit(solution)/shard_map/ppermute | solution.py:355
  25.1 7.7 %collective-permute-start.2 = (bf16[196,512]{1,0:T(8,128)(2,1)S(1)}, bf16[196,512]{1,0:T(8,128)(2,1)S(1)}, u32[]{:S(2)}, u32[]{:S(2)}) collective-permute-start(bf16[196,512]{1,0:T(8,128)(2,1)S(1)} %get-tuple-element.75), channel_id=1, source_target_pairs={{8,0},{16,8},{24,16},{9,1},{17,9},{25,17},{10,2},{18,10},{26,18},{... | collective-permute-start | bytes 602120 | tf_op jit(solution)/shard_map/ppermute | solution.py:355
  36.1 11.2 %collective-permute-start.8 = (bf16[128,3328]{1,0:T(8,128)(2,1)S(1)}, bf16[128,3328]{1,0:T(8,128)(2,1)S(1)}, u32[]{:S(2)}, u32[]{:S(2)}) collective-permute-start(bf16[128,3328]{1,0:T(8,128)(2,1)S(1)} %get-tuple-element.110), channel_id=1, source_target_pairs={{0,2},{1,3},{2,0},{3,1},{4,6},{5,7},{6,4},{7,5},{8,10},{9,11},{10,... | collective-permute-start | bytes 2555912 | tf_op jit(solution)/shard_map/ppermute | solution.py:243
  36.2 2.5 %collective-permute-start.3 = (bf16[32,1536]{1,0:T(8,128)(2,1)S(1)}, bf16[32,1536]{1,0:T(8,128)(2,1)S(1)}, u32[]{:S(2)}, u32[]{:S(2)}) collective-permute-start(bf16[32,1536]{1,0:T(8,128)(2,1)S(1)} %get-tuple-element.108), channel_id=1, source_target_pairs={{0,2},{1,3},{2,0},{3,1},{4,6},{5,7},{6,4},{7,5},{8,10},{9,11},{10,... | collective-permute-start | bytes 294920 | tf_op jit(solution)/shard_map/ppermute | solution.py:243
  38.7 4.9 %collective-permute-start.4 = (bf16[32,1536]{1,0:T(8,128)(2,1)S(1)}, bf16[32,1536]{1,0:T(8,128)(2,1)S(1)}, u32[]{:S(2)}, u32[]{:S(2)}) collective-permute-start(bf16[32,1536]{1,0:T(8,128)(2,1)S(1)} %shard_map.179.own), channel_id=1, source_target_pairs={{0,1},{1,0},{2,3},{3,2},{4,5},{5,4},{6,7},{7,6},{8,9},{9,8},{10,11... | collective-permute-start | bytes 294920 | tf_op jit(solution)/shard_map/ppermute | solution.py:243
  40.2 5.6 %collective-permute-start.5 = (bf16[32,1536]{1,0:T(8,128)(2,1)S(1)}, bf16[32,1536]{1,0:T(8,128)(2,1)S(1)}, u32[]{:S(2)}, u32[]{:S(2)}) collective-permute-start(bf16[32,1536]{1,0:T(8,128)(2,1)S(1)} %shard_map.179.own), channel_id=1, source_target_pairs={{0,4},{1,5},{2,6},{3,7},{4,0},{5,1},{6,2},{7,3},{8,12},{9,13},{10,... | collective-permute-start | bytes 294920 | tf_op jit(solution)/shard_map/ppermute | solution.py:243
  41.7 5.5 %collective-permute-start.6 = (bf16[32,1536]{1,0:T(8,128)(2,1)S(1)}, bf16[32,1536]{1,0:T(8,128)(2,1)S(1)}, u32[]{:S(2)}, u32[]{:S(2)}) collective-permute-start(bf16[32,1536]{1,0:T(8,128)(2,1)S(1)} %shard_map.179.own), channel_id=1, source_target_pairs={{0,5},{1,4},{2,7},{3,6},{4,1},{5,0},{6,3},{7,2},{8,13},{9,12},{10,... | collective-permute-start | bytes 294920 | tf_op jit(solution)/shard_map/ppermute | solution.py:243
  47.3 1.4 %collective-permute-start.7 = (bf16[32,1536]{1,0:T(8,128)(2,1)S(1)}, bf16[32,1536]{1,0:T(8,128)(2,1)S(1)}, u32[]{:S(2)}, u32[]{:S(2)}) collective-permute-start(bf16[32,1536]{1,0:T(8,128)(2,1)S(1)} %shard_map.180.mine), channel_id=1, source_target_pairs={{0,2},{1,3},{2,0},{3,1},{4,6},{5,7},{6,4},{7,5},{8,10},{9,11},{10,... | collective-permute-start | bytes 294920 | tf_op jit(solution)/shard_map/ppermute | solution.py:243
  49.1 7.5 %collective-permute-start.9 = (bf16[32,128]{1,0:T(8,128)(2,1)S(1)}, bf16[32,128]{1,0:T(8,128)(2,1)S(1)}, u32[]{:S(2)}, u32[]{:S(2)}) collective-permute-start(bf16[32,128]{1,0:T(8,128)(2,1)S(1)} %get-tuple-element.117), channel_id=1, source_target_pairs={{0,1},{1,0},{2,3},{3,2},{4,5},{5,4},{6,7},{7,6},{8,9},{9,8},{10,11... | collective-permute-start | bytes 24584 | tf_op jit(solution)/shard_map/ppermute | solution.py:243
  50.3 6.3 %collective-permute-start.10 = (bf16[32,128]{1,0:T(8,128)(2,1)S(1)}, bf16[32,128]{1,0:T(8,128)(2,1)S(1)}, u32[]{:S(2)}, u32[]{:S(2)}) collective-permute-start(bf16[32,128]{1,0:T(8,128)(2,1)S(1)} %get-tuple-element.118), channel_id=1, source_target_pairs={{0,4},{1,5},{2,6},{3,7},{4,0},{5,1},{6,2},{7,3},{8,12},{9,13},{10,... | collective-permute-start | bytes 24584 | tf_op jit(solution)/shard_map/ppermute | solution.py:243
  51.8 4.8 %collective-permute-start.11 = (bf16[32,128]{1,0:T(8,128)(2,1)S(1)}, bf16[32,128]{1,0:T(8,128)(2,1)S(1)}, u32[]{:S(2)}, u32[]{:S(2)}) collective-permute-start(bf16[32,128]{1,0:T(8,128)(2,1)S(1)} %get-tuple-element.119), channel_id=1, source_target_pairs={{0,5},{1,4},{2,7},{3,6},{4,1},{5,0},{6,3},{7,2},{8,13},{9,12},{10,... | collective-permute-start | bytes 24584 | tf_op jit(solution)/shard_map/ppermute | solution.py:243

commit v4 on v3

--- a/solution.py
+++ b/solution.py
@@ -77,29 +77,40 @@
         ].astype(BF16)
 
 
-def forward(inputs, w_reduce, w_spatial, padded, columns, hidden, slope_one, slope_two, side):
+def forward(inputs, w_reduce, w_spatial, padded, columns, hidden, slope_one, slope_two, side,
+            ready=None):
     pre = mm(inputs[...], w_reduce[...])
     logistic = jax.nn.sigmoid(pre)
     slope_one[...] = logistic * (1.0 + pre * (1.0 - logistic))
     spread_taps(pre * logistic, padded, columns, side, False)
+    if ready is not None:
+        ready()
     pre = mm(columns[...], w_spatial[...])
     logistic = jax.nn.sigmoid(pre)
     slope_two[...] = logistic * (1.0 + pre * (1.0 - logistic))
     hidden[...] = (pre * logistic).astype(BF16)
 
 
-def backward(up, w_reduce, w_spatial, w_expand, slope_one, slope_two, padded, taps, side):
+def upper(up, w_expand, slope_two):
+    return (mm(up, w_expand[...], NT) * slope_two[...]).astype(BF16)
+
+
+def lower(up, grad_two, w_reduce, w_spatial, slope_one, padded, taps, side):
     channels = slope_one.shape[1]
-    grad = mm(up, w_expand[...], NT) * slope_two[...]
-    spread_taps(grad, padded, taps, side, True)
+    spread_taps(grad_two.astype(F32), padded, taps, side, True)
     back = None
     for tap in range(9):
         block = slice(tap * channels, (tap + 1) * channels)
         term = mm(taps[:, block], w_spatial[block, :], NT)
         back = term if back is None else back + term
-    grad_two = grad.astype(BF16)
     grad_one = (back * slope_one[...]).astype(BF16)
     leaving = (up.astype(F32) + mm(grad_one, w_reduce[...], NT)).astype(BF16)
+    return grad_one, leaving
+
+
+def backward(up, w_reduce, w_spatial, w_expand, slope_one, slope_two, padded, taps, side):
+    grad_two = upper(up, w_expand, slope_two)
+    grad_one, leaving = lower(up, grad_two, w_reduce, w_spatial, slope_one, padded, taps, side)
     return grad_two, grad_one, leaving
 
 
@@ -112,8 +123,7 @@
     copies[0].wait()
     x[...] = jnp.swapaxes(raw[...], 0, 1)
     copies[1].wait()
-    copies[2].wait()
-    forward(x.at[0], wr, ws, padded, cols, hid, s1, s2, side)
+    forward(x.at[0], wr, ws, padded, cols, hid, s1, s2, side, copies[2].wait)
     copies[3].wait()
     copies[4].wait()
     gb[...], ga[...], dx[...] = backward(up[...], wr, ws, we, s1, s2, padded, taps, side)
@@ -171,24 +181,33 @@
         me[...] = base_e + mm(hid[...], up[...], TN)
 
 
-def last_body(side, tick, x, arrived, loss, wr, ws, we, cols, hid, s1, s2, pt, pr, ps, pe,
-              up, gb, ga, *refs):
-    outs, (padded, taps, factor) = refs[:-3], refs[-3:]
-    dx = outs[0]
+def head_body(tick, arrived, loss, we, cols, hid, s2, pt, ps, pe, up, gb, *refs):
+    outs, factor = refs[:-1], refs[-1]
     value = chosen(arrived, loss, tick)
     up[...] = value
-    gb[...], ga[...], dx[...] = backward(value, wr, ws, we, s1, s2, padded, taps, side)
-    factors = (x.at[tick], cols, hid, value, gb[...], ga[...], pr, ps, pe)
-    if len(outs) == 2:
-        add_factor(pt, outs[1], *factors)
-    else:
-        add_factor(pt, factor, *factors)
-        keep, send = outs[1:]
-        half = keep.shape[1]
-        core = core_index()
-        keep[...] = factor[:, pl.ds(pl.multiple_of(core * half, 128), half)]
-        sent = factor[:, pl.ds(pl.multiple_of((1 - core) * half, 128), half)]
-        send[...] = sent.astype(BF16)
+    grad = upper(value, we, s2)
+    gb[...] = grad
+    spatial = cols.shape[1]
+    start = pt.shape[1] - factor.shape[1]
+    factor[:, :spatial] = pt[:, start : start + spatial] + low_rank(ps[...], grad, cols[...])
+    factor[:, spatial:] = pt[:, start + spatial :] + low_rank(pe[...], value, hid[...])
+    if len(outs) == 1:
+        outs[0][...] = factor[...]
+        return
+    keep, send = outs
+    half = keep.shape[1]
+    core = core_index()
+    keep[...] = factor[:, pl.ds(pl.multiple_of(core * half, 128), half)]
+    sent = factor[:, pl.ds(pl.multiple_of((1 - core) * half, 128), half)]
+    send[...] = sent.astype(BF16)
+
+
+def tail_body(side, tick, x, up, gb, wr, ws, s1, pt, pr, ga, dx, factor, padded, taps):
+    grad, dx[...] = lower(up[...], gb[...], wr, ws, s1, padded, taps, side)
+    ga[...] = grad
+    rows = factor.shape[1]
+    total = pt[:, :rows] + low_rank(pr[...], grad, x[tick])
+    factor[...] = total.astype(factor.dtype)
 
 
 def finish_body(tick, x, mr, ms, me, cols, hid, up, gb, ga, br, bs, be):
@@ -227,6 +246,12 @@
     both[...] = (keep[...] + got[...].astype(F32)).astype(BF16)
 
 
+def gather_body(keep, got, alone, own):
+    half = keep.shape[1]
+    own[:, :half] = (keep[...] + got[...].astype(F32)).astype(BF16)
+    own[:, half:] = alone[...]
+
+
 def core_index():
     return lax.rem(lax.axis_index("node"), 2)
 
@@ -251,11 +276,13 @@
 
 def right_body(splits, mine, other, both, pt, keep, *refs):
     sends, pieces = refs[:-1], refs[-1]
-    half = mine.shape[1]
+    out, taps, _ = splits
+    half = mine.shape[1] - out
     core = core_index()
-    pt[:, pl.ds(pl.multiple_of(core * half, 128), half)] = mine[...]
-    pt[:, pl.ds(pl.multiple_of((1 - core) * half, 128), half)] = other[...]
-    out, taps, _ = splits
+    alone = mine[:, half:].astype(F32) + other[:, half:].astype(F32)
+    pt[:, :out] = alone.astype(BF16)
+    pt[:, pl.ds(pl.multiple_of(out + core * half, 128), half)] = mine[:, :half]
+    pt[:, pl.ds(pl.multiple_of(out + (1 - core) * half, 128), half)] = other[:, :half]
     wide = both.shape[1]
     expand = jnp.concatenate([both[:, wide - out : wide - out // 2], both[:, wide - out // 2 :]], 0)
     parts = (
@@ -277,10 +304,9 @@
         send[...] = pieces[me ^ chip].astype(BF16)
 
 
-def inverse_factors(grams):
-    rank = grams[0].shape[0]
-    high = 8
-    row = lax.broadcasted_iota(jnp.int32, (high, 1), 0)
+def inverse_factors(grams, width=4):
+    rank, high = grams[0].shape[0], 8
+    row = lax.broadcasted_iota(jnp.int32, (high, 2 * rank), 0)
     lane = lax.broadcasted_iota(jnp.int32, (high, 2 * rank), 1)
     tables, pivots = [], []
     for gram in grams:
@@ -290,20 +316,36 @@
             unit = jnp.where(lane == row + (start + rank), 1.0, 0.0)
             blocks.append(jnp.where(lane < rank, wide[start : start + high], unit))
         tables.append(blocks)
-        pivots.append([jnp.ones((high, 1), F32) for _ in blocks])
-    for step in range(rank):
+        pivots.append([jnp.ones((high, 2 * rank), F32) for _ in blocks])
+    for step in range(0, rank, width):
         first, at = step // high, step % high
         for blocks, kept in zip(tables, pivots):
-            pivot = blocks[first][at : at + 1, step : step + 1]
-            line = blocks[first][at : at + 1, :] * (1.0 / pivot)
-            kept[first] = jnp.where(row == at, pivot, kept[first])
-            for index in range(first, len(blocks)):
-                column = blocks[index][:, step : step + 1]
-                if index == first:
-                    column = jnp.where(row > at, column, 0.0)
-                blocks[index] = blocks[index] - column * line
+            lines = [blocks[first][at + p : at + p + 1] for p in range(width)]
+            columns = [
+                [jnp.broadcast_to(block[:, step + p : step + p + 1], block.shape) for p in range(width)]
+                for block in blocks[first:]
+            ]
+            entry = [[columns[0][q][at + p : at + p + 1] for q in range(p + 1)] for p in range(width)]
+            for p in range(width):
+                inverse = 1.0 / entry[p][p]
+                kept[first] = jnp.where(row == at + p, entry[p][p], kept[first])
+                scaled = lines[p] * inverse
+                ratios = [entry[q][p] * inverse for q in range(p + 1, width)]
+                for q, ratio in enumerate(ratios, p + 1):
+                    lines[q] = lines[q] - ratio * lines[p]
+                    for t in range(p + 1, q + 1):
+                        entry[q][t] = entry[q][t] - ratio * entry[t][p]
+                for index, column in enumerate(columns):
+                    factor = column[p]
+                    for q, ratio in enumerate(ratios, p + 1):
+                        column[q] = column[q] - ratio * factor
+                    if index == 0:
+                        factor = jnp.where(row >= at + width, factor, 0.0)
+                    blocks[first + index] = blocks[first + index] - factor * scaled
+            for p in range(1, width):
+                blocks[first] = jnp.where(row == at + p, lines[p], blocks[first])
     return [
-        jnp.concatenate([block[:, rank:] * lax.rsqrt(p) for block, p in zip(blocks, kept)], 0)
+        jnp.concatenate([(block * lax.rsqrt(p))[:, rank:] for block, p in zip(blocks, kept)], 0)
         for blocks, kept in zip(tables, pivots)
     ]
 
@@ -460,16 +502,22 @@
     )
 
     replicas = lax.axis_size(REPLICA_AXES)
-    fast = lax.axis_size("node") == 4 and lax.axis_size("local") == 2 and total % 256 == 0
+    fast = lax.axis_size("node") == 4 and lax.axis_size("local") == 2 and (taps + mid) % 256 == 0
     chips = replicas // 2
-    half = total // 2
+    half = (taps + mid) // 2
     cols, hid, s1, s2 = ahead[4 * ticks - 8 : 4 * ticks - 4]
-    extra = [((rank, half), F32), ((rank, half), BF16)] if fast else [((rank, total), F32)]
-    up, gb, ga, leaving, *factor = call(
-        functools.partial(last_body, side, ticks - 1),
-        (x, arrived, loss) + weights + (cols, hid, s1, s2, pt, pr, ps, pe),
-        [(image, BF16)] + grads + extra,
-        (padded, tap_space, pltpu.VMEM((rank, total), F32)),
+    extra = [((rank, half), F32), ((rank, half), BF16)] if fast else [((rank, 2 * half), F32)]
+    up, gb, *factor = call(
+        functools.partial(head_body, ticks - 1),
+        (arrived, loss, we, cols, hid, s2, pt, ps, pe),
+        [(image, BF16), (inner, BF16)] + extra,
+        (pltpu.VMEM((rank, 2 * half), F32),),
+    )
+    ga, leaving, alone = call(
+        functools.partial(tail_body, side, ticks - 1),
+        (x, up, gb, wr, ws, s1, pt, pr),
+        [(inner, BF16), (image, BF16), ((rank, out), BF16 if fast else F32)],
+        (padded, tap_space),
     )
     sums = (x, mr, ms, me, cols, hid, up, gb, ga)
     if not fast:
@@ -478,11 +526,13 @@
             sums,
             [((mid, out), BF16), ((mid, taps), BF16), ((mid, out), BF16)],
         )
-        bases, rights = general_tail(factor[0], matrices, splits)
+        bases, rights = general_tail(jnp.concatenate([alone, factor[0]], 1), matrices, splits)
         return tuple(value[None] for value in [leaving[None], *bases, *rights])
 
     keep, send = factor
-    (own,) = call(chip_body, (keep, swap(send, flips(0, True))), [((rank, half), BF16)])
+    carried = ((rank, half + out), BF16)
+    got = swap(send, flips(0, True))
+    (own,) = call(gather_body, (keep, got, alone), [carried])
     others = []
     for chip in range(1, chips):
         others.append(swap(own, flips(chip, False)))
@@ -496,7 +546,7 @@
         results=1,
     )
     (both,) = call(chip_body, (keep, swap(send, flips(0, True))), [(packed, BF16)])
-    (mine,) = call(total_body, (own, *others), [((rank, half), BF16)])
+    (mine,) = call(total_body, (own, *others), [carried])
     part = (mid + mid + out) // replicas
     pt, keep, *sends = call(
         functools.partial(right_body, splits),

time: 57.9 us -> 58 us (level)
  waiting for transfers between devices: 23.7 us -> 25.5 us
  Pallas kernels: 20.7 us -> 19.1 us
    ppermute x9, waiting for transfers between devices: 8.07 us -> 9.81 us  [swap(): lax.ppermute(values, REPLICA_AXES, [(i, i ^ mask) for i in range(count)])]
    pallas_call x14 -> x15, Pallas kernels: 20.7 us -> 19.1 us  [call(): pl.pallas_call(body, in_specs=[hbm] * given + [vmem] * (len(operands) - g...]
  transfers between devices with their start and end apart: 12 -> 12, of which waited for: 8 -> 9; matrix products, arithmetic and copies ran while one was open for 0% -> 0% of each run, Pallas kernels for 18% -> 15%
where the time goes in v4:
time: 58 us; the launch traced here: 57.8 us
  waiting for transfers between devices  25.5 us (44%)
  Pallas kernels  19.1 us (33%)
  starting transfers between devices  12.1 us (21%)
  between operations  1.05 us (2%)
    pallas_call x15, Pallas kernels, call(): pl.pallas_call(body, in_specs=[hbm] * given + [vmem] * (len(operands) - g...  19.1 us
    ppermute x3, waiting for transfers between devices, shifted(): return lax.ppermute(block, 'section', [(i, i - 1) for i in range(1, count)])  15.7 us
    ppermute x9, waiting for transfers between devices, swap(): lax.ppermute(values, REPLICA_AXES, [(i, i ^ mask) for i in range(count)])  9.81 us
    ppermute x9, starting transfers between devices, swap(): lax.ppermute(values, REPLICA_AXES, [(i, i ^ mask) for i in range(count)])  7.75 us
    ppermute x3, starting transfers between devices, shifted(): return lax.ppermute(block, 'section', [(i, i - 1) for i in range(1, count)])  4.32 us
  transfers between devices with their start and end apart: 12, of which 9 were waited for; matrix products, arithmetic and copies ran while one was open for 0% of the time, Pallas kernels for 15%

profile of v4, /device:TPU:0, one launch (start us, length us, event | category | flops | bytes accessed | tf_op | source)
XLA Modules:
  0.0 57.8 jit_solution(10378804518845255886)
XLA Ops:
  0.6 3.6 %shard_map.171 = (bf16[4,196,512]{2,1,0:T(8,128)(2,1)S(1)}, bf16[512,256]{1,0:T(8,128)(2,1)S(1)}, bf16[2304,256]{1,0:T(8,128)(2,1)S(1)}, bf16[256,512]{1,0:T(8,1...) custom-call(bf16[196,4,512]{2,1,0:T(4,128)(2,1)} %bitcast.38, ...), custom_call_target="tpu_custom_call" | custom-call | tf_op jit(solution)/shard_map/pallas_call | solution.py:35
  4.3 1.4 %collective-permute-start = (bf16[196,512]{1,0:T(8,128)(2,1)S(1)}, bf16[196,512]{1,0:T(8,128)(2,1)S(1)}, u32[]{:S(2)}, u32[]{:S(2)}) collective-permute-start(bf16[196,512]{1,0:T(8,128)(2,1)S(1)} %get-tuple-element.67), channel_id=1, source_target_pairs={{8,0},{16,8},{24,16},{9,1},{17,9},{25,17},{10,2},{18,10},{26,18},{... | collective-permute-start | bytes 602120 | tf_op jit(solution)/shard_map/ppermute | solution.py:397
  5.7 1.9 %shard_map.172 = (bf16[196,2304]{1,0:T(8,128)(2,1)S(1)}, bf16[196,256]{1,0:T(8,128)(2,1)S(1)}, f32[196,256]{1,0:T(8,128)S(1)}, f32[196,256]{1,0:T(8,128)S(1)}, b...) custom-call(bf16[4,196,512]{2,1,0:T(8,128)(2,1)S(1)} %get-tuple-elem, ...), custom_call_target="tpu_custom_call" | custom-call | tf_op jit(solution)/shard_map/pallas_call | solution.py:35
  7.6 6.8 %collective-permute-done.arrived = bf16[196,512]{1,0:T(8,128)(2,1)S(1)} collective-permute-done((bf16[196,512]{1,0:T(8,128)(2,1)S(1)}, bf16[196,512]{1,0:T(8,128)(2,1)S(1)}, u32[]{:S(2)}, u32[]{:S(2)}) %collective-permute-start) | collective-permute-done | bytes 200736 | tf_op jit(solution)/shard_map/ppermute | solution.py:397
  14.4 1.1 %shard_map.173 = (bf16[196,512]{1,0:T(8,128)(2,1)S(1)}, bf16[196,256]{1,0:T(8,128)(2,1)S(1)}, bf16[196,256]{1,0:T(8,128)(2,1)S(1)}, bf16[196,512]{1,0:T(8,128)(2,1)S(1)}) custom-call(bf16[196,512]{1,0:T(8,128)(2,1)S(1)} %collective-permute-done.arrived, bf16[3,196,512]{2,1,0:T(8,128)(2,1)S(1)} %bitcast.21, bf16[512,256]{1,0:T(8,128)(2,1)S(1)} %get-tuple-element.68.wr, ...), custom_call_target="tpu_custom_call" | custom-call | tf_op jit(solution)/shard_map/pallas_call | solution.py:35
  15.6 1.4 %collective-permute-start.1 = (bf16[196,512]{1,0:T(8,128)(2,1)S(1)}, bf16[196,512]{1,0:T(8,128)(2,1)S(1)}, u32[]{:S(2)}, u32[]{:S(2)}) collective-permute-start(bf16[196,512]{1,0:T(8,128)(2,1)S(1)} %get-tuple-element.73), channel_id=1, source_target_pairs={{8,0},{16,8},{24,16},{9,1},{17,9},{25,17},{10,2},{18,10},{26,18},{... | collective-permute-start | bytes 602120 | tf_op jit(solution)/shard_map/ppermute | solution.py:397
  17.1 6.8 %collective-permute-done.1.arrived = bf16[196,512]{1,0:T(8,128)(2,1)S(1)} collective-permute-done((bf16[196,512]{1,0:T(8,128)(2,1)S(1)}, bf16[196,512]{1,0:T(8,128)(2,1)S(1)}, u32[]{:S(2)}, u32[]{:S(2)}) %collective-permute-start.1) | collective-permute-done | bytes 200736 | tf_op jit(solution)/shard_map/ppermute | solution.py:397
  23.9 1.1 %shard_map.174 = (bf16[196,512]{1,0:T(8,128)(2,1)S(1)}, bf16[196,256]{1,0:T(8,128)(2,1)S(1)}, bf16[196,256]{1,0:T(8,128)(2,1)S(1)}, bf16[196,512]{1,0:T(8,128)(2,1)S(1)}) custom-call(bf16[196,512]{1,0:T(8,128)(2,1)S(1)} %collective-permute-done.1.arrived, bf16[3,196,512]{2,1,0:T(8,128)(2,1)S(1)} %bitcast.22, bf16[512,256]{1,0:T(8,128)(2,1)S(1)} %get-tuple-element.68.wr, ...), custom_call_target="tpu_custom_call" | custom-call | tf_op jit(solution)/shard_map/pallas_call | solution.py:35
  25.0 1.5 %collective-permute-start.2 = (bf16[196,512]{1,0:T(8,128)(2,1)S(1)}, bf16[196,512]{1,0:T(8,128)(2,1)S(1)}, u32[]{:S(2)}, u32[]{:S(2)}) collective-permute-start(bf16[196,512]{1,0:T(8,128)(2,1)S(1)} %get-tuple-element.76), channel_id=1, source_target_pairs={{8,0},{16,8},{24,16},{9,1},{17,9},{25,17},{10,2},{18,10},{26,18},{... | collective-permute-start | bytes 602120 | tf_op jit(solution)/shard_map/ppermute | solution.py:397
  27.2 3.4 %shard_map.176 = (f32[32,3072]{1,0:T(8,128)S(1)}, f32[256,512]{1,0:T(8,128)S(1)}, f32[256,2304]{1,0:T(8,128)S(1)}, f32[256,512]{1,0:T(8,128)S(1)}) custom-call(bf16[4,196,512]{2,1,0:T(8,128)(2,1)S(1)} %get-tuple-element.66.x, f32[256,512]{1,0:T(8,128)S(1)} %get-tuple-element.80.etr, f32[256,2304]{1,0:T(8,128)S(1)} %get-tuple-element.81.ets, ...), custom_call_target="tpu_custom_call" | custom-call | tf_op jit(solution)/shard_map/pallas_call | solution.py:35
  30.7 2.0 %collective-permute-done.2.arrived = bf16[196,512]{1,0:T(8,128)(2,1)S(1)} collective-permute-done((bf16[196,512]{1,0:T(8,128)(2,1)S(1)}, bf16[196,512]{1,0:T(8,128)(2,1)S(1)}, u32[]{:S(2)}, u32[]{:S(2)}) %collective-permute-start.2) | collective-permute-done | bytes 200736 | tf_op jit(solution)/shard_map/ppermute | solution.py:397
  32.7 1.0 %shard_map.177 = (bf16[196,512]{1,0:T(8,128)(2,1)S(1)}, bf16[196,256]{1,0:T(8,128)(2,1)S(1)}, f32[32,1280]{1,0:T(8,128)S(1)}, bf16[32,1280]{1,0:T(8,128)(2,1)S(1)}) custom-call(bf16[196,512]{1,0:T(8,128)(2,1)S(1)} %collective-permute-done.2.arrived, bf16[3,196,512]{2,1,0:T(8,128)(2,1)S(1)} %bitcast.23, bf16[256,512]{1,0:T(8,128)(2,1)S(1)} %get-tuple-element.70.we, ...), custom_call_target="tpu_custom_call" | custom-call | tf_op jit(solution)/shard_map/pallas_call | solution.py:35
  33.7 1.0 %shard_map.178 = (bf16[196,256]{1,0:T(8,128)(2,1)S(1)}, bf16[196,512]{1,0:T(8,128)(2,1)S(1)}, bf16[32,512]{1,0:T(8,128)(2,1)S(1)}) custom-call(bf16[4,196,512]{2,1,0:T(8,128)(2,1)S(1)} %get-tuple-element.66.x, bf16[196,512]{1,0:T(8,128)(2,1)S(1)} %get-tuple-element.99.up, bf16[196,256]{1,0:T(8,128)(2,1)S(1)} %get-tuple-element.100.gb, ...), custom_call_target="tpu_custom_call" | custom-call | tf_op jit(solution)/shard_map/pallas_call | solution.py:35
  34.6 1.5 %shard_map.179 = (f32[128,3328]{1,0:T(8,128)S(1)}, bf16[128,3328]{1,0:T(8,128)(2,1)S(1)}, bf16[196,512]{1,0:T(8,128)(2,1)}) custom-call(bf16[196,512]{1,0:T(8,128)(2,1)S(1)} %get-tuple-element.102.dx, bf16[4,196,512]{2,1,0:T(8,128)(2,1)S(1)} %get-tuple-element.66.x, f32[256,512]{1,0:T(8,128)S(1)} %get-tuple-element.103.mr, ...), custom_call_target="tpu_custom_call" | custom-call | tf_op jit(solution)/shard_map/pallas_call | solution.py:35
  36.7 2.0 %collective-permute-done.3.got = bf16[32,1280]{1,0:T(8,128)(2,1)S(1)} collective-permute-done((bf16[32,1280]{1,0:T(8,128)(2,1)S(1)}, bf16[32,1280]{1,0:T(8,128)(2,1)S(1)}, u32[]{:S(2)}, u32[]{:S(2)}) %collective-permute-start.3) | collective-permute-done | bytes 81952 | tf_op jit(solution)/shard_map/ppermute | solution.py:268
  38.7 2.4 %collective-permute-start.6 = (bf16[32,1792]{1,0:T(8,128)(2,1)S(1)}, bf16[32,1792]{1,0:T(8,128)(2,1)S(1)}, u32[]{:S(2)}, u32[]{:S(2)}) collective-permute-start(bf16[32,1792]{1,0:T(8,128)(2,1)S(1)} %shard_map.180.own), channel_id=1, source_target_pairs={{0,5},{1,4},{2,7},{3,6},{4,1},{5,0},{6,3},{7,2},{8,13},{9,12},{10,... | collective-permute-start | bytes 344072 | tf_op jit(solution)/shard_map/ppermute | solution.py:268
  42.3 3.4 %collective-permute-done.6.flipped_both = bf16[32,1792]{1,0:T(8,128)(2,1)S(1)} collective-permute-done((bf16[32,1792]{1,0:T(8,128)(2,1)S(1)}, bf16[32,1792]{1,0:T(8,128)(2,1)S(1)}, u32[]{:S(2)}, u32[]{:S(2)}) %collective-permute-start.6) | collective-permute-done | bytes 114720 | tf_op jit(solution)/shard_map/ppermute | solution.py:268
  45.7 1.6 %collective-permute-done.5.flipped_node = bf16[32,1792]{1,0:T(8,128)(2,1)S(1)} collective-permute-done((bf16[32,1792]{1,0:T(8,128)(2,1)S(1)}, bf16[32,1792]{1,0:T(8,128)(2,1)S(1)}, u32[]{:S(2)}, u32[]{:S(2)}) %collective-permute-start.5) | collective-permute-done | bytes 114720 | tf_op jit(solution)/shard_map/ppermute | solution.py:268
  47.6 1.1 %collective-permute-done.7.other = bf16[32,1792]{1,0:T(8,128)(2,1)S(1)} collective-permute-done((bf16[32,1792]{1,0:T(8,128)(2,1)S(1)}, bf16[32,1792]{1,0:T(8,128)(2,1)S(1)}, u32[]{:S(2)}, u32[]{:S(2)}) %collective-permute-start.7) | collective-permute-done | bytes 114720 | tf_op jit(solution)/shard_map/ppermute | solution.py:268
  49.2 1.5 %collective-permute-start.9 = (bf16[32,128]{1,0:T(8,128)(2,1)S(1)}, bf16[32,128]{1,0:T(8,128)(2,1)S(1)}, u32[]{:S(2)}, u32[]{:S(2)}) collective-permute-start(bf16[32,128]{1,0:T(8,128)(2,1)S(1)} %get-tuple-element.119), channel_id=1, source_target_pairs={{0,1},{1,0},{2,3},{3,2},{4,5},{5,4},{6,7},{7,6},{8,9},{9,8},{10,11... | collective-permute-start | bytes 24584 | tf_op jit(solution)/shard_map/ppermute | solution.py:268
  50.7 1.5 %collective-permute-start.10 = (bf16[32,128]{1,0:T(8,128)(2,1)S(1)}, bf16[32,128]{1,0:T(8,128)(2,1)S(1)}, u32[]{:S(2)}, u32[]{:S(2)}) collective-permute-start(bf16[32,128]{1,0:T(8,128)(2,1)S(1)} %get-tuple-element.120), channel_id=1, source_target_pairs={{0,4},{1,5},{2,6},{3,7},{4,0},{5,1},{6,2},{7,3},{8,12},{9,13},{10,... | collective-permute-start | bytes 24584 | tf_op jit(solution)/shard_map/ppermute | solution.py:268
  52.8 2.3 %shard_map.184 = (f32[3,32,32]{2,1,0:T(8,128)S(1)}, f32[32,64]{1,0:T(8,128)}, f32[32,288]{1,0:T(8,128)}, f32[32,32]{1,0:T(8,128)}) custom-call(bf16[32,3072]{1,0:T(8,128)(2,1)S(1)} %get-tuple-element.113.pt), custom_call_target="tpu_custom_call" | custom-call | tf_op jit(solution)/shard_map/pallas_call | solution.py:35
  55.1 1.6 %collective-permute-done.11.c = bf16[32,128]{1,0:T(8,128)(2,1)S(1)} collective-permute-done((bf16[32,128]{1,0:T(8,128)(2,1)S(1)}, bf16[32,128]{1,0:T(8,128)(2,1)S(1)}, u32[]{:S(2)}, u32[]{:S(2)}) %collective-permute-start.11) | collective-permute-done | bytes 8224 | tf_op jit(solution)/shard_map/ppermute | solution.py:268
  56.7 0.9 %shard_map.185 = (f32[32,32]{1,0:T(8,128)}, f32[32,32]{1,0:T(8,128)}, f32[32,64]{1,0:T(8,128)}) custom-call(f32[3,32,32]{2,1,0:T(8,128)S(1)} %get-tuple-element.117.inverse, f32[32,128]{1,0:T(8,128)S(1)} %get-tuple-element.118.own, bf16[32,128]{1,0:T(8,128)(2,1)S(1)} %collective-permute-done.9.a, bf16[32,128]{1,0:T(8,128)(2,1)S(1)} %collective-permute-done.10.b, ...), custom_call_target="tpu_custom_call" | custom-call | tf_op jit(solution)/shard_map/pallas_call | solution.py:35
  (29 shorter events, 3.9 us)
Async XLA Ops:
  4.2 10.2 %copy-start = (bf16[1,3,196,512]{3,2,1,0:T(8,128)(2,1)S(1)}, bf16[1,3,196,512]{3,2,1,0:T(8,128)(2,1)}, u32[]{:S(2)}) copy-start(bf16[1,3,196,512]{3,2,1,0:T(8,128)(2,1)} %param.14) | copy-start | bytes 1806340
  4.3 10.2 %collective-permute-start = (bf16[196,512]{1,0:T(8,128)(2,1)S(1)}, bf16[196,512]{1,0:T(8,128)(2,1)S(1)}, u32[]{:S(2)}, u32[]{:S(2)}) collective-permute-start(bf16[196,512]{1,0:T(8,128)(2,1)S(1)} %get-tuple-element.67), channel_id=1, source_target_pairs={{8,0},{16,8},{24,16},{9,1},{17,9},{25,17},{10,2},{18,10},{26,18},{... | collective-permute-start | bytes 602120 | tf_op jit(solution)/shard_map/ppermute | solution.py:397
  15.6 10.9 %copy-start.1 = (bf16[1,1,2304,256]{3,2,1,0:T(8,128)(2,1)S(1)}, bf16[1,1,2304,256]{3,2,1,0:T(8,128)(2,1)}, u32[]{:S(2)}) copy-start(bf16[1,1,2304,256]{3,2,1,0:T(8,128)(2,1)} %param.19) | copy-start | bytes 3538948
  15.6 10.9 %copy-start.2 = (bf16[1,1,256,512]{3,2,1,0:T(8,128)(2,1)S(1)}, bf16[1,1,256,512]{3,2,1,0:T(8,128)(2,1)}, u32[]{:S(2)}) copy-start(bf16[1,1,256,512]{3,2,1,0:T(8,128)(2,1)} %param.20) | copy-start | bytes 786436
  15.6 10.9 %copy-start.3 = (f32[1,32,512]{2,1,0:T(8,128)S(1)}, f32[1,32,512]{2,1,0:T(8,128)}, u32[]{:S(2)}) copy-start(f32[1,32,512]{2,1,0:T(8,128)} %param.23) | copy-start | bytes 196612
  15.6 10.9 %copy-start.4 = (f32[1,32,256]{2,1,0:T(8,128)S(1)}, f32[1,32,256]{2,1,0:T(8,128)}, u32[]{:S(2)}) copy-start(f32[1,32,256]{2,1,0:T(8,128)} %param.22) | copy-start | bytes 98308
  15.6 10.9 %copy-start.5 = (f32[1,32,256]{2,1,0:T(8,128)S(1)}, f32[1,32,256]{2,1,0:T(8,128)}, u32[]{:S(2)}) copy-start(f32[1,32,256]{2,1,0:T(8,128)} %param.21) | copy-start | bytes 98308
  15.6 10.9 %copy-start.6 = (bf16[1,1,512,256]{3,2,1,0:T(8,128)(2,1)S(1)}, bf16[1,1,512,256]{3,2,1,0:T(8,128)(2,1)}, u32[]{:S(2)}) copy-start(bf16[1,1,512,256]{3,2,1,0:T(8,128)(2,1)} %param.18) | copy-start | bytes 786436
  15.6 8.3 %collective-permute-start.1 = (bf16[196,512]{1,0:T(8,128)(2,1)S(1)}, bf16[196,512]{1,0:T(8,128)(2,1)S(1)}, u32[]{:S(2)}, u32[]{:S(2)}) collective-permute-start(bf16[196,512]{1,0:T(8,128)(2,1)S(1)} %get-tuple-element.73), channel_id=1, source_target_pairs={{8,0},{16,8},{24,16},{9,1},{17,9},{25,17},{10,2},{18,10},{26,18},{... | collective-permute-start | bytes 602120 | tf_op jit(solution)/shard_map/ppermute | solution.py:397
  25.0 7.7 %collective-permute-start.2 = (bf16[196,512]{1,0:T(8,128)(2,1)S(1)}, bf16[196,512]{1,0:T(8,128)(2,1)S(1)}, u32[]{:S(2)}, u32[]{:S(2)}) collective-permute-start(bf16[196,512]{1,0:T(8,128)(2,1)S(1)} %get-tuple-element.76), channel_id=1, source_target_pairs={{8,0},{16,8},{24,16},{9,1},{17,9},{25,17},{10,2},{18,10},{26,18},{... | collective-permute-start | bytes 602120 | tf_op jit(solution)/shard_map/ppermute | solution.py:397
  36.1 11.3 %collective-permute-start.8 = (bf16[128,3328]{1,0:T(8,128)(2,1)S(1)}, bf16[128,3328]{1,0:T(8,128)(2,1)S(1)}, u32[]{:S(2)}, u32[]{:S(2)}) collective-permute-start(bf16[128,3328]{1,0:T(8,128)(2,1)S(1)} %get-tuple-element.112), channel_id=1, source_target_pairs={{0,2},{1,3},{2,0},{3,1},{4,6},{5,7},{6,4},{7,5},{8,10},{9,11},{10,... | collective-permute-start | bytes 2555912 | tf_op jit(solution)/shard_map/ppermute | solution.py:268
  36.2 2.5 %collective-permute-start.3 = (bf16[32,1280]{1,0:T(8,128)(2,1)S(1)}, bf16[32,1280]{1,0:T(8,128)(2,1)S(1)}, u32[]{:S(2)}, u32[]{:S(2)}) collective-permute-start(bf16[32,1280]{1,0:T(8,128)(2,1)S(1)} %get-tuple-element.109), channel_id=1, source_target_pairs={{0,2},{1,3},{2,0},{3,1},{4,6},{5,7},{6,4},{7,5},{8,10},{9,11},{10,... | collective-permute-start | bytes 245768 | tf_op jit(solution)/shard_map/ppermute | solution.py:268
  38.7 7.0 %collective-permute-start.6 = (bf16[32,1792]{1,0:T(8,128)(2,1)S(1)}, bf16[32,1792]{1,0:T(8,128)(2,1)S(1)}, u32[]{:S(2)}, u32[]{:S(2)}) collective-permute-start(bf16[32,1792]{1,0:T(8,128)(2,1)S(1)} %shard_map.180.own), channel_id=1, source_target_pairs={{0,5},{1,4},{2,7},{3,6},{4,1},{5,0},{6,3},{7,2},{8,13},{9,12},{10,... | collective-permute-start | bytes 344072 | tf_op jit(solution)/shard_map/ppermute | solution.py:268
  41.1 6.2 %collective-permute-start.5 = (bf16[32,1792]{1,0:T(8,128)(2,1)S(1)}, bf16[32,1792]{1,0:T(8,128)(2,1)S(1)}, u32[]{:S(2)}, u32[]{:S(2)}) collective-permute-start(bf16[32,1792]{1,0:T(8,128)(2,1)S(1)} %shard_map.180.own), channel_id=1, source_target_pairs={{0,4},{1,5},{2,6},{3,7},{4,0},{5,1},{6,2},{7,3},{8,12},{9,13},{10,... | collective-permute-start | bytes 344072 | tf_op jit(solution)/shard_map/ppermute | solution.py:268
  41.6 5.7 %collective-permute-start.4 = (bf16[32,1792]{1,0:T(8,128)(2,1)S(1)}, bf16[32,1792]{1,0:T(8,128)(2,1)S(1)}, u32[]{:S(2)}, u32[]{:S(2)}) collective-permute-start(bf16[32,1792]{1,0:T(8,128)(2,1)S(1)} %shard_map.180.own), channel_id=1, source_target_pairs={{0,1},{1,0},{2,3},{3,2},{4,5},{5,4},{6,7},{7,6},{8,9},{9,8},{10,11... | collective-permute-start | bytes 344072 | tf_op jit(solution)/shard_map/ppermute | solution.py:268
  47.4 1.4 %collective-permute-start.7 = (bf16[32,1792]{1,0:T(8,128)(2,1)S(1)}, bf16[32,1792]{1,0:T(8,128)(2,1)S(1)}, u32[]{:S(2)}, u32[]{:S(2)}) collective-permute-start(bf16[32,1792]{1,0:T(8,128)(2,1)S(1)} %shard_map.181.mine), channel_id=1, source_target_pairs={{0,2},{1,3},{2,0},{3,1},{4,6},{5,7},{6,4},{7,5},{8,10},{9,11},{10,... | collective-permute-start | bytes 344072 | tf_op jit(solution)/shard_map/ppermute | solution.py:268
  49.2 5.9 %collective-permute-start.9 = (bf16[32,128]{1,0:T(8,128)(2,1)S(1)}, bf16[32,128]{1,0:T(8,128)(2,1)S(1)}, u32[]{:S(2)}, u32[]{:S(2)}) collective-permute-start(bf16[32,128]{1,0:T(8,128)(2,1)S(1)} %get-tuple-element.119), channel_id=1, source_target_pairs={{0,1},{1,0},{2,3},{3,2},{4,5},{5,4},{6,7},{7,6},{8,9},{9,8},{10,11... | collective-permute-start | bytes 24584 | tf_op jit(solution)/shard_map/ppermute | solution.py:268
  50.7 4.4 %collective-permute-start.10 = (bf16[32,128]{1,0:T(8,128)(2,1)S(1)}, bf16[32,128]{1,0:T(8,128)(2,1)S(1)}, u32[]{:S(2)}, u32[]{:S(2)}) collective-permute-start(bf16[32,128]{1,0:T(8,128)(2,1)S(1)} %get-tuple-element.120), channel_id=1, source_target_pairs={{0,4},{1,5},{2,6},{3,7},{4,0},{5,1},{6,2},{7,3},{8,12},{9,13},{10,... | collective-permute-start | bytes 24584 | tf_op jit(solution)/shard_map/ppermute | solution.py:268
  52.2 4.5 %collective-permute-start.11 = (bf16[32,128]{1,0:T(8,128)(2,1)S(1)}, bf16[32,128]{1,0:T(8,128)(2,1)S(1)}, u32[]{:S(2)}, u32[]{:S(2)}) collective-permute-start(bf16[32,128]{1,0:T(8,128)(2,1)S(1)} %get-tuple-element.121), channel_id=1, source_target_pairs={{0,5},{1,4},{2,7},{3,6},{4,1},{5,0},{6,3},{7,2},{8,13},{9,12},{10,... | collective-permute-start | bytes 24584 | tf_op jit(solution)/shard_map/ppermute | solution.py:268
